TPU v7x, 32 devices: a whole 2x2x4 slice. The times are simulated.
32 devices in a mesh: tm: 8 (over y, x, core), space: 4 (over z).
Axes of the slice: x: 2, y: 2, z: 4, core: 2. Of those that a mesh axis runs over, the one named last changes fastest.
Arguments:
- point_states: float32 [8, 128, 1024], P('tm', 'space'), may hold values from -6 to 6
- initial_state: float32 [128, 1024], P('space'), may hold values from -6 to 6
- node_rate: float32 [128, 1024], P('space'), may hold values from 0.01 to 0.06
- source_map: float32 [128, 1024], P('space'), may hold values from -6 to 6
- waveform: float32 [128], replicated, may hold values from -2 to 2
- cond_table: float32 [16], replicated, may hold values from 0.25 to 4
- class_map: int32 [16, 8], P('space'), may hold values from 0 to 15
- interval_steps: int32 [8], replicated, may hold values from 1 to 20, 128 in all
Outputs:
- corrected: float32 [8, 128, 1024], P('tm', 'space')
Inputs may be any that keep to these rules, and one draw needn't show every extreme that they name: `interval_steps`: they sum to 128 and the largest equals 20.
All inputs are finite; a program needn't handle non-finite values.
Results may differ from a plain program's by a relative error of at most 0.0003.
Values sent between devices are 32-bit elements; how exact they have to be, the bound alone decides.
No kernel may reach another device: no remote copies, remote signals or barrier semaphores. Data moves between devices by JAX's collectives and lax.ppermute only.
A program may use at most 64 MiB of HBM per device.

v0:
```python
import jax
import jax.numpy as jnp
from jax import lax
from jax.sharding import PartitionSpec as P

STEP_MOST = 20
CSUB = 5
BLK_R = 8
BLK_C = 128


def with_halo(shard, sides, width):
    for axis, dim in sides:
        peers, length = (lax.axis_size(axis), shard.shape[dim])
        up = [(i, (i + 1) % peers) for i in range(peers - 1)]
        down = [(j, i) for i, j in up]
        last = lax.slice_in_dim(shard, length - width, length, axis=dim)
        first = lax.slice_in_dim(shard, 0, width, axis=dim)
        before = lax.ppermute(last, axis, up)
        after = lax.ppermute(first, axis, down)
        shard = jnp.concatenate([before, shard, after], axis=dim)
    return shard


def passed_along(value, axis, steps):
    count = lax.axis_size(axis)
    first, last = (max(0, -steps), min(count, count - steps))
    return lax.ppermute(value, axis, [(source, source + steps) for source in range(first, last)])


def neighbours(values):
    zero_row = jnp.zeros_like(values[..., :1, :])
    zero_col = jnp.zeros_like(values[..., :, :1])
    above_row = jnp.concatenate([zero_row, values[..., :-1, :]], axis=-2)
    below_row = jnp.concatenate([values[..., 1:, :], zero_row], axis=-2)
    left_col = jnp.concatenate([zero_col, values[..., :, :-1]], axis=-1)
    right_col = jnp.concatenate([values[..., :, 1:], zero_col], axis=-1)
    return (above_row, below_row, left_col, right_col)


def side_cols(values):
    zero_col = jnp.zeros_like(values[..., :, :1])
    left_col = jnp.concatenate([zero_col, values[..., :, :-1]], axis=-1)
    right_col = jnp.concatenate([values[..., :, 1:], zero_col], axis=-1)
    return (left_col, right_col)


def restrict(values):
    return 0.25 * (
        values[..., 0::2, 0::2]
        + values[..., 1::2, 0::2]
        + (values[..., 0::2, 1::2] + values[..., 1::2, 1::2])
    )


def prolong(values):
    return jnp.repeat(jnp.repeat(values, 2, axis=-2), 2, axis=-1)


def node_conductance(class_map, cond_table):
    classes = jnp.arange(cond_table.shape[0], dtype=jnp.int32)
    picked = jnp.sum(
        jnp.where(class_map[None] == classes[:, None, None], cond_table[:, None, None], 0.0), axis=0
    )
    return jnp.repeat(jnp.repeat(picked, BLK_R, axis=0), BLK_C, axis=1)


def base_weights(rates, conduct):
    above_row, below_row, left_col, right_col = neighbours(conduct)
    return (
        rates * jnp.sqrt(conduct * above_row),
        rates * jnp.sqrt(conduct * below_row),
        rates * jnp.sqrt(conduct * left_col),
        rates * jnp.sqrt(conduct * right_col),
    )


def combine(state_now, above_row, below_row, left_col, right_col, weights, forcing):
    to_above, to_below, to_left, to_right = weights
    return (
        state_now
        + (
            to_above * (above_row - state_now)
            + to_below * (below_row - state_now)
            + to_left * (left_col - state_now)
            + to_right * (right_col - state_now)
        )
        + forcing
    )


def coarse_step(carried, coarse_weights, factor):
    to_above, to_below, to_left, to_right = coarse_weights
    above_row, below_row, left_col, right_col = neighbours(carried)
    return carried + factor * (
        to_above * (above_row - carried)
        + to_below * (below_row - carried)
        + to_left * (left_col - carried)
        + to_right * (right_col - carried)
    )


def run_block(incoming, residues, coarse_weights, factors, trim):
    carried = incoming
    error_list = [carried]
    for substep in range(CSUB):
        carried = coarse_step(carried, coarse_weights, factors[0])
    carried = carried + residues[0]
    errors = jnp.stack(error_list)
    return (carried[trim:-trim], errors[:, trim:-trim])


def shards(
    point_states,
    initial_state,
    node_rate,
    source_map,
    waveform,
    cond_table,
    class_map,
    interval_steps,
):
    per_dev = point_states.shape[0]
    my_index = lax.axis_index("tm")
    conduct = node_conductance(class_map, cond_table)
    conduct_rim = with_halo(conduct, (("space", 0),), 1)
    left_g, right_g = side_cols(conduct)
    weights = (
        node_rate * jnp.sqrt(conduct * conduct_rim[:-2]),
        node_rate * jnp.sqrt(conduct * conduct_rim[2:]),
        node_rate * jnp.sqrt(conduct * left_g),
        node_rate * jnp.sqrt(conduct * right_g),
    )
    starts_all = jnp.cumsum(interval_steps) - interval_steps
    my_starts = lax.dynamic_slice_in_dim(starts_all, my_index * per_dev, per_dev)
    counts = lax.dynamic_slice_in_dim(interval_steps, my_index * per_dev, per_dev)
    positions = jnp.arange(waveform.shape[0], dtype=jnp.int32)

    def wave_at(fine_step):
        hits = positions[None, :] == (my_starts + fine_step)[:, None]
        return jnp.sum(jnp.where(hits, waveform[None, :], 0.0), axis=1)

    stacked_coef = jnp.stack([weights[0], weights[1], weights[2], weights[3], source_map])
    wide_coef = with_halo(stacked_coef, (("space", 1),), STEP_MOST)
    wide_weights = (wide_coef[0], wide_coef[1], wide_coef[2], wide_coef[3])
    wide_source = wide_coef[4]

    def sweep(state_in):
        widened = with_halo(state_in, (("space", 1),), STEP_MOST)
        for fine_step in range(STEP_MOST):
            above_row, below_row, left_col, right_col = neighbours(widened)
            forcing = wave_at(fine_step)[:, None, None] * wide_source
            updated = combine(
                widened, above_row, below_row, left_col, right_col, wide_weights, forcing
            )
            widened = jnp.where((fine_step < counts)[:, None, None], updated, widened)
        return widened[:, STEP_MOST:-STEP_MOST]

    first_pass = sweep(point_states)
    incoming = passed_along(first_pass[-1], "tm", 1)
    head_state = jnp.where(my_index == 0, initial_state, incoming)
    relaxed = jnp.concatenate([head_state[None], first_pass[:-1]], axis=0)
    second_pass = sweep(relaxed)
    change = restrict(second_pass - first_pass)
    factors = counts.astype(jnp.float32) / (4.0 * CSUB)
    rim_width = per_dev * CSUB
    stacked = jnp.concatenate([change, restrict(node_rate)[None], restrict(conduct)[None]], axis=0)
    widened = with_halo(stacked, (("space", 1),), rim_width + 1)
    full_weights = base_weights(widened[per_dev], widened[per_dev + 1])
    coarse_weights = (
        full_weights[0][1:-1],
        full_weights[1][1:-1],
        full_weights[2][1:-1],
        full_weights[3][1:-1],
    )
    residues = widened[:per_dev, 1:-1]

    def one_turn(turn_index, carry):
        outgoing, stored = carry
        received = passed_along(outgoing, "tm", 1)
        beside_all = with_halo(received, (("space", 0),), rim_width)
        return lax.cond(
            turn_index == my_index,
            lambda: run_block(beside_all, residues, coarse_weights, factors, rim_width),
            lambda: (outgoing, stored),
        )

    start_carry = (jnp.zeros_like(change[0]), jnp.zeros_like(change))
    unused, errors = lax.fori_loop(0, lax.axis_size("tm"), one_turn, start_carry)
    return relaxed + prolong(errors)


def solution(mesh):
    placed = (
        P("tm", "space", None),
        P("space", None),
        P("space", None),
        P("space", None),
        P(),
        P(),
        P("space", None),
        P(),
    )
    return jax.shard_map(
        shards, mesh=mesh, in_specs=placed, out_specs=P("tm", "space", None), check_vma=False
    )
```

profile of v0, /device:TPU:28, one launch (start us, length us, event | category | flops | bytes accessed | tf_op | source)
XLA Modules:
  0.0 257.9 jit_solution(103556880594785168)
XLA Ops:
  2.3 4.5 %collective-permute-start.6 = (f32[1,1024]{1,0:T(1,128)S(1)}, f32[1,1024]{1,0:T(1,128)S(1)}, u32[]{:S(2)}, u32[]{:S(2)}) collective-permute-start(f32[1,1024]{1,0:T(1,128)S(1)} %bitcast.111), channel_id=1, source_target_pairs={{1,0},{2,1},{3,2},{5,4},{6,5},{7,6},{9,8},{10,9},{11,10},{13,12},{... | collective-permute-start | bytes 12296 | tf_op jit(solution)/shard_map/ppermute | solution.py:20
  9.3 4.6 %collective-permute-start.4 = (f32[1,20,1024]{2,1,0:T(8,128)S(1)}, f32[1,20,1024]{2,1,0:T(8,128)S(1)}, u32[]{:S(2)}, u32[]{:S(2)}) collective-permute-start(f32[1,20,1024]{2,1,0:T(8,128)S(1)} %get-tuple-element.476), channel_id=1, source_target_pairs={{1,0},{2,1},{3,2},{5,4},{6,5},{7,6},{9,8},{10,9},{11,10},{13,12},{... | collective-permute-start | bytes 245768 | tf_op jit(solution)/shard_map/ppermute | solution.py:20
  46.1 4.6 %collective-permute-start.8 = (f32[5,20,1024]{2,1,0:T(8,128)S(1)}, f32[5,20,1024]{2,1,0:T(8,128)S(1)}, u32[]{:S(2)}, u32[]{:S(2)}) collective-permute-start(f32[5,20,1024]{2,1,0:T(8,128)S(1)} %get-tuple-element.300), channel_id=1, source_target_pairs={{1,0},{2,1},{3,2},{5,4},{6,5},{7,6},{9,8},{10,9},{11,10},{13,12},{... | collective-permute-start | bytes 1228808 | tf_op jit(solution)/shard_map/ppermute | solution.py:20
  51.0 7.6 %collective-permute-done.7 = f32[5,20,1024]{2,1,0:T(8,128)S(1)} collective-permute-done((f32[5,20,1024]{2,1,0:T(8,128)S(1)}, f32[5,20,1024]{2,1,0:T(8,128)S(1)}, u32[]{:S(2)}, u32[]{:S(2)}) %collective-permute-start.7) | collective-permute-done | bytes 409632 | tf_op jit(solution)/shard_map/ppermute | solution.py:19
  82.9 2.1 collective-permute-start.9
  95.7 5.2 %collective-permute-start.11 = (f32[1,20,1024]{2,1,0:T(8,128)S(1)}, f32[1,20,1024]{2,1,0:T(8,128)S(1)}, u32[]{:S(2)}, u32[]{:S(2)}) collective-permute-start(f32[1,20,1024]{2,1,0:T(8,128)S(1)} %get-tuple-element.472), channel_id=1, source_target_pairs={{1,0},{2,1},{3,2},{5,4},{6,5},{7,6},{9,8},{10,9},{11,10},{13,12},{... | collective-permute-start | bytes 245768 | tf_op jit(solution)/shard_map/ppermute | solution.py:20
  132.0 5.0 %collective-permute-start.13 = (f32[3,6,512]{2,1,0:T(8,128)S(1)}, f32[3,6,512]{2,1,0:T(8,128)S(1)}, u32[]{:S(2)}, u32[]{:S(2)}) collective-permute-start(f32[3,6,512]{2,1,0:T(8,128)S(1)} %get-tuple-element.478), channel_id=1, source_target_pairs={{1,0},{2,1},{3,2},{5,4},{6,5},{7,6},{9,8},{10,9},{11,10},{13,12},{... | collective-permute-start | bytes 110600 | tf_op jit(solution)/shard_map/ppermute | solution.py:20
  139.0 117.6 %while.18 = (s32[]{:T(128)}, f32[16,512]{1,0:T(8,128)S(1)}, f32[1,16,512]{2,1,0:T(8,128)S(1)}, s32[]{:T(128)}, f32[1]{0:T(128)}, /*index=5*/f32[26,512]{1,0:T(8,...) while((s32[]{:T(128)}, f32[16,512]{1,0:T(8,128)S(1)}, ...), condition=%wide.region_25.26_spmd, body=%wide.region_22.25_spmd.sunk | while | flops 859140 | bytes 5416255 | solution.py:189
  139.0 1.9 collective-permute-start
  141.0 4.2 %collective-permute-done = f32[16,512]{1,0:T(8,128)S(1)} collective-permute-done((f32[16,512]{1,0:T(8,128)S(1)}, f32[16,512]{1,0:T(8,128)S(1)}, u32[]{:S(2)}, u32[]{:S(2)}) %collective-permute-start) | collective-permute-done | bytes 32800 | tf_op jit(solution)/shard_map/while/body/eval_jaxpr/ppermute | solution.py:28
  145.2 4.2 %collective-permute-start.1 = (f32[5,512]{1,0:T(8,128)S(1)}, f32[5,512]{1,0:T(8,128)S(1)}, u32[]{:S(2)}, u32[]{:S(2)}) collective-permute-start(f32[5,512]{1,0:T(8,128)S(1)} %get-tuple-element.550), channel_id=1, source_target_pairs={{1,0},{2,1},{3,2},{5,4},{6,5},{7,6},{9,8},{10,9},{11,10},{13,12},{... | collective-permute-start | bytes 30728 | tf_op jit(solution)/shard_map/while/body/eval_jaxpr/ppermute | solution.py:20
  150.9 4.5 %collective-permute-done.2 = f32[5,512]{1,0:T(8,128)S(1)} collective-permute-done((f32[5,512]{1,0:T(8,128)S(1)}, f32[5,512]{1,0:T(8,128)S(1)}, u32[]{:S(2)}, u32[]{:S(2)}) %collective-permute-start.2) | collective-permute-done | bytes 10272 | tf_op jit(solution)/shard_map/while/body/eval_jaxpr/ppermute | solution.py:19
  155.4 1.9 collective-permute-start
  157.3 4.2 %collective-permute-done = f32[16,512]{1,0:T(8,128)S(1)} collective-permute-done((f32[16,512]{1,0:T(8,128)S(1)}, f32[16,512]{1,0:T(8,128)S(1)}, u32[]{:S(2)}, u32[]{:S(2)}) %collective-permute-start) | collective-permute-done | bytes 32800 | tf_op jit(solution)/shard_map/while/body/eval_jaxpr/ppermute | solution.py:28
  161.5 3.9 %collective-permute-start.1 = (f32[5,512]{1,0:T(8,128)S(1)}, f32[5,512]{1,0:T(8,128)S(1)}, u32[]{:S(2)}, u32[]{:S(2)}) collective-permute-start(f32[5,512]{1,0:T(8,128)S(1)} %get-tuple-element.550), channel_id=1, source_target_pairs={{1,0},{2,1},{3,2},{5,4},{6,5},{7,6},{9,8},{10,9},{11,10},{13,12},{... | collective-permute-start | bytes 30728 | tf_op jit(solution)/shard_map/while/body/eval_jaxpr/ppermute | solution.py:20
  166.9 4.2 %collective-permute-done.2 = f32[5,512]{1,0:T(8,128)S(1)} collective-permute-done((f32[5,512]{1,0:T(8,128)S(1)}, f32[5,512]{1,0:T(8,128)S(1)}, u32[]{:S(2)}, u32[]{:S(2)}) %collective-permute-start.2) | collective-permute-done | bytes 10272 | tf_op jit(solution)/shard_map/while/body/eval_jaxpr/ppermute | solution.py:19
  171.1 1.9 collective-permute-start
  173.1 4.2 %collective-permute-done = f32[16,512]{1,0:T(8,128)S(1)} collective-permute-done((f32[16,512]{1,0:T(8,128)S(1)}, f32[16,512]{1,0:T(8,128)S(1)}, u32[]{:S(2)}, u32[]{:S(2)}) %collective-permute-start) | collective-permute-done | bytes 32800 | tf_op jit(solution)/shard_map/while/body/eval_jaxpr/ppermute | solution.py:28
  177.3 3.9 %collective-permute-start.1 = (f32[5,512]{1,0:T(8,128)S(1)}, f32[5,512]{1,0:T(8,128)S(1)}, u32[]{:S(2)}, u32[]{:S(2)}) collective-permute-start(f32[5,512]{1,0:T(8,128)S(1)} %get-tuple-element.550), channel_id=1, source_target_pairs={{1,0},{2,1},{3,2},{5,4},{6,5},{7,6},{9,8},{10,9},{11,10},{13,12},{... | collective-permute-start | bytes 30728 | tf_op jit(solution)/shard_map/while/body/eval_jaxpr/ppermute | solution.py:20
  182.6 4.2 %collective-permute-done.2 = f32[5,512]{1,0:T(8,128)S(1)} collective-permute-done((f32[5,512]{1,0:T(8,128)S(1)}, f32[5,512]{1,0:T(8,128)S(1)}, u32[]{:S(2)}, u32[]{:S(2)}) %collective-permute-start.2) | collective-permute-done | bytes 10272 | tf_op jit(solution)/shard_map/while/body/eval_jaxpr/ppermute | solution.py:19
  186.9 1.9 collective-permute-start
  188.8 4.2 %collective-permute-done = f32[16,512]{1,0:T(8,128)S(1)} collective-permute-done((f32[16,512]{1,0:T(8,128)S(1)}, f32[16,512]{1,0:T(8,128)S(1)}, u32[]{:S(2)}, u32[]{:S(2)}) %collective-permute-start) | collective-permute-done | bytes 32800 | tf_op jit(solution)/shard_map/while/body/eval_jaxpr/ppermute | solution.py:28
  196.4 4.2 %collective-permute-done.2 = f32[5,512]{1,0:T(8,128)S(1)} collective-permute-done((f32[5,512]{1,0:T(8,128)S(1)}, f32[5,512]{1,0:T(8,128)S(1)}, u32[]{:S(2)}, u32[]{:S(2)}) %collective-permute-start.2) | collective-permute-done | bytes 10272 | tf_op jit(solution)/shard_map/while/body/eval_jaxpr/ppermute | solution.py:19
  202.5 4.2 %collective-permute-done = f32[16,512]{1,0:T(8,128)S(1)} collective-permute-done((f32[16,512]{1,0:T(8,128)S(1)}, f32[16,512]{1,0:T(8,128)S(1)}, u32[]{:S(2)}, u32[]{:S(2)}) %collective-permute-start) | collective-permute-done | bytes 32800 | tf_op jit(solution)/shard_map/while/body/eval_jaxpr/ppermute | solution.py:28
  210.1 4.2 %collective-permute-done.2 = f32[5,512]{1,0:T(8,128)S(1)} collective-permute-done((f32[5,512]{1,0:T(8,128)S(1)}, f32[5,512]{1,0:T(8,128)S(1)}, u32[]{:S(2)}, u32[]{:S(2)}) %collective-permute-start.2) | collective-permute-done | bytes 10272 | tf_op jit(solution)/shard_map/while/body/eval_jaxpr/ppermute | solution.py:19
  217.4 4.2 %collective-permute-done = f32[16,512]{1,0:T(8,128)S(1)} collective-permute-done((f32[16,512]{1,0:T(8,128)S(1)}, f32[16,512]{1,0:T(8,128)S(1)}, u32[]{:S(2)}, u32[]{:S(2)}) %collective-permute-start) | collective-permute-done | bytes 32800 | tf_op jit(solution)/shard_map/while/body/eval_jaxpr/ppermute | solution.py:28
  224.9 4.2 %collective-permute-done.2 = f32[5,512]{1,0:T(8,128)S(1)} collective-permute-done((f32[5,512]{1,0:T(8,128)S(1)}, f32[5,512]{1,0:T(8,128)S(1)}, u32[]{:S(2)}, u32[]{:S(2)}) %collective-permute-start.2) | collective-permute-done | bytes 10272 | tf_op jit(solution)/shard_map/while/body/eval_jaxpr/ppermute | solution.py:19
  229.2 1.9 collective-permute-start
  231.1 4.2 %collective-permute-done = f32[16,512]{1,0:T(8,128)S(1)} collective-permute-done((f32[16,512]{1,0:T(8,128)S(1)}, f32[16,512]{1,0:T(8,128)S(1)}, u32[]{:S(2)}, u32[]{:S(2)}) %collective-permute-start) | collective-permute-done | bytes 32800 | tf_op jit(solution)/shard_map/while/body/eval_jaxpr/ppermute | solution.py:28
  238.7 4.2 %collective-permute-done.2 = f32[5,512]{1,0:T(8,128)S(1)} collective-permute-done((f32[5,512]{1,0:T(8,128)S(1)}, f32[5,512]{1,0:T(8,128)S(1)}, u32[]{:S(2)}, u32[]{:S(2)}) %collective-permute-start.2) | collective-permute-done | bytes 10272 | tf_op jit(solution)/shard_map/while/body/eval_jaxpr/ppermute | solution.py:19
  244.8 4.2 %collective-permute-done = f32[16,512]{1,0:T(8,128)S(1)} collective-permute-done((f32[16,512]{1,0:T(8,128)S(1)}, f32[16,512]{1,0:T(8,128)S(1)}, u32[]{:S(2)}, u32[]{:S(2)}) %collective-permute-start) | collective-permute-done | bytes 32800 | tf_op jit(solution)/shard_map/while/body/eval_jaxpr/ppermute | solution.py:28
  252.4 4.2 %collective-permute-done.2 = f32[5,512]{1,0:T(8,128)S(1)} collective-permute-done((f32[5,512]{1,0:T(8,128)S(1)}, f32[5,512]{1,0:T(8,128)S(1)}, u32[]{:S(2)}, u32[]{:S(2)}) %collective-permute-start.2) | collective-permute-done | bytes 10272 | tf_op jit(solution)/shard_map/while/body/eval_jaxpr/ppermute | solution.py:19
  (270 shorter events, 109.1 us)
Async XLA Ops:
  1.0 43.4 %collective-permute-start.5 = (f32[1,1024]{1,0:T(1,128)S(1)}, f32[1,1024]{1,0:T(1,128)S(1)}, u32[]{:S(2)}, u32[]{:S(2)}) collective-permute-start(f32[1,1024]{1,0:T(1,128)S(1)} %bitcast.110), channel_id=1, source_target_pairs={{0,1},{1,2},{2,3},{4,5},{5,6},{6,7},{8,9},{9,10},{10,11},{12,13},{... | collective-permute-start | bytes 12296 | tf_op jit(solution)/shard_map/ppermute | solution.py:19
  2.3 42.1 %collective-permute-start.6 = (f32[1,1024]{1,0:T(1,128)S(1)}, f32[1,1024]{1,0:T(1,128)S(1)}, u32[]{:S(2)}, u32[]{:S(2)}) collective-permute-start(f32[1,1024]{1,0:T(1,128)S(1)} %bitcast.111), channel_id=1, source_target_pairs={{1,0},{2,1},{3,2},{5,4},{6,5},{7,6},{9,8},{10,9},{11,10},{13,12},{... | collective-permute-start | bytes 12296 | tf_op jit(solution)/shard_map/ppermute | solution.py:20
  7.9 42.8 %collective-permute-start.3 = (f32[1,20,1024]{2,1,0:T(8,128)S(1)}, f32[1,20,1024]{2,1,0:T(8,128)S(1)}, u32[]{:S(2)}, u32[]{:S(2)}) collective-permute-start(f32[1,20,1024]{2,1,0:T(8,128)S(1)} %get-tuple-element.475), channel_id=1, source_target_pairs={{0,1},{1,2},{2,3},{4,5},{5,6},{6,7},{8,9},{9,10},{10,11},{12,13},{... | collective-permute-start | bytes 245768 | tf_op jit(solution)/shard_map/ppermute | solution.py:19
  9.3 41.4 %collective-permute-start.4 = (f32[1,20,1024]{2,1,0:T(8,128)S(1)}, f32[1,20,1024]{2,1,0:T(8,128)S(1)}, u32[]{:S(2)}, u32[]{:S(2)}) collective-permute-start(f32[1,20,1024]{2,1,0:T(8,128)S(1)} %get-tuple-element.476), channel_id=1, source_target_pairs={{1,0},{2,1},{3,2},{5,4},{6,5},{7,6},{9,8},{10,9},{11,10},{13,12},{... | collective-permute-start | bytes 245768 | tf_op jit(solution)/shard_map/ppermute | solution.py:20
  44.8 13.7 %collective-permute-start.7 = (f32[5,20,1024]{2,1,0:T(8,128)S(1)}, f32[5,20,1024]{2,1,0:T(8,128)S(1)}, u32[]{:S(2)}, u32[]{:S(2)}) collective-permute-start(f32[5,20,1024]{2,1,0:T(8,128)S(1)} %get-tuple-element.299), channel_id=1, source_target_pairs={{0,1},{1,2},{2,3},{4,5},{5,6},{6,7},{8,9},{9,10},{10,11},{12,13},{... | collective-permute-start | bytes 1228808 | tf_op jit(solution)/shard_map/ppermute | solution.py:19
  46.1 13.6 %collective-permute-start.8 = (f32[5,20,1024]{2,1,0:T(8,128)S(1)}, f32[5,20,1024]{2,1,0:T(8,128)S(1)}, u32[]{:S(2)}, u32[]{:S(2)}) collective-permute-start(f32[5,20,1024]{2,1,0:T(8,128)S(1)} %get-tuple-element.300), channel_id=1, source_target_pairs={{1,0},{2,1},{3,2},{5,4},{6,5},{7,6},{9,8},{10,9},{11,10},{13,12},{... | collective-permute-start | bytes 1228808 | tf_op jit(solution)/shard_map/ppermute | solution.py:20
  82.9 11.4 %collective-permute-start.9 = (f32[32,1024]{1,0:T(8,128)S(1)}, f32[32,1024]{1,0:T(8,128)S(1)}, u32[]{:S(2)}, u32[]{:S(2)}) collective-permute-start(f32[32,1024]{1,0:T(8,128)S(1)} %bitcast.108), channel_id=1, source_target_pairs={{0,4},{4,8},{8,12},{12,16},{16,20},{20,24},{24,28},{1,5},{5,9},{9,... | collective-permute-start | bytes 393224 | tf_op jit(solution)/shard_map/ppermute | solution.py:28
  94.4 7.1 %collective-permute-start.10 = (f32[1,20,1024]{2,1,0:T(8,128)S(1)}, f32[1,20,1024]{2,1,0:T(8,128)S(1)}, u32[]{:S(2)}, u32[]{:S(2)}) collective-permute-start(f32[1,20,1024]{2,1,0:T(8,128)S(1)} %get-tuple-element.471), channel_id=1, source_target_pairs={{0,1},{1,2},{2,3},{4,5},{5,6},{6,7},{8,9},{9,10},{10,11},{12,13},{... | collective-permute-start | bytes 245768 | tf_op jit(solution)/shard_map/ppermute | solution.py:19
  95.7 7.6 %collective-permute-start.11 = (f32[1,20,1024]{2,1,0:T(8,128)S(1)}, f32[1,20,1024]{2,1,0:T(8,128)S(1)}, u32[]{:S(2)}, u32[]{:S(2)}) collective-permute-start(f32[1,20,1024]{2,1,0:T(8,128)S(1)} %get-tuple-element.472), channel_id=1, source_target_pairs={{1,0},{2,1},{3,2},{5,4},{6,5},{7,6},{9,8},{10,9},{11,10},{13,12},{... | collective-permute-start | bytes 245768 | tf_op jit(solution)/shard_map/ppermute | solution.py:20
  130.7 7.0 %collective-permute-start.12 = (f32[3,6,512]{2,1,0:T(8,128)S(1)}, f32[3,6,512]{2,1,0:T(8,128)S(1)}, u32[]{:S(2)}, u32[]{:S(2)}) collective-permute-start(f32[3,6,512]{2,1,0:T(8,128)S(1)} %get-tuple-element.477), channel_id=1, source_target_pairs={{0,1},{1,2},{2,3},{4,5},{5,6},{6,7},{8,9},{9,10},{10,11},{12,13},{... | collective-permute-start | bytes 110600 | tf_op jit(solution)/shard_map/ppermute | solution.py:19
  132.0 6.8 %collective-permute-start.13 = (f32[3,6,512]{2,1,0:T(8,128)S(1)}, f32[3,6,512]{2,1,0:T(8,128)S(1)}, u32[]{:S(2)}, u32[]{:S(2)}) collective-permute-start(f32[3,6,512]{2,1,0:T(8,128)S(1)} %get-tuple-element.478), channel_id=1, source_target_pairs={{1,0},{2,1},{3,2},{5,4},{6,5},{7,6},{9,8},{10,9},{11,10},{13,12},{... | collective-permute-start | bytes 110600 | tf_op jit(solution)/shard_map/ppermute | solution.py:20
  139.0 6.1 %collective-permute-start = (f32[16,512]{1,0:T(8,128)S(1)}, f32[16,512]{1,0:T(8,128)S(1)}, u32[]{:S(2)}, u32[]{:S(2)}) collective-permute-start(f32[16,512]{1,0:T(8,128)S(1)} %get-tuple-element.570), channel_id=1, source_target_pairs={{0,4},{4,8},{8,12},{12,16},{16,20},{20,24},{24,28},{1,5},{5,9},{9,... | collective-permute-start | bytes 98312 | tf_op jit(solution)/shard_map/while/body/eval_jaxpr/ppermute | solution.py:28
  145.2 5.7 %collective-permute-start.1 = (f32[5,512]{1,0:T(8,128)S(1)}, f32[5,512]{1,0:T(8,128)S(1)}, u32[]{:S(2)}, u32[]{:S(2)}) collective-permute-start(f32[5,512]{1,0:T(8,128)S(1)} %get-tuple-element.550), channel_id=1, source_target_pairs={{1,0},{2,1},{3,2},{5,4},{6,5},{7,6},{9,8},{10,9},{11,10},{13,12},{... | collective-permute-start | bytes 30728 | tf_op jit(solution)/shard_map/while/body/eval_jaxpr/ppermute | solution.py:20
  149.4 5.9 %collective-permute-start.2 = (f32[5,512]{1,0:T(8,128)S(1)}, f32[5,512]{1,0:T(8,128)S(1)}, u32[]{:S(2)}, u32[]{:S(2)}) collective-permute-start(f32[5,512]{1,0:T(8,128)S(1)} %get-tuple-element.551), channel_id=1, source_target_pairs={{0,1},{1,2},{2,3},{4,5},{5,6},{6,7},{8,9},{9,10},{10,11},{12,13},{... | collective-permute-start | bytes 30728 | tf_op jit(solution)/shard_map/while/body/eval_jaxpr/ppermute | solution.py:19
  155.4 6.1 %collective-permute-start = (f32[16,512]{1,0:T(8,128)S(1)}, f32[16,512]{1,0:T(8,128)S(1)}, u32[]{:S(2)}, u32[]{:S(2)}) collective-permute-start(f32[16,512]{1,0:T(8,128)S(1)} %get-tuple-element.570), channel_id=1, source_target_pairs={{0,4},{4,8},{8,12},{12,16},{16,20},{20,24},{24,28},{1,5},{5,9},{9,... | collective-permute-start | bytes 98312 | tf_op jit(solution)/shard_map/while/body/eval_jaxpr/ppermute | solution.py:28
  161.5 5.3 %collective-permute-start.1 = (f32[5,512]{1,0:T(8,128)S(1)}, f32[5,512]{1,0:T(8,128)S(1)}, u32[]{:S(2)}, u32[]{:S(2)}) collective-permute-start(f32[5,512]{1,0:T(8,128)S(1)} %get-tuple-element.550), channel_id=1, source_target_pairs={{1,0},{2,1},{3,2},{5,4},{6,5},{7,6},{9,8},{10,9},{11,10},{13,12},{... | collective-permute-start | bytes 30728 | tf_op jit(solution)/shard_map/while/body/eval_jaxpr/ppermute | solution.py:20
  165.4 5.6 %collective-permute-start.2 = (f32[5,512]{1,0:T(8,128)S(1)}, f32[5,512]{1,0:T(8,128)S(1)}, u32[]{:S(2)}, u32[]{:S(2)}) collective-permute-start(f32[5,512]{1,0:T(8,128)S(1)} %get-tuple-element.551), channel_id=1, source_target_pairs={{0,1},{1,2},{2,3},{4,5},{5,6},{6,7},{8,9},{9,10},{10,11},{12,13},{... | collective-permute-start | bytes 30728 | tf_op jit(solution)/shard_map/while/body/eval_jaxpr/ppermute | solution.py:19
  171.1 6.1 %collective-permute-start = (f32[16,512]{1,0:T(8,128)S(1)}, f32[16,512]{1,0:T(8,128)S(1)}, u32[]{:S(2)}, u32[]{:S(2)}) collective-permute-start(f32[16,512]{1,0:T(8,128)S(1)} %get-tuple-element.570), channel_id=1, source_target_pairs={{0,4},{4,8},{8,12},{12,16},{16,20},{20,24},{24,28},{1,5},{5,9},{9,... | collective-permute-start | bytes 98312 | tf_op jit(solution)/shard_map/while/body/eval_jaxpr/ppermute | solution.py:28
  177.3 5.3 %collective-permute-start.1 = (f32[5,512]{1,0:T(8,128)S(1)}, f32[5,512]{1,0:T(8,128)S(1)}, u32[]{:S(2)}, u32[]{:S(2)}) collective-permute-start(f32[5,512]{1,0:T(8,128)S(1)} %get-tuple-element.550), channel_id=1, source_target_pairs={{1,0},{2,1},{3,2},{5,4},{6,5},{7,6},{9,8},{10,9},{11,10},{13,12},{... | collective-permute-start | bytes 30728 | tf_op jit(solution)/shard_map/while/body/eval_jaxpr/ppermute | solution.py:20
  181.2 5.6 %collective-permute-start.2 = (f32[5,512]{1,0:T(8,128)S(1)}, f32[5,512]{1,0:T(8,128)S(1)}, u32[]{:S(2)}, u32[]{:S(2)}) collective-permute-start(f32[5,512]{1,0:T(8,128)S(1)} %get-tuple-element.551), channel_id=1, source_target_pairs={{0,1},{1,2},{2,3},{4,5},{5,6},{6,7},{8,9},{9,10},{10,11},{12,13},{... | collective-permute-start | bytes 30728 | tf_op jit(solution)/shard_map/while/body/eval_jaxpr/ppermute | solution.py:19
  186.9 6.1 %collective-permute-start = (f32[16,512]{1,0:T(8,128)S(1)}, f32[16,512]{1,0:T(8,128)S(1)}, u32[]{:S(2)}, u32[]{:S(2)}) collective-permute-start(f32[16,512]{1,0:T(8,128)S(1)} %get-tuple-element.570), channel_id=1, source_target_pairs={{0,4},{4,8},{8,12},{12,16},{16,20},{20,24},{24,28},{1,5},{5,9},{9,... | collective-permute-start | bytes 98312 | tf_op jit(solution)/shard_map/while/body/eval_jaxpr/ppermute | solution.py:28
  193.0 3.3 %collective-permute-start.1 = (f32[5,512]{1,0:T(8,128)S(1)}, f32[5,512]{1,0:T(8,128)S(1)}, u32[]{:S(2)}, u32[]{:S(2)}) collective-permute-start(f32[5,512]{1,0:T(8,128)S(1)} %get-tuple-element.550), channel_id=1, source_target_pairs={{1,0},{2,1},{3,2},{5,4},{6,5},{7,6},{9,8},{10,9},{11,10},{13,12},{... | collective-permute-start | bytes 30728 | tf_op jit(solution)/shard_map/while/body/eval_jaxpr/ppermute | solution.py:20
  194.9 5.6 %collective-permute-start.2 = (f32[5,512]{1,0:T(8,128)S(1)}, f32[5,512]{1,0:T(8,128)S(1)}, u32[]{:S(2)}, u32[]{:S(2)}) collective-permute-start(f32[5,512]{1,0:T(8,128)S(1)} %get-tuple-element.551), channel_id=1, source_target_pairs={{0,1},{1,2},{2,3},{4,5},{5,6},{6,7},{8,9},{9,10},{10,11},{12,13},{... | collective-permute-start | bytes 30728 | tf_op jit(solution)/shard_map/while/body/eval_jaxpr/ppermute | solution.py:19
  200.6 6.1 %collective-permute-start = (f32[16,512]{1,0:T(8,128)S(1)}, f32[16,512]{1,0:T(8,128)S(1)}, u32[]{:S(2)}, u32[]{:S(2)}) collective-permute-start(f32[16,512]{1,0:T(8,128)S(1)} %get-tuple-element.570), channel_id=1, source_target_pairs={{0,4},{4,8},{8,12},{12,16},{16,20},{20,24},{24,28},{1,5},{5,9},{9,... | collective-permute-start | bytes 98312 | tf_op jit(solution)/shard_map/while/body/eval_jaxpr/ppermute | solution.py:28
  208.7 5.6 %collective-permute-start.2 = (f32[5,512]{1,0:T(8,128)S(1)}, f32[5,512]{1,0:T(8,128)S(1)}, u32[]{:S(2)}, u32[]{:S(2)}) collective-permute-start(f32[5,512]{1,0:T(8,128)S(1)} %get-tuple-element.551), channel_id=1, source_target_pairs={{0,1},{1,2},{2,3},{4,5},{5,6},{6,7},{8,9},{9,10},{10,11},{12,13},{... | collective-permute-start | bytes 30728 | tf_op jit(solution)/shard_map/while/body/eval_jaxpr/ppermute | solution.py:19
  215.4 6.1 %collective-permute-start = (f32[16,512]{1,0:T(8,128)S(1)}, f32[16,512]{1,0:T(8,128)S(1)}, u32[]{:S(2)}, u32[]{:S(2)}) collective-permute-start(f32[16,512]{1,0:T(8,128)S(1)} %get-tuple-element.570), channel_id=1, source_target_pairs={{0,4},{4,8},{8,12},{12,16},{16,20},{20,24},{24,28},{1,5},{5,9},{9,... | collective-permute-start | bytes 98312 | tf_op jit(solution)/shard_map/while/body/eval_jaxpr/ppermute | solution.py:28
  223.5 5.6 %collective-permute-start.2 = (f32[5,512]{1,0:T(8,128)S(1)}, f32[5,512]{1,0:T(8,128)S(1)}, u32[]{:S(2)}, u32[]{:S(2)}) collective-permute-start(f32[5,512]{1,0:T(8,128)S(1)} %get-tuple-element.551), channel_id=1, source_target_pairs={{0,1},{1,2},{2,3},{4,5},{5,6},{6,7},{8,9},{9,10},{10,11},{12,13},{... | collective-permute-start | bytes 30728 | tf_op jit(solution)/shard_map/while/body/eval_jaxpr/ppermute | solution.py:19
  229.2 6.1 %collective-permute-start = (f32[16,512]{1,0:T(8,128)S(1)}, f32[16,512]{1,0:T(8,128)S(1)}, u32[]{:S(2)}, u32[]{:S(2)}) collective-permute-start(f32[16,512]{1,0:T(8,128)S(1)} %get-tuple-element.570), channel_id=1, source_target_pairs={{0,4},{4,8},{8,12},{12,16},{16,20},{20,24},{24,28},{1,5},{5,9},{9,... | collective-permute-start | bytes 98312 | tf_op jit(solution)/shard_map/while/body/eval_jaxpr/ppermute | solution.py:28
  235.3 3.3 %collective-permute-start.1 = (f32[5,512]{1,0:T(8,128)S(1)}, f32[5,512]{1,0:T(8,128)S(1)}, u32[]{:S(2)}, u32[]{:S(2)}) collective-permute-start(f32[5,512]{1,0:T(8,128)S(1)} %get-tuple-element.550), channel_id=1, source_target_pairs={{1,0},{2,1},{3,2},{5,4},{6,5},{7,6},{9,8},{10,9},{11,10},{13,12},{... | collective-permute-start | bytes 30728 | tf_op jit(solution)/shard_map/while/body/eval_jaxpr/ppermute | solution.py:20
  237.2 5.6 %collective-permute-start.2 = (f32[5,512]{1,0:T(8,128)S(1)}, f32[5,512]{1,0:T(8,128)S(1)}, u32[]{:S(2)}, u32[]{:S(2)}) collective-permute-start(f32[5,512]{1,0:T(8,128)S(1)} %get-tuple-element.551), channel_id=1, source_target_pairs={{0,1},{1,2},{2,3},{4,5},{5,6},{6,7},{8,9},{9,10},{10,11},{12,13},{... | collective-permute-start | bytes 30728 | tf_op jit(solution)/shard_map/while/body/eval_jaxpr/ppermute | solution.py:19
  242.9 6.1 %collective-permute-start = (f32[16,512]{1,0:T(8,128)S(1)}, f32[16,512]{1,0:T(8,128)S(1)}, u32[]{:S(2)}, u32[]{:S(2)}) collective-permute-start(f32[16,512]{1,0:T(8,128)S(1)} %get-tuple-element.570), channel_id=1, source_target_pairs={{0,4},{4,8},{8,12},{12,16},{16,20},{20,24},{24,28},{1,5},{5,9},{9,... | collective-permute-start | bytes 98312 | tf_op jit(solution)/shard_map/while/body/eval_jaxpr/ppermute | solution.py:28
  251.0 5.6 %collective-permute-start.2 = (f32[5,512]{1,0:T(8,128)S(1)}, f32[5,512]{1,0:T(8,128)S(1)}, u32[]{:S(2)}, u32[]{:S(2)}) collective-permute-start(f32[5,512]{1,0:T(8,128)S(1)} %get-tuple-element.551), channel_id=1, source_target_pairs={{0,1},{1,2},{2,3},{4,5},{5,6},{6,7},{8,9},{9,10},{10,11},{12,13},{... | collective-permute-start | bytes 30728 | tf_op jit(solution)/shard_map/while/body/eval_jaxpr/ppermute | solution.py:19
  (9 other events, 169.6 us)
where the time goes:
time: 260 us; the launch traced here: 258 us
  waiting for transfers between devices  80.7 us (31%)
  starting transfers between devices  79.9 us (31%)
  other arithmetic  44.8 us (17%)
  between operations  26.6 us (10%)
  local copies, waits for them, and re-layouts  25.3 us (10%)
    ppermute x13, starting transfers between devices, with_halo(): after = lax.ppermute(first, axis, down)  45.5 us
    ppermute x13, waiting for transfers between devices, with_halo(): before = lax.ppermute(last, axis, up)  42.1 us
    select_n x38, other arithmetic, sweep(): widened = jnp.where((fine_step < counts)[:, None, None], updated, widened)  35.4 us
    ppermute x9, waiting for transfers between devices, passed_along(): lax.ppermute(value, axis, [(source, source + steps) for source in range(f...  33.6 us
    ppermute x9, starting transfers between devices, passed_along(): lax.ppermute(value, axis, [(source, source + steps) for source in range(f...  17.5 us
    ppermute x13, starting transfers between devices, with_halo(): before = lax.ppermute(last, axis, up)  16.9 us
    slice x45, local copies, waits for them, and re-layouts, neighbours(): left_col = jnp.concatenate([zero_col, values[..., :, :-1]], axis=-1)  5.8 us
  transfers between devices with their start and end apart: 35, of which 29 were waited for; matrix products, arithmetic and copies ran while one was open for 6% of the time, Pallas kernels for 0%

commit v1 on v0

v1 whole, which is shorter than its diff:
```python
import functools

import jax
import jax.numpy as jnp
from jax import lax
from jax.experimental import pallas as pl
from jax.experimental.pallas import tpu as pltpu
from jax.sharding import PartitionSpec as P

STEP_MOST = 20
CSUB = 5
BLK_R = 8
BLK_C = 128
SUB = 8
LANES = 128
MAIN = STEP_MOST // SUB * SUB
REST = STEP_MOST - MAIN
HALO = -(-STEP_MOST // SUB) * SUB
HT = HALO // SUB
PAD = SUB
VM = pl.BlockSpec(memory_space=pltpu.VMEM)
SM = pl.BlockSpec(memory_space=pltpu.SMEM)
F32 = jnp.float32


def f32(*shape):
    return jax.ShapeDtypeStruct(shape, F32)


def call(body, ins, outs, scratch, flops):
    return pl.pallas_call(
        body,
        out_shape=outs,
        in_specs=ins,
        out_specs=jax.tree.map(lambda _: VM, outs),
        scratch_shapes=scratch,
        cost_estimate=pl.CostEstimate(flops=flops, bytes_accessed=1 << 20, transcendentals=0),
    )


def iota(axis, shape=(SUB, LANES)):
    return lax.broadcasted_iota(jnp.int32, shape, axis)


def cols(c):
    return slice(c * LANES, (c + 1) * LANES)


def beside(tiles, c, left_edge=None):
    lane = iota(1)
    before = pltpu.roll(tiles[c], 1, 1)
    after = pltpu.roll(tiles[c], LANES - 1, 1)
    if c > 0:
        before = jnp.where(lane == 0, pltpu.roll(tiles[c - 1], 1, 1), before)
    elif left_edge is not None:
        before = jnp.where(lane == 0, left_edge, before)
    if c + 1 < len(tiles):
        after = jnp.where(lane == LANES - 1, pltpu.roll(tiles[c + 1], LANES - 1, 1), after)
    elif left_edge is not None:
        after = jnp.where(lane == LANES - 1, left_edge, after)
    return before, after


def halve():
    wide, narrow = iota(0, (2 * LANES, LANES)), iota(1, (2 * LANES, LANES))
    return jnp.where(wide // 2 == narrow, 1.0, 0.0).astype(F32)


def double():
    narrow, wide = iota(0, (LANES, 2 * LANES)), iota(1, (LANES, 2 * LANES))
    return jnp.where(wide // 2 == narrow, 1.0, 0.0).astype(F32)


def dot(a, b):
    return jnp.dot(a, b, precision=lax.Precision.HIGHEST, preferred_element_type=F32)


def row_pairs(ref, index, first, rows):
    top = ref[(*index, pl.ds(first, rows, stride=2), slice(None))]
    return top + ref[(*index, pl.ds(first + 1, rows, stride=2), slice(None))]


def pack_body(point, rate, source, table, classes, pay_a, pay_b, coarse, tmp):
    rows, width = point.shape
    blocks, tiles = rows // BLK_R, width // LANES
    odd = lax.rem(lax.axis_index("space"), 2) == 1

    def fill(out, high):
        main = rows - MAIN if high else 0
        rest = rows - MAIN - REST if high else MAIN
        for i, ref in enumerate((point, rate, source)):
            out[i * MAIN : (i + 1) * MAIN, :] = ref[main : main + MAIN, :]
            at = 3 * MAIN + i * REST
            out[at : at + REST, :] = ref[rest : rest + REST, :]
        first = blocks - HT if high else 0
        for b in range(HT):
            for c in range(tiles):
                value = table[classes[first + b, c]]
                at = 3 * MAIN + 3 * REST + b
                out[at : at + 1, cols(c)] = jnp.full((1, LANES), value, F32)

    @pl.when(odd)
    def _():
        fill(pay_a, False)
        fill(pay_b, True)

    @pl.when(jnp.logical_not(odd))
    def _():
        fill(pay_a, True)
        fill(pay_b, False)

    for c in range(tiles):
        tmp[c, :, :] = rate[:, cols(c)]
    pairs = halve()
    for c in range(tiles // 2):
        wide = jnp.concatenate([row_pairs(tmp, (2 * c + k,), 0, rows // 2) for k in (0, 1)], axis=1)
        coarse[: rows // 2, cols(c)] = 0.25 * dot(wide, pairs)
        for b in range(blocks):
            halves = [jnp.full((1, LANES), table[classes[b, 2 * c + k]], F32) for k in (0, 1)]
            at = rows // 2 + b
            coarse[at : at + 1, cols(c)] = jnp.where(iota(1, (1, LANES)) < LANES // 2, halves[0], halves[1])


def sweep(state, weights, force, count, tiles, strip_tiles, wave):
    def step(t, reach):
        now = lax.rem(t, 2)
        amount = None if wave is None else wave(t)
        for r in range(HT - reach, HT + strip_tiles + reach):
            at = PAD + r * SUB
            here = [state[now, c, at : at + SUB, :] for c in range(tiles)]
            for c in range(tiles):
                left, right = beside(here, c)
                above = state[now, c, at - 1 : at + SUB - 1, :]
                below = state[now, c, at + 1 : at + SUB + 1, :]
                w = [weights[k, c, r * SUB : (r + 1) * SUB, :] for k in range(5)]
                new = (w[0] * here[c] + w[1] * above) + (w[2] * below + w[3] * left) + w[4] * right
                if amount is not None:
                    new = new + amount * force[c, r * SUB : (r + 1) * SUB, :]
                state[1 - now, c, at : at + SUB, :] = new

    begin = 0
    for reach in range(HT, -1, -1):
        if reach == HT:
            steps = jnp.maximum(count - 1 - SUB * (HT - 1), 0)
        elif reach > 0:
            steps = jnp.clip(count - 1 - SUB * (reach - 1), 0, SUB)
        else:
            steps = 1
        lax.fori_loop(begin, begin + steps, lambda t, _, reach=reach: step(t, reach), None)
        begin = begin + steps
    return lax.rem(count, 2)


def with_halos(odd, got_a, got_b, place):
    @pl.when(odd)
    def _():
        place(got_a, True)
        place(got_b, False)

    @pl.when(jnp.logical_not(odd))
    def _():
        place(got_b, True)
        place(got_a, False)


def unpack(out, lead, tiles, rows, payload, above, which, at=0):
    for c in range(tiles):
        if above:
            main, rest = at + HALO - MAIN, at + HALO - MAIN - REST
        else:
            main, rest = at + HALO + rows, at + HALO + rows + MAIN
        first = 3 * MAIN + which * REST
        out[(*lead, c, slice(main, main + MAIN), slice(None))] = payload[which * MAIN : (which + 1) * MAIN, cols(c)]
        out[(*lead, c, slice(rest, rest + REST), slice(None))] = payload[first : first + REST, cols(c)]


def first_body(
    point, rate, source, got_a, got_b, initial, table, classes, steps, waveform,
    relaxed, edge_a, edge_b, weights, state, force, rates, conduct,
):
    rows, width = point.shape
    tiles, strip_tiles, blocks = width // LANES, rows // SUB, rows // BLK_R
    mine, strip = lax.axis_index("tm"), lax.axis_index("space")
    odd = lax.rem(strip, 2) == 1
    start = lax.fori_loop(0, mine, lambda i, total: total + steps[i], jnp.int32(0))
    count = steps[mine]

    for c in range(tiles):
        for r in range(strip_tiles):
            at, to = slice(r * SUB, (r + 1) * SUB), slice(HALO + r * SUB, HALO + (r + 1) * SUB)
            state[0, c, PAD + HALO + r * SUB : PAD + HALO + (r + 1) * SUB, :] = point[at, cols(c)]
            rates[c, to, :] = rate[at, cols(c)]
            force[c, to, :] = source[at, cols(c)]
        for b in range(blocks):
            at = PAD + HALO + b * BLK_R
            conduct[c, at : at + BLK_R, :] = jnp.full((BLK_R, LANES), table[classes[b, c]], F32)
        zero = jnp.zeros((SUB, LANES), F32)
        conduct[c, 0:PAD, :] = zero
        conduct[c, PAD + 2 * HALO + rows :, :] = zero
        for at in (0, HALO + rows + HALO - SUB):
            rates[c, at : at + SUB, :] = zero
            force[c, at : at + SUB, :] = zero
            state[0, c, PAD + at : PAD + at + SUB, :] = zero

    def place(payload, above):
        unpack(state, (0,), tiles, rows, payload, above, 0, PAD)
        unpack(rates, (), tiles, rows, payload, above, 1)
        unpack(force, (), tiles, rows, payload, above, 2)
        for b in range(HT):
            at = PAD + b * BLK_R + (0 if above else HALO + rows)
            row = 3 * MAIN + 3 * REST + b
            for c in range(tiles):
                conduct[c, at : at + BLK_R, :] = jnp.broadcast_to(payload[row : row + 1, cols(c)], (BLK_R, LANES))

    with_halos(odd, got_a, got_b, place)

    zero = jnp.zeros((SUB, LANES), F32)
    for r in range(2 * HT + strip_tiles):
        at = PAD + r * SUB
        here = [conduct[c, at : at + SUB, :] for c in range(tiles)]
        for c in range(tiles):
            left, right = beside(here, c, zero)
            above = conduct[c, at - 1 : at + SUB - 1, :]
            below = conduct[c, at + 1 : at + SUB + 1, :]
            own = rates[c, r * SUB : (r + 1) * SUB, :]
            w = [own * jnp.sqrt(here[c] * other) for other in (above, below, left, right)]
            weights[0, c, r * SUB : (r + 1) * SUB, :] = 1.0 - (((w[0] + w[1]) + w[2]) + w[3])
            for k in range(4):
                weights[k + 1, c, r * SUB : (r + 1) * SUB, :] = w[k]

    now = sweep(state, weights, force, count, tiles, strip_tiles, lambda t: waveform[start + t])

    def give(read):
        for c in range(tiles):
            for r in range(strip_tiles):
                relaxed[r * SUB : (r + 1) * SUB, cols(c)] = read(r, c)

        @pl.when(odd)
        def _():
            for c in range(tiles):
                for r in range(HT):
                    edge_a[r * SUB : (r + 1) * SUB, cols(c)] = read(r, c)
                    edge_b[r * SUB : (r + 1) * SUB, cols(c)] = read(strip_tiles - HT + r, c)

        @pl.when(jnp.logical_not(odd))
        def _():
            for c in range(tiles):
                for r in range(HT):
                    edge_b[r * SUB : (r + 1) * SUB, cols(c)] = read(r, c)
                    edge_a[r * SUB : (r + 1) * SUB, cols(c)] = read(strip_tiles - HT + r, c)

    last = mine == lax.axis_size("tm") - 1

    @pl.when(last)
    def _():
        give(lambda r, c: initial[r * SUB : (r + 1) * SUB, cols(c)])

    @pl.when(jnp.logical_not(last))
    def _():
        give(lambda r, c: state[now, c, pl.ds(PAD + HALO + r * SUB, SUB), :])


def second_body(relaxed, edge_a, edge_b, point, got_a, got_b, weights, steps, coarse, state, tmp):
    rows, width = point.shape
    tiles, strip_tiles = width // LANES, rows // SUB
    mine, strip = lax.axis_index("tm"), lax.axis_index("space")
    odd = lax.rem(strip, 2) == 1
    count = steps[mine]
    for c in range(tiles):
        for r in range(strip_tiles):
            at = slice(r * SUB, (r + 1) * SUB)
            to = PAD + HALO + r * SUB
            state[0, c, to : to + SUB, :] = relaxed[at, cols(c)] - point[at, cols(c)]
        for at in (0, HALO + rows + HALO - SUB):
            tmp[c, at : at + SUB, :] = jnp.zeros((SUB, LANES), F32)

    def place(pair, above):
        edge, payload = pair
        unpack(tmp, (), tiles, rows, payload, above, 0)
        base = 0 if above else HALO + rows
        for c in range(tiles):
            for r in range(HT):
                at = base + r * SUB
                state[0, c, PAD + at : PAD + at + SUB, :] = edge[r * SUB : (r + 1) * SUB, cols(c)] - tmp[c, at : at + SUB, :]

    with_halos(odd, (edge_a, got_a), (edge_b, got_b), place)
    now = sweep(state, weights, None, count, tiles, strip_tiles, None)
    pairs = halve()
    for c in range(tiles // 2):
        wide = [row_pairs(state, (now, 2 * c + k), PAD + HALO, rows // 2) for k in (0, 1)]
        coarse[:, cols(c)] = 0.25 * dot(jnp.concatenate(wide, axis=1), pairs)


def assemble_body(strips, fields, total, weights, conduct):
    count = len(strips)
    rows, width = strips[0].shape
    tiles = width // LANES
    mine = lax.axis_index("space")
    per_block = BLK_R // 2
    zero = jnp.zeros((SUB, LANES), F32)
    for c in range(tiles):
        conduct[c, 0:PAD, :] = zero
        conduct[c, PAD + count * rows :, :] = zero
    for k in range(count):
        base = (mine ^ k) * rows
        for c in range(tiles):
            for r in range(rows // SUB):
                to = pl.multiple_of(base + r * SUB, SUB)
                total[c, pl.ds(to, SUB), :] = strips[k][r * SUB : (r + 1) * SUB, cols(c)]
                weights[0, c, pl.ds(to, SUB), :] = fields[k][r * SUB : (r + 1) * SUB, cols(c)]
                block = rows + r * (SUB // per_block)
                two = [jnp.broadcast_to(fields[k][block + i : block + i + 1, cols(c)], (SUB, LANES)) for i in (0, 1)]
                conduct[c, pl.ds(PAD + to, SUB), :] = jnp.where(iota(0) < per_block, two[0], two[1])
    for r in range(count * rows // SUB):
        at = PAD + r * SUB
        here = [conduct[c, at : at + SUB, :] for c in range(tiles)]
        for c in range(tiles):
            left, right = beside(here, c, zero)
            above = conduct[c, at - 1 : at + SUB - 1, :]
            below = conduct[c, at + 1 : at + SUB + 1, :]
            own = weights[0, c, r * SUB : (r + 1) * SUB, :]
            w = [own * jnp.sqrt(here[c] * other) for other in (above, below, left, right)]
            weights[0, c, r * SUB : (r + 1) * SUB, :] = ((w[0] + w[1]) + w[2]) + w[3]
            for k in range(4):
                weights[k + 1, c, r * SUB : (r + 1) * SUB, :] = w[k]


def link_steps(state, weights, factor):
    _, tiles, padded, _ = state.shape

    def step(now):
        for r in range((padded - 2 * PAD) // SUB):
            at = PAD + r * SUB
            here = [state[now, c, at : at + SUB, :] for c in range(tiles)]
            for c in range(tiles):
                left, right = beside(here, c)
                above = state[now, c, at - 1 : at + SUB - 1, :]
                below = state[now, c, at + 1 : at + SUB + 1, :]
                w = [weights[k, c, r * SUB : (r + 1) * SUB, :] for k in range(5)]
                change = (w[1] * above + w[2] * below) + (w[3] * left + w[4] * right) - w[0] * here[c]
                state[1 - now, c, at : at + SUB, :] = here[c] + factor * change

    def one(i, now):
        step(now)
        return 1 - now

    return one


def scan_body(stage, final, refs):
    total, got, before, weights, steps = refs[:5]
    tiles, height, _ = total.shape
    size = 1 << stage
    mine, strip = lax.axis_index("tm"), lax.axis_index("space")
    upper = lax.rem(mine // size, 2) == 1
    first = (mine // (2 * size)) * (2 * size) + size
    if final:
        relaxed, out, state, errors, tmp = refs[5:]
        rows = 2 * relaxed.shape[0] // 4
    else:
        total_out, errors, state = refs[5:]
        rows = errors.shape[1]
    mine_rows = pl.multiple_of(strip * rows, SUB)
    zero = jnp.zeros((SUB, LANES), F32)
    for c in range(tiles):
        for b in (0, 1):
            state[b, c, 0:PAD, :] = zero
            state[b, c, PAD + height :, :] = zero

    def load(ref):
        for c in range(tiles):
            for r in range(height // SUB):
                state[0, c, PAD + r * SUB : PAD + (r + 1) * SUB, :] = ref[c, r * SUB : (r + 1) * SUB, :]

    @pl.when(upper)
    def _():
        load(got)

    @pl.when(jnp.logical_not(upper))
    def _():
        load(total)

    def keep(now):
        for c in range(tiles):
            piece = state[now, c, pl.ds(PAD + mine_rows, rows), :]
            errors[c, :, :] = piece if before is None else before[c, :, :] + piece

    def pass_on():
        for c in range(tiles):
            if before is None:
                errors[c, :, :] = jnp.zeros((rows, LANES), F32)
            else:
                errors[c, :, :] = before[c, :, :]

    pass_on()

    def turn(i, now):
        @pl.when(jnp.logical_and(upper, first + i == mine))
        def _():
            keep(now)

        factor = steps[first + i].astype(F32) * (1.0 / (4.0 * CSUB))
        return lax.fori_loop(0, CSUB, link_steps(state, weights, factor), now)

    if final:
        turns = jnp.where(upper, mine - first, 0)
        now = lax.fori_loop(0, turns, turn, jnp.int32(0))

        @pl.when(upper)
        def _():
            keep(now)

        pairs = double()
        for c in range(tiles):
            wide = dot(errors[c, :, :], pairs)
            for k in (0, 1):
                part = wide[:, k * LANES : (k + 1) * LANES]
                tmp[2 * c + k, pl.ds(0, rows, stride=2), :] = part
                tmp[2 * c + k, pl.ds(1, rows, stride=2), :] = part
        for c in range(2 * tiles):
            out[:, cols(c)] = relaxed[:, cols(c)] + tmp[c, :, :]
    else:
        now = lax.fori_loop(0, size, turn, jnp.int32(0))

        def close(ref):
            for c in range(tiles):
                for r in range(height // SUB):
                    at = slice(r * SUB, (r + 1) * SUB)
                    total_out[c, at, :] = ref[c, at, :] + state[now, c, pl.ds(PAD + r * SUB, SUB), :]

        @pl.when(upper)
        def _():
            close(total)

        @pl.when(jnp.logical_not(upper))
        def _():
            close(got)


def shards(point_states, initial_state, node_rate, source_map, waveform, cond_table, class_map, interval_steps):
    assert point_states.shape[0] == 1
    intervals, strips = lax.axis_size("tm"), lax.axis_size("space")
    assert intervals & (intervals - 1) == 0 and strips & (strips - 1) == 0
    point = point_states[0]
    rows, width = point.shape
    tiles, ctiles, crows, blocks = width // LANES, width // LANES // 2, rows // 2, rows // BLK_R
    height, cheight = rows + 2 * HALO, crows * strips
    packed = -(-(3 * STEP_MOST + HT) // SUB) * SUB
    fields_rows = -(-(crows + blocks) // SUB) * SUB
    both = ("tm", "space")

    def side(s, which):
        other = s ^ 1 if which == "a" else (s + 1 if s % 2 else s - 1)
        return other if 0 <= other < strips else None

    def exchange(value, ahead, move):
        pairs = []
        for j in range(intervals):
            for s in range(strips):
                to = move(s)
                if to is not None:
                    pairs.append((j * strips + s, ((j + ahead) % intervals) * strips + to))
        return lax.ppermute(value, both, pairs)

    pay_a, pay_b, field = call(
        pack_body, [VM, VM, VM, SM, SM],
        (f32(packed, width), f32(packed, width), f32(fields_rows, width // 2)),
        [pltpu.VMEM((tiles, rows, LANES), F32)], 1 << 20,
    )(point, node_rate, source_map, cond_table, class_map)
    got_a = exchange(pay_a, 0, lambda s: side(s, "a"))
    got_b = exchange(pay_b, 0, lambda s: side(s, "b"))
    fields = [field] + [exchange(field, 0, lambda s, k=k: s ^ k) for k in range(1, strips)]

    passed, edge_a, edge_b, weights = call(
        first_body, [VM] * 6 + [SM] * 4,
        (f32(rows, width), f32(HALO, width), f32(HALO, width), f32(5, tiles, height, LANES)),
        [
            pltpu.VMEM((2, tiles, height + 2 * PAD, LANES), F32),
            pltpu.VMEM((tiles, height, LANES), F32),
            pltpu.VMEM((tiles, height, LANES), F32),
            pltpu.VMEM((tiles, height + 2 * PAD, LANES), F32),
        ],
        1 << 24,
    )(point, node_rate, source_map, got_a, got_b, initial_state, cond_table, class_map, interval_steps, waveform)
    relaxed = exchange(passed, 1, lambda s: s)
    edge_a = exchange(edge_a, 1, lambda s: side(s, "a"))
    edge_b = exchange(edge_b, 1, lambda s: side(s, "b"))

    change = call(
        second_body, [VM] * 7 + [SM], f32(crows, width // 2),
        [pltpu.VMEM((2, tiles, height + 2 * PAD, LANES), F32), pltpu.VMEM((tiles, height, LANES), F32)],
        1 << 24,
    )(relaxed, edge_a, edge_b, point, got_a, got_b, weights, interval_steps)
    changes = [change] + [exchange(change, 0, lambda s, k=k: s ^ k) for k in range(1, strips)]

    def assemble(*refs):
        assemble_body(refs[:strips], refs[strips : 2 * strips], *refs[2 * strips :])

    total, coarse_weights = call(
        assemble, [VM] * (2 * strips), (f32(ctiles, cheight, LANES), f32(5, ctiles, cheight, LANES)),
        [pltpu.VMEM((ctiles, cheight + 2 * PAD, LANES), F32)], 1 << 20,
    )(*changes, *fields)

    errors = None
    stages = intervals.bit_length() - 1
    for stage in range(stages):
        got = lax.ppermute(total, "tm", [(j, j ^ (1 << stage)) for j in range(intervals)])
        final = stage == stages - 1
        some = errors is not None

        def body(*refs, stage=stage, final=final, some=some):
            refs = refs if some else (*refs[:2], None, *refs[2:])
            scan_body(stage, final, refs)

        state = pltpu.VMEM((2, ctiles, cheight + 2 * PAD, LANES), F32)
        lead = [total, got] + ([errors] if some else []) + [coarse_weights, interval_steps]
        specs = [VM] * (len(lead) - 1) + [SM]
        if final:
            out = call(
                body, specs + [VM], f32(rows, width),
                [state, pltpu.VMEM((ctiles, crows, LANES), F32), pltpu.VMEM((tiles, rows, LANES), F32)], 1 << 23,
            )(*lead, relaxed)
        else:
            total, errors = call(
                body, specs, (f32(ctiles, cheight, LANES), f32(ctiles, crows, LANES)), [state], 1 << 23
            )(*lead)
    return out[None]


def solution(mesh):
    placed = (
        P("tm", "space", None),
        P("space", None),
        P("space", None),
        P("space", None),
        P(),
        P(),
        P("space", None),
        P(),
    )
    return jax.shard_map(shards, mesh=mesh, in_specs=placed, out_specs=P("tm", "space", None), check_vma=False)
```

time: 260 us -> 95.2 us (0.37)
  the two profiles are of different devices: /device:TPU:28 before, /device:TPU:7 now
where the time goes in v1:
time: 95.2 us; the launch traced here: 94.8 us
  Pallas kernels  52.1 us (55%)
  starting transfers between devices  20.7 us (22%)
  waiting for transfers between devices  17.2 us (18%)
  local copies, waits for them, and re-layouts  4.68 us (5%)
    pallas_call x2, Pallas kernels, shards(): call(body, specs, (f32(ctiles, cheight, LANES), f32(ctiles, crows, LANES)...  16.1 us
    ppermute x11, starting transfers between devices, exchange(): return lax.ppermute(value, both, pairs)  16 us
    pallas_call x1, Pallas kernels, shards(): call(body, specs + [VM], f32(rows, width), [state, pltpu.VMEM((ctiles, cr...  14.4 us
    pallas_call x1, Pallas kernels, shards(): call(first_body, [VM] * 6 + [SM] * 4, (f32(rows, width), f32(HALO, width)...  9.03 us
    ppermute x3, waiting for transfers between devices, shards(): lax.ppermute(total, 'tm', [(j, j ^ 1 << stage) for j in range(intervals)])  9 us
    pallas_call x1, Pallas kernels, shards(): call(second_body, [VM] * 7 + [SM], f32(crows, width // 2), [pltpu.VMEM((2...  8.56 us
    ppermute x11, waiting for transfers between devices, exchange(): return lax.ppermute(value, both, pairs)  8.17 us
    ppermute x3, starting transfers between devices, shards(): lax.ppermute(total, 'tm', [(j, j ^ 1 << stage) for j in range(intervals)])  4.74 us
  transfers between devices with their start and end apart: 14, of which 6 were waited for; matrix products, arithmetic and copies ran while one was open for 0% of the time, Pallas kernels for 9%

profile of v1, /device:TPU:7, one launch (start us, length us, event | category | flops | bytes accessed | tf_op | source)
XLA Modules:
  0.0 94.8 jit_solution(9988086974790258854)
XLA Ops:
  0.0 2.1 %shard_map.82 = (f32[64,1024]{1,0:T(8,128)}, f32[64,1024]{1,0:T(8,128)}, f32[24,512]{1,0:T(8,128)}) custom-call(f32[32,1024]{1,0:T(8,128)} %bitcast.2, f32[32,1024]{1,0:T(8,128)} %rate.3, f32[32,1024]{1,0:T(8,128)} %source.3, f32[16]{0:T(128)} %table.3, s32[4,8]{1,0:T(4,128)} %classes.3), custom_call_target="tpu_custom_call" | custom-call | flops 1048576 | bytes 1048576 | tf_op jit(solution)/shard_map/pallas_call | solution.py:465
  2.1 1.3 %collective-permute-start = (f32[64,1024]{1,0:T(8,128)}, f32[64,1024]{1,0:T(8,128)S(1)}, u32[]{:S(2)}, u32[]{:S(2)}) collective-permute-start(f32[64,1024]{1,0:T(8,128)} %get-tuple-element.18), channel_id=1, source_target_pairs={{0,1},{1,0},{2,3},{3,2},{4,5},{5,4},{6,7},{7,6},{8,9},{9,8},{10,11... | collective-permute-start | bytes 786440 | tf_op jit(solution)/shard_map/ppermute | solution.py:463
  3.4 0.7 collective-permute-start.1
  4.1 5.4 %collective-permute-done.got_a = f32[64,1024]{1,0:T(8,128)S(1)} collective-permute-done((f32[64,1024]{1,0:T(8,128)}, f32[64,1024]{1,0:T(8,128)S(1)}, u32[]{:S(2)}, u32[]{:S(2)}) %collective-permute-start) | collective-permute-done | bytes 262176 | tf_op jit(solution)/shard_map/ppermute | solution.py:463
  9.5 0.7 copy-done
  10.2 0.7 copy-done.1
  10.9 9.0 %shard_map.83 = (f32[32,1024]{1,0:T(8,128)}, f32[24,1024]{1,0:T(8,128)}, f32[24,1024]{1,0:T(8,128)}, f32[5,8,80,128]{3,2,1,0:T(8,128)}) custom-call(f32[32,1024]{1,0:T(8,128)} %bitcast.3, f32[32,1024]{1,0:T(8,128)} %rate.3, f32[32,1024]{1,0:T(8,128)} %source.3, f32[64,1024]{1,0:T(8,128)} %copy-done, f32[64,1024]{1,0:T(8,128)} %copy-done.1, ...), custom_call_target="tpu_custom_call" | custom-call | flops 16777216 | bytes 1048576 | tf_op jit(solution)/shard_map/pallas_call | solution.py:474
  19.9 2.3 %collective-permute-start.3 = (f32[24,1024]{1,0:T(8,128)}, f32[24,1024]{1,0:T(8,128)S(1)}, u32[]{:S(2)}, u32[]{:S(2)}) collective-permute-start(f32[24,1024]{1,0:T(8,128)} %get-tuple-element.21), channel_id=1, source_target_pairs={{0,5},{1,4},{2,7},{3,6},{4,9},{5,8},{6,11},{7,10},{8,13},{9,12},{1... | collective-permute-start | bytes 294920 | tf_op jit(solution)/shard_map/ppermute | solution.py:463
  22.3 0.7 collective-permute-start.4
  22.9 2.1 %collective-permute-start.10 = (f32[24,512]{1,0:T(8,128)}, f32[24,512]{1,0:T(8,128)S(1)}, u32[]{:S(2)}, u32[]{:S(2)}) collective-permute-start(f32[24,512]{1,0:T(8,128)} %get-tuple-element.24.refs_4_), channel_id=1, source_target_pairs={{0,3},{1,2},{2,1},{3,0},{4,7},{5,6},{6,5},{7,4},{8,11},{9,10},{10,... | collective-permute-start | bytes 147464 | tf_op jit(solution)/shard_map/ppermute | solution.py:463
  25.1 3.6 %collective-permute-start.8 = (f32[24,512]{1,0:T(8,128)}, f32[24,512]{1,0:T(8,128)S(1)}, u32[]{:S(2)}, u32[]{:S(2)}) collective-permute-start(f32[24,512]{1,0:T(8,128)} %get-tuple-element.24.refs_4_), channel_id=1, source_target_pairs={{0,1},{1,0},{2,3},{3,2},{4,5},{5,4},{6,7},{7,6},{8,9},{9,8},{10,11... | collective-permute-start | bytes 147464 | tf_op jit(solution)/shard_map/ppermute | solution.py:463
  28.7 1.2 %collective-permute-start.9 = (f32[24,512]{1,0:T(8,128)}, f32[24,512]{1,0:T(8,128)S(1)}, u32[]{:S(2)}, u32[]{:S(2)}) collective-permute-start(f32[24,512]{1,0:T(8,128)} %get-tuple-element.24.refs_4_), channel_id=1, source_target_pairs={{0,2},{1,3},{2,0},{3,1},{4,6},{5,7},{6,4},{7,5},{8,10},{9,11},{10,... | collective-permute-start | bytes 147464 | tf_op jit(solution)/shard_map/ppermute | solution.py:463
  29.9 0.6 copy-done.7
  30.6 8.6 %shard_map.84.refs_0_ = f32[16,512]{1,0:T(8,128)} custom-call(f32[32,1024]{1,0:T(8,128)} %copy-done.2, f32[24,1024]{1,0:T(8,128)} %copy-done.6, f32[24,1024]{1,0:T(8,128)} %copy-done.7, f32[32,1024]{1,0:T(8,128)} %bitcast.4, f32[64,1024]{1,0:T(8,128)} %copy-done, f32[64,1024]{1,0:T(8,128)} %copy-done.1, f32[5,8,80,128]{3,2,1,0:T(8,128)} %get-tuple-element.23.weights, ...), custom_call_target="tpu_custom_call" | custom-call | flops 16777216 | bytes 1048576 | tf_op jit(solution)/shard_map/pallas_call | solution.py:489
  39.1 2.0 %collective-permute-start.5 = (f32[16,512]{1,0:T(8,128)}, f32[16,512]{1,0:T(8,128)S(1)}, u32[]{:S(2)}, u32[]{:S(2)}) collective-permute-start(f32[16,512]{1,0:T(8,128)} %shard_map.84.refs_0_), channel_id=1, source_target_pairs={{0,1},{1,0},{2,3},{3,2},{4,5},{5,4},{6,7},{7,6},{8,9},{9,8},{10,11... | collective-permute-start | bytes 98312 | tf_op jit(solution)/shard_map/ppermute | solution.py:463
  41.2 2.1 %collective-permute-start.7 = (f32[16,512]{1,0:T(8,128)}, f32[16,512]{1,0:T(8,128)S(1)}, u32[]{:S(2)}, u32[]{:S(2)}) collective-permute-start(f32[16,512]{1,0:T(8,128)} %shard_map.84.refs_0_), channel_id=1, source_target_pairs={{0,3},{1,2},{2,1},{3,0},{4,7},{5,6},{6,5},{7,4},{8,11},{9,10},{10,... | collective-permute-start | bytes 98312 | tf_op jit(solution)/shard_map/ppermute | solution.py:463
  43.3 1.9 %collective-permute-done.6.refs_2_ = f32[16,512]{1,0:T(8,128)S(1)} collective-permute-done((f32[16,512]{1,0:T(8,128)}, f32[16,512]{1,0:T(8,128)S(1)}, u32[]{:S(2)}, u32[]{:S(2)}) %collective-permute-start.6) | collective-permute-done | bytes 32800 | tf_op jit(solution)/shard_map/ppermute | solution.py:463
  45.2 0.8 collective-permute-done.7.refs_3_
  46.1 0.6 copy-done.13
  46.7 2.0 %shard_map.85 = (f32[4,64,128]{2,1,0:T(8,128)}, f32[5,4,64,128]{3,2,1,0:T(8,128)}) custom-call(f32[16,512]{1,0:T(8,128)} %shard_map.84.refs_0_, f32[16,512]{1,0:T(8,128)} %copy-done.11, f32[16,512]{1,0:T(8,128)} %copy-done.12, f32[16,512]{1,0:T(8,128)} %copy-done.13, f32[24,512]{1,0:T(8,128)} %get-tuple-element.24.refs_4_, f32[24,512]{1,0:T(8,128)} %copy-done.9, ...), custom_call_target="tpu_custom_call" | custom-call | flops 1048576 | bytes 1048576 | tf_op jit(solution)/shard_map/pallas_call | solution.py:499
  48.7 3.6 %collective-permute-start.11 = (f32[4,64,128]{2,1,0:T(8,128)}, f32[4,64,128]{2,1,0:T(8,128)S(1)}, u32[]{:S(2)}, u32[]{:S(2)}) collective-permute-start(f32[4,64,128]{2,1,0:T(8,128)} %get-tuple-element.25.refs_0_), channel_id=1, source_target_pairs={{0,4},{4,0},{8,12},{12,8},{16,20},{20,16},{24,28},{28,24},{1,5},{5... | collective-permute-start | bytes 393224 | tf_op jit(solution)/shard_map/ppermute | solution.py:507
  52.3 1.2 %collective-permute-done.11.refs_1_ = f32[4,64,128]{2,1,0:T(8,128)S(1)} collective-permute-done((f32[4,64,128]{2,1,0:T(8,128)}, f32[4,64,128]{2,1,0:T(8,128)S(1)}, u32[]{:S(2)}, u32[]{:S(2)}) %collective-permute-start.11) | collective-permute-done | bytes 131104 | tf_op jit(solution)/shard_map/ppermute | solution.py:507
  53.5 0.7 copy-done.5
  54.1 6.0 %shard_map.86 = (f32[4,64,128]{2,1,0:T(8,128)}, f32[4,16,128]{2,1,0:T(8,128)}) custom-call(f32[4,64,128]{2,1,0:T(8,128)} %get-tuple-element.25.refs_0_, f32[4,64,128]{2,1,0:T(8,128)} %copy-done.5, f32[5,4,64,128]{3,2,1,0:T(8,128)} %get-tuple-element.26.refs_2_.refs_3_, s32[8]{0:T(128)} %refs_4_.3), custom_call_target="tpu_custom_call" | custom-call | flops 8388608 | bytes 1048576 | tf_op jit(solution)/shard_map/pallas_call | solution.py:524
  60.2 0.9 collective-permute-start.12
  61.1 4.0 %collective-permute-done.12.refs_1_ = f32[4,64,128]{2,1,0:T(8,128)S(1)} collective-permute-done((f32[4,64,128]{2,1,0:T(8,128)}, f32[4,64,128]{2,1,0:T(8,128)S(1)}, u32[]{:S(2)}, u32[]{:S(2)}) %collective-permute-start.12) | collective-permute-done | bytes 131104 | tf_op jit(solution)/shard_map/ppermute | solution.py:507
  65.1 0.7 copy-done.3
  65.7 10.1 %shard_map.87 = (f32[4,64,128]{2,1,0:T(8,128)}, f32[4,16,128]{2,1,0:T(8,128)}) custom-call(f32[4,64,128]{2,1,0:T(8,128)} %get-tuple-element.27.refs_0_, f32[4,64,128]{2,1,0:T(8,128)} %copy-done.3, f32[4,16,128]{2,1,0:T(8,128)} %get-tuple-element.28.refs_2_, f32[5,4,64,128]{3,2,1,0:T(8,128)} %get-tuple-element.26.refs_2_.refs_3_, s32[8]{0:T(128)} %refs_4_.3), custom_call_target="tpu_custom_call" | custom-call | flops 8388608 | bytes 1048576 | tf_op jit(solution)/shard_map/pallas_call | solution.py:524
  75.8 0.2 collective-permute-start.13
  76.0 3.8 %collective-permute-done.13.refs_1_ = f32[4,64,128]{2,1,0:T(8,128)S(1)} collective-permute-done((f32[4,64,128]{2,1,0:T(8,128)}, f32[4,64,128]{2,1,0:T(8,128)S(1)}, u32[]{:S(2)}, u32[]{:S(2)}) %collective-permute-start.13) | collective-permute-done | bytes 131104 | tf_op jit(solution)/shard_map/ppermute | solution.py:507
  79.8 0.7 copy-done.4
  80.5 14.4 %shard_map.88 = f32[32,1024]{1,0:T(8,128)} custom-call(f32[4,64,128]{2,1,0:T(8,128)} %get-tuple-element.29.refs_0_, f32[4,64,128]{2,1,0:T(8,128)} %copy-done.4, f32[4,16,128]{2,1,0:T(8,128)} %get-tuple-element.30.refs_2_, f32[5,4,64,128]{3,2,1,0:T(8,128)} %get-tuple-element.26.refs_2_.refs_3_, s32[8]{0:T(128)} %refs_4_.3, f32[32,1024]{1,0:T(8,128)} %copy-done.2), custom_call_target="tpu_custom_call" | custom-call | flops 8388608 | bytes 1048576 | tf_op jit(solution)/shard_map/pallas_call | solution.py:519
  (31 shorter events, 0.1 us)
Async XLA Ops:
  2.1 7.4 %collective-permute-start = (f32[64,1024]{1,0:T(8,128)}, f32[64,1024]{1,0:T(8,128)S(1)}, u32[]{:S(2)}, u32[]{:S(2)}) collective-permute-start(f32[64,1024]{1,0:T(8,128)} %get-tuple-element.18), channel_id=1, source_target_pairs={{0,1},{1,0},{2,3},{3,2},{4,5},{5,4},{6,7},{7,6},{8,9},{9,8},{10,11... | collective-permute-start | bytes 786440 | tf_op jit(solution)/shard_map/ppermute | solution.py:463
  3.4 6.1 %collective-permute-start.1 = (f32[64,1024]{1,0:T(8,128)}, f32[64,1024]{1,0:T(8,128)S(1)}, u32[]{:S(2)}, u32[]{:S(2)}) collective-permute-start(f32[64,1024]{1,0:T(8,128)} %get-tuple-element.19), channel_id=1, source_target_pairs={{1,2},{2,1},{5,6},{6,5},{9,10},{10,9},{13,14},{14,13},{17,18},{18,... | collective-permute-start | bytes 786440 | tf_op jit(solution)/shard_map/ppermute | solution.py:463
  9.5 0.7 copy-start
  10.2 0.7 copy-start.1
  19.9 9.9 %collective-permute-start.2 = (f32[32,1024]{1,0:T(8,128)}, f32[32,1024]{1,0:T(8,128)S(1)}, u32[]{:S(2)}, u32[]{:S(2)}) collective-permute-start(f32[32,1024]{1,0:T(8,128)} %get-tuple-element.20), channel_id=1, source_target_pairs={{0,4},{1,5},{2,6},{3,7},{4,8},{5,9},{6,10},{7,11},{8,12},{9,13},{1... | collective-permute-start | bytes 393224 | tf_op jit(solution)/shard_map/ppermute | solution.py:463
  19.9 8.7 %collective-permute-start.3 = (f32[24,1024]{1,0:T(8,128)}, f32[24,1024]{1,0:T(8,128)S(1)}, u32[]{:S(2)}, u32[]{:S(2)}) collective-permute-start(f32[24,1024]{1,0:T(8,128)} %get-tuple-element.21), channel_id=1, source_target_pairs={{0,5},{1,4},{2,7},{3,6},{4,9},{5,8},{6,11},{7,10},{8,13},{9,12},{1... | collective-permute-start | bytes 294920 | tf_op jit(solution)/shard_map/ppermute | solution.py:463
  22.3 7.6 %collective-permute-start.4 = (f32[24,1024]{1,0:T(8,128)}, f32[24,1024]{1,0:T(8,128)S(1)}, u32[]{:S(2)}, u32[]{:S(2)}) collective-permute-start(f32[24,1024]{1,0:T(8,128)} %get-tuple-element.22), channel_id=1, source_target_pairs={{1,6},{2,5},{5,10},{6,9},{9,14},{10,13},{13,18},{14,17},{17,22},{1... | collective-permute-start | bytes 294920 | tf_op jit(solution)/shard_map/ppermute | solution.py:463
  22.9 18.2 %collective-permute-start.10 = (f32[24,512]{1,0:T(8,128)}, f32[24,512]{1,0:T(8,128)S(1)}, u32[]{:S(2)}, u32[]{:S(2)}) collective-permute-start(f32[24,512]{1,0:T(8,128)} %get-tuple-element.24.refs_4_), channel_id=1, source_target_pairs={{0,3},{1,2},{2,1},{3,0},{4,7},{5,6},{6,5},{7,4},{8,11},{9,10},{10,... | collective-permute-start | bytes 147464 | tf_op jit(solution)/shard_map/ppermute | solution.py:463
  25.1 18.2 %collective-permute-start.8 = (f32[24,512]{1,0:T(8,128)}, f32[24,512]{1,0:T(8,128)S(1)}, u32[]{:S(2)}, u32[]{:S(2)}) collective-permute-start(f32[24,512]{1,0:T(8,128)} %get-tuple-element.24.refs_4_), channel_id=1, source_target_pairs={{0,1},{1,0},{2,3},{3,2},{4,5},{5,4},{6,7},{7,6},{8,9},{9,8},{10,11... | collective-permute-start | bytes 147464 | tf_op jit(solution)/shard_map/ppermute | solution.py:463
  28.7 1.2 %copy-start.6 = (f32[24,1024]{1,0:T(8,128)}, f32[24,1024]{1,0:T(8,128)S(1)}, u32[]{:S(2)}) copy-start(f32[24,1024]{1,0:T(8,128)S(1)} %collective-permute-done.3.edge_a) | copy-start | bytes 294916
  28.7 14.6 %collective-permute-start.9 = (f32[24,512]{1,0:T(8,128)}, f32[24,512]{1,0:T(8,128)S(1)}, u32[]{:S(2)}, u32[]{:S(2)}) collective-permute-start(f32[24,512]{1,0:T(8,128)} %get-tuple-element.24.refs_4_), channel_id=1, source_target_pairs={{0,2},{1,3},{2,0},{3,1},{4,6},{5,7},{6,4},{7,5},{8,10},{9,11},{10,... | collective-permute-start | bytes 147464 | tf_op jit(solution)/shard_map/ppermute | solution.py:463
  29.9 0.6 copy-start.7
  29.9 0.7 copy-start.2
  39.1 4.2 %collective-permute-start.5 = (f32[16,512]{1,0:T(8,128)}, f32[16,512]{1,0:T(8,128)S(1)}, u32[]{:S(2)}, u32[]{:S(2)}) collective-permute-start(f32[16,512]{1,0:T(8,128)} %shard_map.84.refs_0_), channel_id=1, source_target_pairs={{0,1},{1,0},{2,3},{3,2},{4,5},{5,4},{6,7},{7,6},{8,9},{9,8},{10,11... | collective-permute-start | bytes 98312 | tf_op jit(solution)/shard_map/ppermute | solution.py:463
  41.2 4.0 %collective-permute-start.6 = (f32[16,512]{1,0:T(8,128)}, f32[16,512]{1,0:T(8,128)S(1)}, u32[]{:S(2)}, u32[]{:S(2)}) collective-permute-start(f32[16,512]{1,0:T(8,128)} %shard_map.84.refs_0_), channel_id=1, source_target_pairs={{0,2},{1,3},{2,0},{3,1},{4,6},{5,7},{6,4},{7,5},{8,10},{9,11},{10,... | collective-permute-start | bytes 98312 | tf_op jit(solution)/shard_map/ppermute | solution.py:463
  41.2 4.8 %copy-start.8 = (f32[24,512]{1,0:T(8,128)}, f32[24,512]{1,0:T(8,128)S(1)}, u32[]{:S(2)}) copy-start(f32[24,512]{1,0:T(8,128)S(1)} %collective-permute-done.10.refs_7_) | copy-start | bytes 147460
  41.2 4.8 %collective-permute-start.7 = (f32[16,512]{1,0:T(8,128)}, f32[16,512]{1,0:T(8,128)S(1)}, u32[]{:S(2)}, u32[]{:S(2)}) collective-permute-start(f32[16,512]{1,0:T(8,128)} %shard_map.84.refs_0_), channel_id=1, source_target_pairs={{0,3},{1,2},{2,1},{3,0},{4,7},{5,6},{6,5},{7,4},{8,11},{9,10},{10,... | collective-permute-start | bytes 98312 | tf_op jit(solution)/shard_map/ppermute | solution.py:463
  43.3 2.8 %copy-start.9 = (f32[24,512]{1,0:T(8,128)}, f32[24,512]{1,0:T(8,128)S(1)}, u32[]{:S(2)}) copy-start(f32[24,512]{1,0:T(8,128)S(1)} %collective-permute-done.8.refs_5_) | copy-start | bytes 147460
  43.3 2.8 %copy-start.10 = (f32[24,512]{1,0:T(8,128)}, f32[24,512]{1,0:T(8,128)S(1)}, u32[]{:S(2)}) copy-start(f32[24,512]{1,0:T(8,128)S(1)} %collective-permute-done.9.refs_6_) | copy-start | bytes 147460
  43.3 2.7 %copy-start.11 = (f32[16,512]{1,0:T(8,128)}, f32[16,512]{1,0:T(8,128)S(1)}, u32[]{:S(2)}) copy-start(f32[16,512]{1,0:T(8,128)S(1)} %collective-permute-done.5.refs_1_) | copy-start | bytes 98308
  45.2 0.8 copy-start.12
  46.0 0.6 copy-start.13
  48.7 4.8 %collective-permute-start.11 = (f32[4,64,128]{2,1,0:T(8,128)}, f32[4,64,128]{2,1,0:T(8,128)S(1)}, u32[]{:S(2)}, u32[]{:S(2)}) collective-permute-start(f32[4,64,128]{2,1,0:T(8,128)} %get-tuple-element.25.refs_0_), channel_id=1, source_target_pairs={{0,4},{4,0},{8,12},{12,8},{16,20},{20,16},{24,28},{28,24},{1,5},{5... | collective-permute-start | bytes 393224 | tf_op jit(solution)/shard_map/ppermute | solution.py:507
  53.5 0.7 copy-start.5
  60.2 4.9 %collective-permute-start.12 = (f32[4,64,128]{2,1,0:T(8,128)}, f32[4,64,128]{2,1,0:T(8,128)S(1)}, u32[]{:S(2)}, u32[]{:S(2)}) collective-permute-start(f32[4,64,128]{2,1,0:T(8,128)} %get-tuple-element.27.refs_0_), channel_id=1, source_target_pairs={{0,8},{4,12},{8,0},{12,4},{16,24},{20,28},{24,16},{28,20},{1,9},{5... | collective-permute-start | bytes 393224 | tf_op jit(solution)/shard_map/ppermute | solution.py:507
  65.1 0.7 copy-start.3
  75.8 4.0 %collective-permute-start.13 = (f32[4,64,128]{2,1,0:T(8,128)}, f32[4,64,128]{2,1,0:T(8,128)S(1)}, u32[]{:S(2)}, u32[]{:S(2)}) collective-permute-start(f32[4,64,128]{2,1,0:T(8,128)} %get-tuple-element.29.refs_0_), channel_id=1, source_target_pairs={{0,16},{4,20},{8,24},{12,28},{16,0},{20,4},{24,8},{28,12},{1,17},{... | collective-permute-start | bytes 393224 | tf_op jit(solution)/shard_map/ppermute | solution.py:507
  79.8 0.7 copy-start.4

commit v2 on v1

--- a/solution.py
+++ b/solution.py
@@ -121,34 +121,39 @@
             coarse[at : at + 1, cols(c)] = jnp.where(iota(1, (1, LANES)) < LANES // 2, halves[0], halves[1])
 
 
-def sweep(state, weights, force, count, tiles, strip_tiles, wave):
-    def step(t, reach):
-        now = lax.rem(t, 2)
+def sweep(state, spare, weights, force, count, tiles, strip_tiles, wave):
+    def step(source, target, t, reach):
         amount = None if wave is None else wave(t)
         for r in range(HT - reach, HT + strip_tiles + reach):
             at = PAD + r * SUB
-            here = [state[now, c, at : at + SUB, :] for c in range(tiles)]
+            here = [source[c, at : at + SUB, :] for c in range(tiles)]
             for c in range(tiles):
                 left, right = beside(here, c)
-                above = state[now, c, at - 1 : at + SUB - 1, :]
-                below = state[now, c, at + 1 : at + SUB + 1, :]
+                above = source[c, at - 1 : at + SUB - 1, :]
+                below = source[c, at + 1 : at + SUB + 1, :]
                 w = [weights[k, c, r * SUB : (r + 1) * SUB, :] for k in range(5)]
                 new = (w[0] * here[c] + w[1] * above) + (w[2] * below + w[3] * left) + w[4] * right
                 if amount is not None:
                     new = new + amount * force[c, r * SUB : (r + 1) * SUB, :]
-                state[1 - now, c, at : at + SUB, :] = new
+                target[c, at : at + SUB, :] = new
+
+    def pair(p, _, reach):
+        step(state, spare, 2 * p, reach)
+        step(spare, state, 2 * p + 1, reach)
 
     begin = 0
-    for reach in range(HT, -1, -1):
-        if reach == HT:
-            steps = jnp.maximum(count - 1 - SUB * (HT - 1), 0)
-        elif reach > 0:
-            steps = jnp.clip(count - 1 - SUB * (reach - 1), 0, SUB)
-        else:
-            steps = 1
-        lax.fori_loop(begin, begin + steps, lambda t, _, reach=reach: step(t, reach), None)
-        begin = begin + steps
-    return lax.rem(count, 2)
+    for reach in range(HT, 0, -1):
+        end = jnp.maximum(count - SUB * (reach - 1), 0) // 2
+        lax.fori_loop(begin, end, functools.partial(pair, reach=reach), None)
+        begin = end
+
+    @pl.when(lax.rem(count, 2) == 1)
+    def _():
+        step(state, spare, count - 1, 0)
+        for c in range(tiles):
+            for r in range(strip_tiles):
+                at = PAD + HALO + r * SUB
+                state[c, at : at + SUB, :] = spare[c, at : at + SUB, :]
 
 
 def with_halos(odd, got_a, got_b, place):
@@ -163,20 +168,20 @@
         place(got_a, False)
 
 
-def unpack(out, lead, tiles, rows, payload, above, which, at=0):
+def unpack(out, tiles, rows, payload, above, which, at=0):
     for c in range(tiles):
         if above:
             main, rest = at + HALO - MAIN, at + HALO - MAIN - REST
         else:
             main, rest = at + HALO + rows, at + HALO + rows + MAIN
         first = 3 * MAIN + which * REST
-        out[(*lead, c, slice(main, main + MAIN), slice(None))] = payload[which * MAIN : (which + 1) * MAIN, cols(c)]
-        out[(*lead, c, slice(rest, rest + REST), slice(None))] = payload[first : first + REST, cols(c)]
+        out[c, main : main + MAIN, :] = payload[which * MAIN : (which + 1) * MAIN, cols(c)]
+        out[c, rest : rest + REST, :] = payload[first : first + REST, cols(c)]
 
 
 def first_body(
     point, rate, source, got_a, got_b, initial, table, classes, steps, waveform,
-    relaxed, edge_a, edge_b, weights, state, force, rates, conduct,
+    relaxed, edge_a, edge_b, weights, state, spare, force, rates, conduct,
 ):
     rows, width = point.shape
     tiles, strip_tiles, blocks = width // LANES, rows // SUB, rows // BLK_R
@@ -188,7 +193,7 @@
     for c in range(tiles):
         for r in range(strip_tiles):
             at, to = slice(r * SUB, (r + 1) * SUB), slice(HALO + r * SUB, HALO + (r + 1) * SUB)
-            state[0, c, PAD + HALO + r * SUB : PAD + HALO + (r + 1) * SUB, :] = point[at, cols(c)]
+            state[c, PAD + HALO + r * SUB : PAD + HALO + (r + 1) * SUB, :] = point[at, cols(c)]
             rates[c, to, :] = rate[at, cols(c)]
             force[c, to, :] = source[at, cols(c)]
         for b in range(blocks):
@@ -200,12 +205,12 @@
         for at in (0, HALO + rows + HALO - SUB):
             rates[c, at : at + SUB, :] = zero
             force[c, at : at + SUB, :] = zero
-            state[0, c, PAD + at : PAD + at + SUB, :] = zero
+            state[c, PAD + at : PAD + at + SUB, :] = zero
 
     def place(payload, above):
-        unpack(state, (0,), tiles, rows, payload, above, 0, PAD)
-        unpack(rates, (), tiles, rows, payload, above, 1)
-        unpack(force, (), tiles, rows, payload, above, 2)
+        unpack(state, tiles, rows, payload, above, 0, PAD)
+        unpack(rates, tiles, rows, payload, above, 1)
+        unpack(force, tiles, rows, payload, above, 2)
         for b in range(HT):
             at = PAD + b * BLK_R + (0 if above else HALO + rows)
             row = 3 * MAIN + 3 * REST + b
@@ -228,7 +233,7 @@
             for k in range(4):
                 weights[k + 1, c, r * SUB : (r + 1) * SUB, :] = w[k]
 
-    now = sweep(state, weights, force, count, tiles, strip_tiles, lambda t: waveform[start + t])
+    sweep(state, spare, weights, force, count, tiles, strip_tiles, lambda t: waveform[start + t])
 
     def give(read):
         for c in range(tiles):
@@ -257,10 +262,10 @@
 
     @pl.when(jnp.logical_not(last))
     def _():
-        give(lambda r, c: state[now, c, pl.ds(PAD + HALO + r * SUB, SUB), :])
-
-
-def second_body(relaxed, edge_a, edge_b, point, got_a, got_b, weights, steps, coarse, state, tmp):
+        give(lambda r, c: state[c, PAD + HALO + r * SUB : PAD + HALO + (r + 1) * SUB, :])
+
+
+def second_body(relaxed, edge_a, edge_b, point, got_a, got_b, weights, steps, coarse, state, spare, tmp):
     rows, width = point.shape
     tiles, strip_tiles = width // LANES, rows // SUB
     mine, strip = lax.axis_index("tm"), lax.axis_index("space")
@@ -270,24 +275,24 @@
         for r in range(strip_tiles):
             at = slice(r * SUB, (r + 1) * SUB)
             to = PAD + HALO + r * SUB
-            state[0, c, to : to + SUB, :] = relaxed[at, cols(c)] - point[at, cols(c)]
+            state[c, to : to + SUB, :] = relaxed[at, cols(c)] - point[at, cols(c)]
         for at in (0, HALO + rows + HALO - SUB):
             tmp[c, at : at + SUB, :] = jnp.zeros((SUB, LANES), F32)
 
     def place(pair, above):
         edge, payload = pair
-        unpack(tmp, (), tiles, rows, payload, above, 0)
+        unpack(tmp, tiles, rows, payload, above, 0)
         base = 0 if above else HALO + rows
         for c in range(tiles):
             for r in range(HT):
                 at = base + r * SUB
-                state[0, c, PAD + at : PAD + at + SUB, :] = edge[r * SUB : (r + 1) * SUB, cols(c)] - tmp[c, at : at + SUB, :]
+                state[c, PAD + at : PAD + at + SUB, :] = edge[r * SUB : (r + 1) * SUB, cols(c)] - tmp[c, at : at + SUB, :]
 
     with_halos(odd, (edge_a, got_a), (edge_b, got_b), place)
-    now = sweep(state, weights, None, count, tiles, strip_tiles, None)
+    sweep(state, spare, weights, None, count, tiles, strip_tiles, None)
     pairs = halve()
     for c in range(tiles // 2):
-        wide = [row_pairs(state, (now, 2 * c + k), PAD + HALO, rows // 2) for k in (0, 1)]
+        wide = [row_pairs(state, (2 * c + k,), PAD + HALO, rows // 2) for k in (0, 1)]
         coarse[:, cols(c)] = 0.25 * dot(jnp.concatenate(wide, axis=1), pairs)
 
 
@@ -325,26 +330,27 @@
                 weights[k + 1, c, r * SUB : (r + 1) * SUB, :] = w[k]
 
 
-def link_steps(state, weights, factor):
-    _, tiles, padded, _ = state.shape
-
-    def step(now):
+def link(buffers, weights, factor):
+    state, one, two = buffers
+    tiles, padded, _ = state.shape
+
+    def step(source, target):
         for r in range((padded - 2 * PAD) // SUB):
             at = PAD + r * SUB
-            here = [state[now, c, at : at + SUB, :] for c in range(tiles)]
+            here = [source[c, at : at + SUB, :] for c in range(tiles)]
             for c in range(tiles):
                 left, right = beside(here, c)
-                above = state[now, c, at - 1 : at + SUB - 1, :]
-                below = state[now, c, at + 1 : at + SUB + 1, :]
+                above = source[c, at - 1 : at + SUB - 1, :]
+                below = source[c, at + 1 : at + SUB + 1, :]
                 w = [weights[k, c, r * SUB : (r + 1) * SUB, :] for k in range(5)]
                 change = (w[1] * above + w[2] * below) + (w[3] * left + w[4] * right) - w[0] * here[c]
-                state[1 - now, c, at : at + SUB, :] = here[c] + factor * change
-
-    def one(i, now):
-        step(now)
-        return 1 - now
-
-    return one
+                target[c, at : at + SUB, :] = here[c] + factor * change
+
+    source = state
+    for k in range(CSUB):
+        target = state if k == CSUB - 1 else (two if source is one else one)
+        step(source, target)
+        source = target
 
 
 def scan_body(stage, final, refs):
@@ -355,22 +361,23 @@
     upper = lax.rem(mine // size, 2) == 1
     first = (mine // (2 * size)) * (2 * size) + size
     if final:
-        relaxed, out, state, errors, tmp = refs[5:]
+        relaxed, out, *buffers, errors, tmp = refs[5:]
         rows = 2 * relaxed.shape[0] // 4
     else:
-        total_out, errors, state = refs[5:]
+        total_out, errors, *buffers = refs[5:]
         rows = errors.shape[1]
     mine_rows = pl.multiple_of(strip * rows, SUB)
     zero = jnp.zeros((SUB, LANES), F32)
+    state = buffers[0]
     for c in range(tiles):
-        for b in (0, 1):
-            state[b, c, 0:PAD, :] = zero
-            state[b, c, PAD + height :, :] = zero
+        for buffer in buffers:
+            buffer[c, 0:PAD, :] = zero
+            buffer[c, PAD + height :, :] = zero
 
     def load(ref):
         for c in range(tiles):
             for r in range(height // SUB):
-                state[0, c, PAD + r * SUB : PAD + (r + 1) * SUB, :] = ref[c, r * SUB : (r + 1) * SUB, :]
+                state[c, PAD + r * SUB : PAD + (r + 1) * SUB, :] = ref[c, r * SUB : (r + 1) * SUB, :]
 
     @pl.when(upper)
     def _():
@@ -380,9 +387,9 @@
     def _():
         load(total)
 
-    def keep(now):
-        for c in range(tiles):
-            piece = state[now, c, pl.ds(PAD + mine_rows, rows), :]
+    def keep():
+        for c in range(tiles):
+            piece = state[c, pl.ds(PAD + mine_rows, rows), :]
             errors[c, :, :] = piece if before is None else before[c, :, :] + piece
 
     def pass_on():
@@ -394,21 +401,20 @@
 
     pass_on()
 
-    def turn(i, now):
+    def turn(i, _):
         @pl.when(jnp.logical_and(upper, first + i == mine))
         def _():
-            keep(now)
-
-        factor = steps[first + i].astype(F32) * (1.0 / (4.0 * CSUB))
-        return lax.fori_loop(0, CSUB, link_steps(state, weights, factor), now)
+            keep()
+
+        link(buffers, weights, steps[first + i].astype(F32) * (1.0 / (4.0 * CSUB)))
 
     if final:
         turns = jnp.where(upper, mine - first, 0)
-        now = lax.fori_loop(0, turns, turn, jnp.int32(0))
+        lax.fori_loop(0, turns, turn, None)
 
         @pl.when(upper)
         def _():
-            keep(now)
+            keep()
 
         pairs = double()
         for c in range(tiles):
@@ -420,13 +426,13 @@
         for c in range(2 * tiles):
             out[:, cols(c)] = relaxed[:, cols(c)] + tmp[c, :, :]
     else:
-        now = lax.fori_loop(0, size, turn, jnp.int32(0))
+        lax.fori_loop(0, size, turn, None)
 
         def close(ref):
             for c in range(tiles):
                 for r in range(height // SUB):
                     at = slice(r * SUB, (r + 1) * SUB)
-                    total_out[c, at, :] = ref[c, at, :] + state[now, c, pl.ds(PAD + r * SUB, SUB), :]
+                    total_out[c, at, :] = ref[c, at, :] + state[c, PAD + r * SUB : PAD + (r + 1) * SUB, :]
 
         @pl.when(upper)
         def _():
@@ -475,7 +481,8 @@
         first_body, [VM] * 6 + [SM] * 4,
         (f32(rows, width), f32(HALO, width), f32(HALO, width), f32(5, tiles, height, LANES)),
         [
-            pltpu.VMEM((2, tiles, height + 2 * PAD, LANES), F32),
+            pltpu.VMEM((tiles, height + 2 * PAD, LANES), F32),
+            pltpu.VMEM((tiles, height + 2 * PAD, LANES), F32),
             pltpu.VMEM((tiles, height, LANES), F32),
             pltpu.VMEM((tiles, height, LANES), F32),
             pltpu.VMEM((tiles, height + 2 * PAD, LANES), F32),
@@ -488,7 +495,7 @@
 
     change = call(
         second_body, [VM] * 7 + [SM], f32(crows, width // 2),
-        [pltpu.VMEM((2, tiles, height + 2 * PAD, LANES), F32), pltpu.VMEM((tiles, height, LANES), F32)],
+        [pltpu.VMEM((tiles, height + 2 * PAD, LANES), F32)] * 2 + [pltpu.VMEM((tiles, height, LANES), F32)],
         1 << 24,
     )(relaxed, edge_a, edge_b, point, got_a, got_b, weights, interval_steps)
     changes = [change] + [exchange(change, 0, lambda s, k=k: s ^ k) for k in range(1, strips)]
@@ -512,17 +519,17 @@
             refs = refs if some else (*refs[:2], None, *refs[2:])
             scan_body(stage, final, refs)
 
-        state = pltpu.VMEM((2, ctiles, cheight + 2 * PAD, LANES), F32)
+        buffers = [pltpu.VMEM((ctiles, cheight + 2 * PAD, LANES), F32)] * 3
         lead = [total, got] + ([errors] if some else []) + [coarse_weights, interval_steps]
         specs = [VM] * (len(lead) - 1) + [SM]
         if final:
             out = call(
                 body, specs + [VM], f32(rows, width),
-                [state, pltpu.VMEM((ctiles, crows, LANES), F32), pltpu.VMEM((tiles, rows, LANES), F32)], 1 << 23,
+                buffers + [pltpu.VMEM((ctiles, crows, LANES), F32), pltpu.VMEM((tiles, rows, LANES), F32)], 1 << 23,
             )(*lead, relaxed)
         else:
             total, errors = call(
-                body, specs, (f32(ctiles, cheight, LANES), f32(ctiles, crows, LANES)), [state], 1 << 23
+                body, specs, (f32(ctiles, cheight, LANES), f32(ctiles, crows, LANES)), buffers, 1 << 23
             )(*lead)
     return out[None]
 

time: 95.2 us -> 71.7 us (0.75)
  the two profiles are of different devices: /device:TPU:7 before, /device:TPU:0 now
where the time goes in v2:
time: 71.7 us; the launch traced here: 71.3 us
  starting transfers between devices  24.7 us (34%)
  Pallas kernels  21.9 us (31%)
  waiting for transfers between devices  19.9 us (28%)
  local copies, waits for them, and re-layouts  4.68 us (7%)
    ppermute x11, starting transfers between devices, exchange(): return lax.ppermute(value, both, pairs)  21.6 us
    ppermute x11, waiting for transfers between devices, exchange(): return lax.ppermute(value, both, pairs)  10.4 us
    ppermute x3, waiting for transfers between devices, shards(): lax.ppermute(total, 'tm', [(j, j ^ 1 << stage) for j in range(intervals)])  9.5 us
    pallas_call x1, Pallas kernels, shards(): call(first_body, [VM] * 6 + [SM] * 4, (f32(rows, width), f32(HALO, width)...  5.31 us
    pallas_call x2, Pallas kernels, shards(): call(body, specs, (f32(ctiles, cheight, LANES), f32(ctiles, crows, LANES)...  5.29 us
    pallas_call x1, Pallas kernels, shards(): call(second_body, [VM] * 7 + [SM], f32(crows, width // 2), [pltpu.VMEM((t...  4.95 us
    unnamed x28, local copies, waits for them, and re-layouts  4.68 us
    ppermute x3, starting transfers between devices, shards(): lax.ppermute(total, 'tm', [(j, j ^ 1 << stage) for j in range(intervals)])  3.15 us
  transfers between devices with their start and end apart: 14, of which 6 were waited for; matrix products, arithmetic and copies ran while one was open for 0% of the time, Pallas kernels for 7%

profile of v2, /device:TPU:0, one launch (start us, length us, event | category | flops | bytes accessed | tf_op | source)
XLA Modules:
  0.0 71.3 jit_solution(12124914937206449943)
XLA Ops:
  0.0 2.1 %shard_map.82 = (f32[64,1024]{1,0:T(8,128)}, f32[64,1024]{1,0:T(8,128)}, f32[24,512]{1,0:T(8,128)}) custom-call(f32[32,1024]{1,0:T(8,128)} %bitcast.2, f32[32,1024]{1,0:T(8,128)} %rate.3, f32[32,1024]{1,0:T(8,128)} %source.3, f32[16]{0:T(128)} %table.3, s32[4,8]{1,0:T(4,128)} %classes.3), custom_call_target="tpu_custom_call" | custom-call | flops 1048576 | bytes 1048576 | tf_op jit(solution)/shard_map/pallas_call | solution.py:471
  2.1 3.1 %collective-permute-start = (f32[64,1024]{1,0:T(8,128)}, f32[64,1024]{1,0:T(8,128)S(1)}, u32[]{:S(2)}, u32[]{:S(2)}) collective-permute-start(f32[64,1024]{1,0:T(8,128)} %get-tuple-element.18), channel_id=1, source_target_pairs={{0,1},{1,0},{2,3},{3,2},{4,5},{5,4},{6,7},{7,6},{8,9},{9,8},{10,11... | collective-permute-start | bytes 786440 | tf_op jit(solution)/shard_map/ppermute | solution.py:469
  5.1 0.7 collective-permute-start.1
  5.8 5.8 %collective-permute-done.got_a = f32[64,1024]{1,0:T(8,128)S(1)} collective-permute-done((f32[64,1024]{1,0:T(8,128)}, f32[64,1024]{1,0:T(8,128)S(1)}, u32[]{:S(2)}, u32[]{:S(2)}) %collective-permute-start) | collective-permute-done | bytes 262176 | tf_op jit(solution)/shard_map/ppermute | solution.py:469
  11.7 0.7 copy-done
  12.4 0.7 copy-done.1
  13.1 5.3 %shard_map.83 = (f32[32,1024]{1,0:T(8,128)}, f32[24,1024]{1,0:T(8,128)}, f32[24,1024]{1,0:T(8,128)}, f32[5,8,80,128]{3,2,1,0:T(8,128)}) custom-call(f32[32,1024]{1,0:T(8,128)} %bitcast.3, f32[32,1024]{1,0:T(8,128)} %rate.3, f32[32,1024]{1,0:T(8,128)} %source.3, f32[64,1024]{1,0:T(8,128)} %copy-done, f32[64,1024]{1,0:T(8,128)} %copy-done.1, ...), custom_call_target="tpu_custom_call" | custom-call | flops 16777216 | bytes 1048576 | tf_op jit(solution)/shard_map/pallas_call | solution.py:480
  18.8 5.6 %collective-permute-start.3 = (f32[24,1024]{1,0:T(8,128)}, f32[24,1024]{1,0:T(8,128)S(1)}, u32[]{:S(2)}, u32[]{:S(2)}) collective-permute-start(f32[24,1024]{1,0:T(8,128)} %get-tuple-element.21), channel_id=1, source_target_pairs={{0,5},{1,4},{2,7},{3,6},{4,9},{5,8},{6,11},{7,10},{8,13},{9,12},{1... | collective-permute-start | bytes 294920 | tf_op jit(solution)/shard_map/ppermute | solution.py:469
  24.4 0.7 collective-permute-start.4
  25.1 2.7 %collective-permute-start.10 = (f32[24,512]{1,0:T(8,128)}, f32[24,512]{1,0:T(8,128)S(1)}, u32[]{:S(2)}, u32[]{:S(2)}) collective-permute-start(f32[24,512]{1,0:T(8,128)} %get-tuple-element.24.refs_4_), channel_id=1, source_target_pairs={{0,3},{1,2},{2,1},{3,0},{4,7},{5,6},{6,5},{7,4},{8,11},{9,10},{10,... | collective-permute-start | bytes 147464 | tf_op jit(solution)/shard_map/ppermute | solution.py:469
  27.8 0.6 collective-permute-start.8
  28.4 1.5 %collective-permute-start.9 = (f32[24,512]{1,0:T(8,128)}, f32[24,512]{1,0:T(8,128)S(1)}, u32[]{:S(2)}, u32[]{:S(2)}) collective-permute-start(f32[24,512]{1,0:T(8,128)} %get-tuple-element.24.refs_4_), channel_id=1, source_target_pairs={{0,2},{1,3},{2,0},{3,1},{4,6},{5,7},{6,4},{7,5},{8,10},{9,11},{10,... | collective-permute-start | bytes 147464 | tf_op jit(solution)/shard_map/ppermute | solution.py:469
  30.0 0.6 copy-done.7
  30.7 5.0 %shard_map.84.refs_0_ = f32[16,512]{1,0:T(8,128)} custom-call(f32[32,1024]{1,0:T(8,128)} %copy-done.2, f32[24,1024]{1,0:T(8,128)} %copy-done.6, f32[24,1024]{1,0:T(8,128)} %copy-done.7, f32[32,1024]{1,0:T(8,128)} %bitcast.4, f32[64,1024]{1,0:T(8,128)} %copy-done, f32[64,1024]{1,0:T(8,128)} %copy-done.1, f32[5,8,80,128]{3,2,1,0:T(8,128)} %get-tuple-element.23.weights, ...), custom_call_target="tpu_custom_call" | custom-call | flops 16777216 | bytes 1048576 | tf_op jit(solution)/shard_map/pallas_call | solution.py:496
  35.6 2.6 %collective-permute-start.5 = (f32[16,512]{1,0:T(8,128)}, f32[16,512]{1,0:T(8,128)S(1)}, u32[]{:S(2)}, u32[]{:S(2)}) collective-permute-start(f32[16,512]{1,0:T(8,128)} %shard_map.84.refs_0_), channel_id=1, source_target_pairs={{0,1},{1,0},{2,3},{3,2},{4,5},{5,4},{6,7},{7,6},{8,9},{9,8},{10,11... | collective-permute-start | bytes 98312 | tf_op jit(solution)/shard_map/ppermute | solution.py:469
  38.2 2.1 %collective-permute-start.6 = (f32[16,512]{1,0:T(8,128)}, f32[16,512]{1,0:T(8,128)S(1)}, u32[]{:S(2)}, u32[]{:S(2)}) collective-permute-start(f32[16,512]{1,0:T(8,128)} %shard_map.84.refs_0_), channel_id=1, source_target_pairs={{0,2},{1,3},{2,0},{3,1},{4,6},{5,7},{6,4},{7,5},{8,10},{9,11},{10,... | collective-permute-start | bytes 98312 | tf_op jit(solution)/shard_map/ppermute | solution.py:469
  40.4 1.5 %collective-permute-start.7 = (f32[16,512]{1,0:T(8,128)}, f32[16,512]{1,0:T(8,128)S(1)}, u32[]{:S(2)}, u32[]{:S(2)}) collective-permute-start(f32[16,512]{1,0:T(8,128)} %shard_map.84.refs_0_), channel_id=1, source_target_pairs={{0,3},{1,2},{2,1},{3,0},{4,7},{5,6},{6,5},{7,4},{8,11},{9,10},{10,... | collective-permute-start | bytes 98312 | tf_op jit(solution)/shard_map/ppermute | solution.py:469
  41.9 1.3 %collective-permute-done.6.refs_2_ = f32[16,512]{1,0:T(8,128)S(1)} collective-permute-done((f32[16,512]{1,0:T(8,128)}, f32[16,512]{1,0:T(8,128)S(1)}, u32[]{:S(2)}, u32[]{:S(2)}) %collective-permute-start.6) | collective-permute-done | bytes 32800 | tf_op jit(solution)/shard_map/ppermute | solution.py:469
  43.3 3.2 %collective-permute-done.7.refs_3_ = f32[16,512]{1,0:T(8,128)S(1)} collective-permute-done((f32[16,512]{1,0:T(8,128)}, f32[16,512]{1,0:T(8,128)S(1)}, u32[]{:S(2)}, u32[]{:S(2)}) %collective-permute-start.7) | collective-permute-done | bytes 32800 | tf_op jit(solution)/shard_map/ppermute | solution.py:469
  46.5 0.6 copy-done.13
  47.1 2.0 %shard_map.85 = (f32[4,64,128]{2,1,0:T(8,128)}, f32[5,4,64,128]{3,2,1,0:T(8,128)}) custom-call(f32[16,512]{1,0:T(8,128)} %shard_map.84.refs_0_, f32[16,512]{1,0:T(8,128)} %copy-done.11, f32[16,512]{1,0:T(8,128)} %copy-done.12, f32[16,512]{1,0:T(8,128)} %copy-done.13, f32[24,512]{1,0:T(8,128)} %get-tuple-element.24.refs_4_, f32[24,512]{1,0:T(8,128)} %copy-done.9, ...), custom_call_target="tpu_custom_call" | custom-call | flops 1048576 | bytes 1048576 | tf_op jit(solution)/shard_map/pallas_call | solution.py:506
  49.1 1.6 %collective-permute-done.11.refs_1_ = f32[4,64,128]{2,1,0:T(8,128)S(1)} collective-permute-done((f32[4,64,128]{2,1,0:T(8,128)}, f32[4,64,128]{2,1,0:T(8,128)S(1)}, u32[]{:S(2)}, u32[]{:S(2)}) %collective-permute-start.11) | collective-permute-done | bytes 131104 | tf_op jit(solution)/shard_map/ppermute | solution.py:514
  50.7 0.7 copy-done.5
  51.3 2.4 %shard_map.86 = (f32[4,64,128]{2,1,0:T(8,128)}, f32[4,16,128]{2,1,0:T(8,128)}) custom-call(f32[4,64,128]{2,1,0:T(8,128)} %get-tuple-element.25.refs_0_, f32[4,64,128]{2,1,0:T(8,128)} %copy-done.5, f32[5,4,64,128]{3,2,1,0:T(8,128)} %get-tuple-element.26.refs_2_.refs_3_, s32[8]{0:T(128)} %refs_4_.3), custom_call_target="tpu_custom_call" | custom-call | flops 8388608 | bytes 1048576 | tf_op jit(solution)/shard_map/pallas_call | solution.py:531
  53.7 1.9 %collective-permute-start.12 = (f32[4,64,128]{2,1,0:T(8,128)}, f32[4,64,128]{2,1,0:T(8,128)S(1)}, u32[]{:S(2)}, u32[]{:S(2)}) collective-permute-start(f32[4,64,128]{2,1,0:T(8,128)} %get-tuple-element.27.refs_0_), channel_id=1, source_target_pairs={{0,8},{4,12},{8,0},{12,4},{16,24},{20,28},{24,16},{28,20},{1,9},{5... | collective-permute-start | bytes 393224 | tf_op jit(solution)/shard_map/ppermute | solution.py:514
  55.6 4.0 %collective-permute-done.12.refs_1_ = f32[4,64,128]{2,1,0:T(8,128)S(1)} collective-permute-done((f32[4,64,128]{2,1,0:T(8,128)}, f32[4,64,128]{2,1,0:T(8,128)S(1)}, u32[]{:S(2)}, u32[]{:S(2)}) %collective-permute-start.12) | collective-permute-done | bytes 131104 | tf_op jit(solution)/shard_map/ppermute | solution.py:514
  59.7 0.7 copy-done.3
  60.3 2.9 %shard_map.87 = (f32[4,64,128]{2,1,0:T(8,128)}, f32[4,16,128]{2,1,0:T(8,128)}) custom-call(f32[4,64,128]{2,1,0:T(8,128)} %get-tuple-element.27.refs_0_, f32[4,64,128]{2,1,0:T(8,128)} %copy-done.3, f32[4,16,128]{2,1,0:T(8,128)} %get-tuple-element.28.refs_2_, f32[5,4,64,128]{3,2,1,0:T(8,128)} %get-tuple-element.26.refs_2_.refs_3_, s32[8]{0:T(128)} %refs_4_.3), custom_call_target="tpu_custom_call" | custom-call | flops 8388608 | bytes 1048576 | tf_op jit(solution)/shard_map/pallas_call | solution.py:531
  63.2 1.2 %collective-permute-start.13 = (f32[4,64,128]{2,1,0:T(8,128)}, f32[4,64,128]{2,1,0:T(8,128)S(1)}, u32[]{:S(2)}, u32[]{:S(2)}) collective-permute-start(f32[4,64,128]{2,1,0:T(8,128)} %get-tuple-element.29.refs_0_), channel_id=1, source_target_pairs={{0,16},{4,20},{8,24},{12,28},{16,0},{20,4},{24,8},{28,12},{1,17},{... | collective-permute-start | bytes 393224 | tf_op jit(solution)/shard_map/ppermute | solution.py:514
  64.4 3.9 %collective-permute-done.13.refs_1_ = f32[4,64,128]{2,1,0:T(8,128)S(1)} collective-permute-done((f32[4,64,128]{2,1,0:T(8,128)}, f32[4,64,128]{2,1,0:T(8,128)S(1)}, u32[]{:S(2)}, u32[]{:S(2)}) %collective-permute-start.13) | collective-permute-done | bytes 131104 | tf_op jit(solution)/shard_map/ppermute | solution.py:514
  68.4 0.7 copy-done.4
  69.0 2.3 %shard_map.88 = f32[32,1024]{1,0:T(8,128)} custom-call(f32[4,64,128]{2,1,0:T(8,128)} %get-tuple-element.29.refs_0_, f32[4,64,128]{2,1,0:T(8,128)} %copy-done.4, f32[4,16,128]{2,1,0:T(8,128)} %get-tuple-element.30.refs_2_, f32[5,4,64,128]{3,2,1,0:T(8,128)} %get-tuple-element.26.refs_2_.refs_3_, s32[8]{0:T(128)} %refs_4_.3, f32[32,1024]{1,0:T(8,128)} %copy-done.2), custom_call_target="tpu_custom_call" | custom-call | flops 8388608 | bytes 1048576 | tf_op jit(solution)/shard_map/pallas_call | solution.py:526
  (31 shorter events, 0.6 us)
Async XLA Ops:
  2.1 9.6 %collective-permute-start = (f32[64,1024]{1,0:T(8,128)}, f32[64,1024]{1,0:T(8,128)S(1)}, u32[]{:S(2)}, u32[]{:S(2)}) collective-permute-start(f32[64,1024]{1,0:T(8,128)} %get-tuple-element.18), channel_id=1, source_target_pairs={{0,1},{1,0},{2,3},{3,2},{4,5},{5,4},{6,7},{7,6},{8,9},{9,8},{10,11... | collective-permute-start | bytes 786440 | tf_op jit(solution)/shard_map/ppermute | solution.py:469
  5.1 6.5 %collective-permute-start.1 = (f32[64,1024]{1,0:T(8,128)}, f32[64,1024]{1,0:T(8,128)S(1)}, u32[]{:S(2)}, u32[]{:S(2)}) collective-permute-start(f32[64,1024]{1,0:T(8,128)} %get-tuple-element.19), channel_id=1, source_target_pairs={{1,2},{2,1},{5,6},{6,5},{9,10},{10,9},{13,14},{14,13},{17,18},{18,... | collective-permute-start | bytes 786440 | tf_op jit(solution)/shard_map/ppermute | solution.py:469
  11.7 0.7 copy-start
  12.4 0.7 copy-start.1
  18.4 11.6 %collective-permute-start.2 = (f32[32,1024]{1,0:T(8,128)}, f32[32,1024]{1,0:T(8,128)S(1)}, u32[]{:S(2)}, u32[]{:S(2)}) collective-permute-start(f32[32,1024]{1,0:T(8,128)} %get-tuple-element.20), channel_id=1, source_target_pairs={{0,4},{1,5},{2,6},{3,7},{4,8},{5,9},{6,10},{7,11},{8,12},{9,13},{1... | collective-permute-start | bytes 393224 | tf_op jit(solution)/shard_map/ppermute | solution.py:469
  18.8 9.6 %collective-permute-start.3 = (f32[24,1024]{1,0:T(8,128)}, f32[24,1024]{1,0:T(8,128)S(1)}, u32[]{:S(2)}, u32[]{:S(2)}) collective-permute-start(f32[24,1024]{1,0:T(8,128)} %get-tuple-element.21), channel_id=1, source_target_pairs={{0,5},{1,4},{2,7},{3,6},{4,9},{5,8},{6,11},{7,10},{8,13},{9,12},{1... | collective-permute-start | bytes 294920 | tf_op jit(solution)/shard_map/ppermute | solution.py:469
  24.4 5.6 %collective-permute-start.4 = (f32[24,1024]{1,0:T(8,128)}, f32[24,1024]{1,0:T(8,128)S(1)}, u32[]{:S(2)}, u32[]{:S(2)}) collective-permute-start(f32[24,1024]{1,0:T(8,128)} %get-tuple-element.22), channel_id=1, source_target_pairs={{1,6},{2,5},{5,10},{6,9},{9,14},{10,13},{13,18},{14,17},{17,22},{1... | collective-permute-start | bytes 294920 | tf_op jit(solution)/shard_map/ppermute | solution.py:469
  25.1 15.3 %collective-permute-start.10 = (f32[24,512]{1,0:T(8,128)}, f32[24,512]{1,0:T(8,128)S(1)}, u32[]{:S(2)}, u32[]{:S(2)}) collective-permute-start(f32[24,512]{1,0:T(8,128)} %get-tuple-element.24.refs_4_), channel_id=1, source_target_pairs={{0,3},{1,2},{2,1},{3,0},{4,7},{5,6},{6,5},{7,4},{8,11},{9,10},{10,... | collective-permute-start | bytes 147464 | tf_op jit(solution)/shard_map/ppermute | solution.py:469
  27.8 14.1 %collective-permute-start.8 = (f32[24,512]{1,0:T(8,128)}, f32[24,512]{1,0:T(8,128)S(1)}, u32[]{:S(2)}, u32[]{:S(2)}) collective-permute-start(f32[24,512]{1,0:T(8,128)} %get-tuple-element.24.refs_4_), channel_id=1, source_target_pairs={{0,1},{1,0},{2,3},{3,2},{4,5},{5,4},{6,7},{7,6},{8,9},{9,8},{10,11... | collective-permute-start | bytes 147464 | tf_op jit(solution)/shard_map/ppermute | solution.py:469
  28.4 1.6 %copy-start.6 = (f32[24,1024]{1,0:T(8,128)}, f32[24,1024]{1,0:T(8,128)S(1)}, u32[]{:S(2)}) copy-start(f32[24,1024]{1,0:T(8,128)S(1)} %collective-permute-done.3.edge_a) | copy-start | bytes 294916
  28.4 13.5 %collective-permute-start.9 = (f32[24,512]{1,0:T(8,128)}, f32[24,512]{1,0:T(8,128)S(1)}, u32[]{:S(2)}, u32[]{:S(2)}) collective-permute-start(f32[24,512]{1,0:T(8,128)} %get-tuple-element.24.refs_4_), channel_id=1, source_target_pairs={{0,2},{1,3},{2,0},{3,1},{4,6},{5,7},{6,4},{7,5},{8,10},{9,11},{10,... | collective-permute-start | bytes 147464 | tf_op jit(solution)/shard_map/ppermute | solution.py:469
  30.0 0.6 copy-start.7
  30.0 0.7 copy-start.2
  35.6 6.3 %collective-permute-start.5 = (f32[16,512]{1,0:T(8,128)}, f32[16,512]{1,0:T(8,128)S(1)}, u32[]{:S(2)}, u32[]{:S(2)}) collective-permute-start(f32[16,512]{1,0:T(8,128)} %shard_map.84.refs_0_), channel_id=1, source_target_pairs={{0,1},{1,0},{2,3},{3,2},{4,5},{5,4},{6,7},{7,6},{8,9},{9,8},{10,11... | collective-permute-start | bytes 98312 | tf_op jit(solution)/shard_map/ppermute | solution.py:469
  38.2 5.0 %collective-permute-start.6 = (f32[16,512]{1,0:T(8,128)}, f32[16,512]{1,0:T(8,128)S(1)}, u32[]{:S(2)}, u32[]{:S(2)}) collective-permute-start(f32[16,512]{1,0:T(8,128)} %shard_map.84.refs_0_), channel_id=1, source_target_pairs={{0,2},{1,3},{2,0},{3,1},{4,6},{5,7},{6,4},{7,5},{8,10},{9,11},{10,... | collective-permute-start | bytes 98312 | tf_op jit(solution)/shard_map/ppermute | solution.py:469
  40.4 6.1 %copy-start.8 = (f32[24,512]{1,0:T(8,128)}, f32[24,512]{1,0:T(8,128)S(1)}, u32[]{:S(2)}) copy-start(f32[24,512]{1,0:T(8,128)S(1)} %collective-permute-done.10.refs_7_) | copy-start | bytes 147460
  40.4 6.1 %collective-permute-start.7 = (f32[16,512]{1,0:T(8,128)}, f32[16,512]{1,0:T(8,128)S(1)}, u32[]{:S(2)}, u32[]{:S(2)}) collective-permute-start(f32[16,512]{1,0:T(8,128)} %shard_map.84.refs_0_), channel_id=1, source_target_pairs={{0,3},{1,2},{2,1},{3,0},{4,7},{5,6},{6,5},{7,4},{8,11},{9,10},{10,... | collective-permute-start | bytes 98312 | tf_op jit(solution)/shard_map/ppermute | solution.py:469
  41.9 4.5 %copy-start.9 = (f32[24,512]{1,0:T(8,128)}, f32[24,512]{1,0:T(8,128)S(1)}, u32[]{:S(2)}) copy-start(f32[24,512]{1,0:T(8,128)S(1)} %collective-permute-done.8.refs_5_) | copy-start | bytes 147460
  41.9 4.5 %copy-start.10 = (f32[24,512]{1,0:T(8,128)}, f32[24,512]{1,0:T(8,128)S(1)}, u32[]{:S(2)}) copy-start(f32[24,512]{1,0:T(8,128)S(1)} %collective-permute-done.9.refs_6_) | copy-start | bytes 147460
  41.9 4.5 %copy-start.11 = (f32[16,512]{1,0:T(8,128)}, f32[16,512]{1,0:T(8,128)S(1)}, u32[]{:S(2)}) copy-start(f32[16,512]{1,0:T(8,128)S(1)} %collective-permute-done.5.refs_1_) | copy-start | bytes 98308
  43.3 3.2 %copy-start.12 = (f32[16,512]{1,0:T(8,128)}, f32[16,512]{1,0:T(8,128)S(1)}, u32[]{:S(2)}) copy-start(f32[16,512]{1,0:T(8,128)S(1)} %collective-permute-done.6.refs_2_) | copy-start | bytes 98308
  46.5 0.6 copy-start.13
  49.1 1.6 %collective-permute-start.11 = (f32[4,64,128]{2,1,0:T(8,128)}, f32[4,64,128]{2,1,0:T(8,128)S(1)}, u32[]{:S(2)}, u32[]{:S(2)}) collective-permute-start(f32[4,64,128]{2,1,0:T(8,128)} %get-tuple-element.25.refs_0_), channel_id=1, source_target_pairs={{0,4},{4,0},{8,12},{12,8},{16,20},{20,16},{24,28},{28,24},{1,5},{5... | collective-permute-start | bytes 393224 | tf_op jit(solution)/shard_map/ppermute | solution.py:514
  50.7 0.7 copy-start.5
  53.7 5.9 %collective-permute-start.12 = (f32[4,64,128]{2,1,0:T(8,128)}, f32[4,64,128]{2,1,0:T(8,128)S(1)}, u32[]{:S(2)}, u32[]{:S(2)}) collective-permute-start(f32[4,64,128]{2,1,0:T(8,128)} %get-tuple-element.27.refs_0_), channel_id=1, source_target_pairs={{0,8},{4,12},{8,0},{12,4},{16,24},{20,28},{24,16},{28,20},{1,9},{5... | collective-permute-start | bytes 393224 | tf_op jit(solution)/shard_map/ppermute | solution.py:514
  59.7 0.7 copy-start.3
  63.2 5.2 %collective-permute-start.13 = (f32[4,64,128]{2,1,0:T(8,128)}, f32[4,64,128]{2,1,0:T(8,128)S(1)}, u32[]{:S(2)}, u32[]{:S(2)}) collective-permute-start(f32[4,64,128]{2,1,0:T(8,128)} %get-tuple-element.29.refs_0_), channel_id=1, source_target_pairs={{0,16},{4,20},{8,24},{12,28},{16,0},{20,4},{24,8},{28,12},{1,17},{... | collective-permute-start | bytes 393224 | tf_op jit(solution)/shard_map/ppermute | solution.py:514
  68.4 0.7 copy-start.4

commit v3 on v2

--- a/solution.py
+++ b/solution.py
@@ -21,6 +21,7 @@
 VM = pl.BlockSpec(memory_space=pltpu.VMEM)
 SM = pl.BlockSpec(memory_space=pltpu.SMEM)
 F32 = jnp.float32
+GRANT = 16 << 20
 
 
 def f32(*shape):
@@ -34,6 +35,7 @@
         in_specs=ins,
         out_specs=jax.tree.map(lambda _: VM, outs),
         scratch_shapes=scratch,
+        compiler_params=pltpu.CompilerParams(vmem_limit_bytes=GRANT),
         cost_estimate=pl.CostEstimate(flops=flops, bytes_accessed=1 << 20, transcendentals=0),
     )
 

time: 71.7 us -> 65.7 us (0.916)
  Pallas kernels: 21.9 us -> 15.7 us
  starting transfers between devices: 24.7 us -> 22.3 us
  local copies, waits for them, and re-layouts: 4.68 us -> 6.92 us
    pallas_call x2, Pallas kernels: 5.29 us -> 2.76 us  [shards(): call(body, specs, (f32(ctiles, cheight, LANES), f32(ctiles, crows, LANES)...]
    unnamed x28 -> x20, local copies, waits for them, and re-layouts: 4.68 us -> 6.92 us
    pallas_call x1, Pallas kernels: 2.01 us -> 0.23 us  [shards(): call(assemble, [VM] * (2 * strips), (f32(ctiles, cheight, LANES), f32(5,...]
    ppermute x3, starting transfers between devices: 3.15 us -> 1.67 us  [shards(): lax.ppermute(total, 'tm', [(j, j ^ 1 << stage) for j in range(intervals)])]
    pallas_call x1, Pallas kernels: 2.09 us -> 0.99 us  [shards(): call(pack_body, [VM, VM, VM, SM, SM], (f32(packed, width), f32(packed, wi...]
    ppermute x3, waiting for transfers between devices: 9.5 us -> 10.5 us  [shards(): lax.ppermute(total, 'tm', [(j, j ^ 1 << stage) for j in range(intervals)])]
    ppermute x11, starting transfers between devices: 21.6 us -> 20.6 us  [exchange(): return lax.ppermute(value, both, pairs)]
    ppermute x11, waiting for transfers between devices: 10.4 us -> 9.43 us  [exchange(): return lax.ppermute(value, both, pairs)]
  transfers between devices with their start and end apart: 14 -> 14, of which waited for: 6 -> 6; matrix products, arithmetic and copies ran while one was open for 0% -> 0% of each run, Pallas kernels for 7% -> 8%
where the time goes in v3:
time: 65.7 us; the launch traced here: 64.9 us
  starting transfers between devices  22.3 us (34%)
  waiting for transfers between devices  19.9 us (30%)
  Pallas kernels  15.7 us (24%)
  local copies, waits for them, and re-layouts  6.92 us (11%)
    ppermute x11, starting transfers between devices, exchange(): return lax.ppermute(value, both, pairs)  20.6 us
    ppermute x3, waiting for transfers between devices, shards(): lax.ppermute(total, 'tm', [(j, j ^ 1 << stage) for j in range(intervals)])  10.5 us
    ppermute x11, waiting for transfers between devices, exchange(): return lax.ppermute(value, both, pairs)  9.43 us
    unnamed x20, local copies, waits for them, and re-layouts  6.92 us
    pallas_call x1, Pallas kernels, shards(): call(first_body, [VM] * 6 + [SM] * 4, (f32(rows, width), f32(HALO, width)...  5.27 us
    pallas_call x1, Pallas kernels, shards(): call(second_body, [VM] * 7 + [SM], f32(crows, width // 2), [pltpu.VMEM((t...  4.89 us
    pallas_call x2, Pallas kernels, shards(): call(body, specs, (f32(ctiles, cheight, LANES), f32(ctiles, crows, LANES)...  2.76 us
    ppermute x3, starting transfers between devices, shards(): lax.ppermute(total, 'tm', [(j, j ^ 1 << stage) for j in range(intervals)])  1.67 us
  transfers between devices with their start and end apart: 14, of which 6 were waited for; matrix products, arithmetic and copies ran while one was open for 0% of the time, Pallas kernels for 8%

profile of v3, /device:TPU:0, one launch (start us, length us, event | category | flops | bytes accessed | tf_op | source)
XLA Modules:
  0.0 64.9 jit_solution(9350007995517145665)
XLA Ops:
  0.0 0.9 %copy-done = f32[1,32,1024]{2,1,0:T(8,128)S(1)} copy-done((f32[1,32,1024]{2,1,0:T(8,128)S(1)}, f32[1,32,1024]{2,1,0:T(8,128)}, u32[]{:S(2)}) %copy-start) | copy-done | bytes 131096
  0.9 0.9 %copy-done.1 = f32[32,1024]{1,0:T(8,128)S(1)} copy-done((f32[32,1024]{1,0:T(8,128)S(1)}, f32[32,1024]{1,0:T(8,128)}, u32[]{:S(2)}) %copy-start.1) | copy-done | bytes 131096
  1.8 0.9 %copy-done.2 = f32[32,1024]{1,0:T(8,128)S(1)} copy-done((f32[32,1024]{1,0:T(8,128)S(1)}, f32[32,1024]{1,0:T(8,128)}, u32[]{:S(2)}) %copy-start.2) | copy-done | bytes 131096
  2.7 0.7 %copy-done.7 = s32[4,8]{1,0:T(4,128)S(1)} copy-done((s32[4,8]{1,0:T(4,128)S(1)}, s32[4,8]{1,0:T(4,128)}, u32[]{:S(2)}) %copy-start.7) | copy-done | bytes 152
  3.4 0.7 %copy-done.8 = f32[16]{0:T(128)S(1)} copy-done((f32[16]{0:T(128)S(1)}, f32[16]{0:T(128)}, u32[]{:S(2)}) %copy-start.8) | copy-done | bytes 88
  4.1 1.0 %shard_map.82 = (f32[64,1024]{1,0:T(8,128)S(1)}, f32[64,1024]{1,0:T(8,128)S(1)}, f32[24,512]{1,0:T(8,128)S(1)}) custom-call(f32[32,1024]{1,0:T(8,128)S(1)} %bitcast.2, f32[32,1024]{1,0:T(8,128)S(1)} %copy-done.1, f32[32,1024]{1,0:T(8,128)S(1)} %copy-done.2, f32[16]{0:T(128)S(1)} %copy-done.8, s32[4,8]{1,0:T(4,128)S(1)} %copy-done.7), custom_call_target="tpu_custom_call" | custom-call | flops 1048576 | bytes 1048576 | tf_op jit(solution)/shard_map/pallas_call | solution.py:473
  5.0 3.1 %collective-permute-start = (f32[64,1024]{1,0:T(8,128)S(1)}, f32[64,1024]{1,0:T(8,128)S(1)}, u32[]{:S(2)}, u32[]{:S(2)}) collective-permute-start(f32[64,1024]{1,0:T(8,128)S(1)} %get-tuple-element.18), channel_id=1, source_target_pairs={{0,1},{1,0},{2,3},{3,2},{4,5},{5,4},{6,7},{7,6},{8,9},{9,8},{10,11... | collective-permute-start | bytes 786440 | tf_op jit(solution)/shard_map/ppermute | solution.py:471
  8.2 0.7 %collective-permute-start.1 = (f32[64,1024]{1,0:T(8,128)S(1)}, f32[64,1024]{1,0:T(8,128)S(1)}, u32[]{:S(2)}, u32[]{:S(2)}) collective-permute-start(f32[64,1024]{1,0:T(8,128)S(1)} %get-tuple-element.19), channel_id=1, source_target_pairs={{1,2},{2,1},{5,6},{6,5},{9,10},{10,9},{13,14},{14,13},{17,18},{18,... | collective-permute-start | bytes 786440 | tf_op jit(solution)/shard_map/ppermute | solution.py:471
  8.8 5.6 %collective-permute-done.got_a = f32[64,1024]{1,0:T(8,128)S(1)} collective-permute-done((f32[64,1024]{1,0:T(8,128)S(1)}, f32[64,1024]{1,0:T(8,128)S(1)}, u32[]{:S(2)}, u32[]{:S(2)}) %collective-permute-start) | collective-permute-done | bytes 262176 | tf_op jit(solution)/shard_map/ppermute | solution.py:471
  14.5 0.9 %copy-done.3 = f32[32,1024]{1,0:T(8,128)S(1)} copy-done((f32[32,1024]{1,0:T(8,128)S(1)}, f32[32,1024]{1,0:T(8,128)}, u32[]{:S(2)}) %copy-start.3) | copy-done | bytes 131096
  15.4 0.7 %copy-done.4 = s32[8]{0:T(128)S(1)} copy-done((s32[8]{0:T(128)S(1)}, s32[8]{0:T(128)}, u32[]{:S(2)}) %copy-start.4) | copy-done | bytes 56
  16.0 0.7 %copy-done.9 = f32[128]{0:T(128)S(1)} copy-done((f32[128]{0:T(128)S(1)}, f32[128]{0:T(128)}, u32[]{:S(2)}) %copy-start.9) | copy-done | bytes 536
  16.7 5.3 %shard_map.83 = (f32[32,1024]{1,0:T(8,128)S(1)}, f32[24,1024]{1,0:T(8,128)S(1)}, f32[24,1024]{1,0:T(8,128)S(1)}, f32[5,8,80,128]{3,2,1,0:T(8,128)S(1)}) custom-call(f32[32,1024]{1,0:T(8,128)S(1)} %bitcast.3, f32[32,1024]{1,0:T(8,128)S(1)} %copy-done.1, f32[32,1024]{1,0:T(8,128)S(1)} %copy-done.2, f32[64,1024]{1,0:T(8,128)S(1)} %collective-permute-done.got_a, ...), custom_call_target="tpu_custom_call" | custom-call | flops 16777216 | bytes 1048576 | tf_op jit(solution)/shard_map/pallas_call | solution.py:482
  22.1 6.4 %collective-permute-start.3 = (f32[24,1024]{1,0:T(8,128)S(1)}, f32[24,1024]{1,0:T(8,128)S(1)}, u32[]{:S(2)}, u32[]{:S(2)}) collective-permute-start(f32[24,1024]{1,0:T(8,128)S(1)} %get-tuple-element.21), channel_id=1, source_target_pairs={{0,5},{1,4},{2,7},{3,6},{4,9},{5,8},{6,11},{7,10},{8,13},{9,12},{1... | collective-permute-start | bytes 294920 | tf_op jit(solution)/shard_map/ppermute | solution.py:471
  28.4 0.7 %collective-permute-start.4 = (f32[24,1024]{1,0:T(8,128)S(1)}, f32[24,1024]{1,0:T(8,128)S(1)}, u32[]{:S(2)}, u32[]{:S(2)}) collective-permute-start(f32[24,1024]{1,0:T(8,128)S(1)} %get-tuple-element.22), channel_id=1, source_target_pairs={{1,6},{2,5},{5,10},{6,9},{9,14},{10,13},{13,18},{14,17},{17,22},{1... | collective-permute-start | bytes 294920 | tf_op jit(solution)/shard_map/ppermute | solution.py:471
  29.1 2.7 %collective-permute-start.10 = (f32[24,512]{1,0:T(8,128)S(1)}, f32[24,512]{1,0:T(8,128)S(1)}, u32[]{:S(2)}, u32[]{:S(2)}) collective-permute-start(f32[24,512]{1,0:T(8,128)S(1)} %get-tuple-element.24.refs_4_), channel_id=1, source_target_pairs={{0,3},{1,2},{2,1},{3,0},{4,7},{5,6},{6,5},{7,4},{8,11},{9,10},{10,... | collective-permute-start | bytes 147464 | tf_op jit(solution)/shard_map/ppermute | solution.py:471
  31.8 0.6 collective-permute-start.8
  32.4 1.7 %collective-permute-start.9 = (f32[24,512]{1,0:T(8,128)S(1)}, f32[24,512]{1,0:T(8,128)S(1)}, u32[]{:S(2)}, u32[]{:S(2)}) collective-permute-start(f32[24,512]{1,0:T(8,128)S(1)} %get-tuple-element.24.refs_4_), channel_id=1, source_target_pairs={{0,2},{1,3},{2,0},{3,1},{4,6},{5,7},{6,4},{7,5},{8,10},{9,11},{10,... | collective-permute-start | bytes 147464 | tf_op jit(solution)/shard_map/ppermute | solution.py:471
  34.1 0.7 %copy-done.5 = s32[8]{0:T(128)S(1)} copy-done((s32[8]{0:T(128)S(1)}, s32[8]{0:T(128)}, u32[]{:S(2)}) %copy-start.5) | copy-done | bytes 56
  34.8 4.9 %shard_map.84.refs_0_ = f32[16,512]{1,0:T(8,128)S(1)} custom-call(f32[32,1024]{1,0:T(8,128)S(1)} %collective-permute-done.2.relaxed.refs_5_, f32[24,1024]{1,0:T(8,128)S(1)} %collective-permute-done.3.edge_a, f32[24,1024]{1,0:T(8,128)S(1)} %collective-permute-done.4.edge_b, f32[32,1024]{1,0:T(8,128)S(1)} %bitcast.4, ...), custom_call_target="tpu_custom_call" | custom-call | flops 16777216 | bytes 1048576 | tf_op jit(solution)/shard_map/pallas_call | solution.py:498
  39.7 2.3 %collective-permute-start.5 = (f32[16,512]{1,0:T(8,128)S(1)}, f32[16,512]{1,0:T(8,128)S(1)}, u32[]{:S(2)}, u32[]{:S(2)}) collective-permute-start(f32[16,512]{1,0:T(8,128)S(1)} %shard_map.84.refs_0_), channel_id=1, source_target_pairs={{0,1},{1,0},{2,3},{3,2},{4,5},{5,4},{6,7},{7,6},{8,9},{9,8},{10,11... | collective-permute-start | bytes 98312 | tf_op jit(solution)/shard_map/ppermute | solution.py:471
  42.0 0.4 collective-permute-start.6
  42.4 2.0 %collective-permute-start.7 = (f32[16,512]{1,0:T(8,128)S(1)}, f32[16,512]{1,0:T(8,128)S(1)}, u32[]{:S(2)}, u32[]{:S(2)}) collective-permute-start(f32[16,512]{1,0:T(8,128)S(1)} %shard_map.84.refs_0_), channel_id=1, source_target_pairs={{0,3},{1,2},{2,1},{3,0},{4,7},{5,6},{6,5},{7,4},{8,11},{9,10},{10,... | collective-permute-start | bytes 98312 | tf_op jit(solution)/shard_map/ppermute | solution.py:471
  44.4 2.9 %collective-permute-done.6.refs_2_ = f32[16,512]{1,0:T(8,128)S(1)} collective-permute-done((f32[16,512]{1,0:T(8,128)S(1)}, f32[16,512]{1,0:T(8,128)S(1)}, u32[]{:S(2)}, u32[]{:S(2)}) %collective-permute-start.6) | collective-permute-done | bytes 32800 | tf_op jit(solution)/shard_map/ppermute | solution.py:471
  47.3 0.9 %collective-permute-done.7.refs_3_ = f32[16,512]{1,0:T(8,128)S(1)} collective-permute-done((f32[16,512]{1,0:T(8,128)S(1)}, f32[16,512]{1,0:T(8,128)S(1)}, u32[]{:S(2)}, u32[]{:S(2)}) %collective-permute-start.7) | collective-permute-done | bytes 32800 | tf_op jit(solution)/shard_map/ppermute | solution.py:471
  48.7 1.1 %collective-permute-done.11.refs_1_ = f32[4,64,128]{2,1,0:T(8,128)S(1)} collective-permute-done((f32[4,64,128]{2,1,0:T(8,128)S(1)}, f32[4,64,128]{2,1,0:T(8,128)S(1)}, u32[]{:S(2)}, u32[]{:S(2)}) %collective-permute-start.11) | collective-permute-done | bytes 131104 | tf_op jit(solution)/shard_map/ppermute | solution.py:516
  49.8 1.1 %shard_map.86 = (f32[4,64,128]{2,1,0:T(8,128)S(1)}, f32[4,16,128]{2,1,0:T(8,128)S(1)}) custom-call(f32[4,64,128]{2,1,0:T(8,128)S(1)} %get-tuple-element.25.refs_0_, f32[4,64,128]{2,1,0:T(8,128)S(1)} %collective-permute-done.11.refs_1_, f32[5,4,64,128]{3,2,1,0:T(8,128)S(1)} %get-tuple-element.26.refs_2_.refs_3_, s32[8]{0:T(128)S(1)} %copy-done.6), custom_call_target="tpu_custom_call" | custom-call | flops 8388608 | bytes 1048576 | tf_op jit(solution)/shard_map/pallas_call | solution.py:533
  51.0 1.3 %collective-permute-start.12 = (f32[4,64,128]{2,1,0:T(8,128)S(1)}, f32[4,64,128]{2,1,0:T(8,128)S(1)}, u32[]{:S(2)}, u32[]{:S(2)}) collective-permute-start(f32[4,64,128]{2,1,0:T(8,128)S(1)} %get-tuple-element.27.refs_0_), channel_id=1, source_target_pairs={{0,8},{4,12},{8,0},{12,4},{16,24},{20,28},{24,16},{28,20},{1,9},{5... | collective-permute-start | bytes 393224 | tf_op jit(solution)/shard_map/ppermute | solution.py:516
  52.3 4.4 %collective-permute-done.12.refs_1_ = f32[4,64,128]{2,1,0:T(8,128)S(1)} collective-permute-done((f32[4,64,128]{2,1,0:T(8,128)S(1)}, f32[4,64,128]{2,1,0:T(8,128)S(1)}, u32[]{:S(2)}, u32[]{:S(2)}) %collective-permute-start.12) | collective-permute-done | bytes 131104 | tf_op jit(solution)/shard_map/ppermute | solution.py:516
  56.7 1.6 %shard_map.87 = (f32[4,64,128]{2,1,0:T(8,128)S(1)}, f32[4,16,128]{2,1,0:T(8,128)S(1)}) custom-call(f32[4,64,128]{2,1,0:T(8,128)S(1)} %get-tuple-element.27.refs_0_, f32[4,64,128]{2,1,0:T(8,128)S(1)} %collective-permute-done.12.refs_1_, f32[4,16,128]{2,1,0:T(8,128)S(1)} %get-tuple-element.28.refs_2_, f32[5,4,64,128]{3,2,1,0:T(8,128)S(1)} %get-tuple-element.26.refs_2_.refs_3_, ...), custom_call_target="tpu_custom_call" | custom-call | flops 8388608 | bytes 1048576 | tf_op jit(solution)/shard_map/pallas_call | solution.py:533
  58.4 5.0 %collective-permute-done.13.refs_1_ = f32[4,64,128]{2,1,0:T(8,128)S(1)} collective-permute-done((f32[4,64,128]{2,1,0:T(8,128)S(1)}, f32[4,64,128]{2,1,0:T(8,128)S(1)}, u32[]{:S(2)}, u32[]{:S(2)}) %collective-permute-start.13) | collective-permute-done | bytes 131104 | tf_op jit(solution)/shard_map/ppermute | solution.py:516
  63.3 1.6 %shard_map.88 = f32[32,1024]{1,0:T(8,128)} custom-call(f32[4,64,128]{2,1,0:T(8,128)S(1)} %get-tuple-element.29.refs_0_, f32[4,64,128]{2,1,0:T(8,128)S(1)} %collective-permute-done.13.refs_1_, f32[4,16,128]{2,1,0:T(8,128)S(1)} %get-tuple-element.30.refs_2_, f32[5,4,64,128]{3,2,1,0:T(8,128)S(1)} %get-tuple-element.26.refs_2_.refs_3_, s32[8]{0:T(128)S(1)} %copy-done.6, ...), custom_call_target="tpu_custom_call" | custom-call | flops 8388608 | bytes 1048576 | tf_op jit(solution)/shard_map/pallas_call | solution.py:528
  (23 shorter events, 0.7 us)
Async XLA Ops:
  0.0 0.9 %copy-start = (f32[1,32,1024]{2,1,0:T(8,128)S(1)}, f32[1,32,1024]{2,1,0:T(8,128)}, u32[]{:S(2)}) copy-start(f32[1,32,1024]{2,1,0:T(8,128)} %param.8) | copy-start | bytes 393220
  0.9 0.9 %copy-start.1 = (f32[32,1024]{1,0:T(8,128)S(1)}, f32[32,1024]{1,0:T(8,128)}, u32[]{:S(2)}) copy-start(f32[32,1024]{1,0:T(8,128)} %rate.3) | copy-start | bytes 393220
  1.8 0.9 %copy-start.2 = (f32[32,1024]{1,0:T(8,128)S(1)}, f32[32,1024]{1,0:T(8,128)}, u32[]{:S(2)}) copy-start(f32[32,1024]{1,0:T(8,128)} %source.3) | copy-start | bytes 393220
  2.7 0.7 %copy-start.7 = (s32[4,8]{1,0:T(4,128)S(1)}, s32[4,8]{1,0:T(4,128)}, u32[]{:S(2)}) copy-start(s32[4,8]{1,0:T(4,128)} %classes.3) | copy-start | bytes 388
  3.4 0.7 %copy-start.8 = (f32[16]{0:T(128)S(1)}, f32[16]{0:T(128)}, u32[]{:S(2)}) copy-start(f32[16]{0:T(128)} %table.3) | copy-start | bytes 196
  5.0 9.4 %collective-permute-start = (f32[64,1024]{1,0:T(8,128)S(1)}, f32[64,1024]{1,0:T(8,128)S(1)}, u32[]{:S(2)}, u32[]{:S(2)}) collective-permute-start(f32[64,1024]{1,0:T(8,128)S(1)} %get-tuple-element.18), channel_id=1, source_target_pairs={{0,1},{1,0},{2,3},{3,2},{4,5},{5,4},{6,7},{7,6},{8,9},{9,8},{10,11... | collective-permute-start | bytes 786440 | tf_op jit(solution)/shard_map/ppermute | solution.py:471
  8.2 6.3 %collective-permute-start.1 = (f32[64,1024]{1,0:T(8,128)S(1)}, f32[64,1024]{1,0:T(8,128)S(1)}, u32[]{:S(2)}, u32[]{:S(2)}) collective-permute-start(f32[64,1024]{1,0:T(8,128)S(1)} %get-tuple-element.19), channel_id=1, source_target_pairs={{1,2},{2,1},{5,6},{6,5},{9,10},{10,9},{13,14},{14,13},{17,18},{18,... | collective-permute-start | bytes 786440 | tf_op jit(solution)/shard_map/ppermute | solution.py:471
  14.5 0.9 %copy-start.3 = (f32[32,1024]{1,0:T(8,128)S(1)}, f32[32,1024]{1,0:T(8,128)}, u32[]{:S(2)}) copy-start(f32[32,1024]{1,0:T(8,128)} %initial.1) | copy-start | bytes 393220
  15.4 0.7 %copy-start.4 = (s32[8]{0:T(128)S(1)}, s32[8]{0:T(128)}, u32[]{:S(2)}) copy-start(s32[8]{0:T(128)} %refs_4_.3) | copy-start | bytes 100
  16.0 0.7 %copy-start.9 = (f32[128]{0:T(128)S(1)}, f32[128]{0:T(128)}, u32[]{:S(2)}) copy-start(f32[128]{0:T(128)} %waveform.1) | copy-start | bytes 1540
  22.0 27.9 %copy-start.6 = (s32[8]{0:T(128)S(1)}, s32[8]{0:T(128)}, u32[]{:S(2)}) copy-start(s32[8]{0:T(128)} %refs_4_.3) | copy-start | bytes 100
  22.0 12.2 %collective-permute-start.2 = (f32[32,1024]{1,0:T(8,128)S(1)}, f32[32,1024]{1,0:T(8,128)S(1)}, u32[]{:S(2)}, u32[]{:S(2)}) collective-permute-start(f32[32,1024]{1,0:T(8,128)S(1)} %get-tuple-element.20), channel_id=1, source_target_pairs={{0,4},{1,5},{2,6},{3,7},{4,8},{5,9},{6,10},{7,11},{8,12},{9,13},{1... | collective-permute-start | bytes 393224 | tf_op jit(solution)/shard_map/ppermute | solution.py:471
  22.1 10.4 %collective-permute-start.3 = (f32[24,1024]{1,0:T(8,128)S(1)}, f32[24,1024]{1,0:T(8,128)S(1)}, u32[]{:S(2)}, u32[]{:S(2)}) collective-permute-start(f32[24,1024]{1,0:T(8,128)S(1)} %get-tuple-element.21), channel_id=1, source_target_pairs={{0,5},{1,4},{2,7},{3,6},{4,9},{5,8},{6,11},{7,10},{8,13},{9,12},{1... | collective-permute-start | bytes 294920 | tf_op jit(solution)/shard_map/ppermute | solution.py:471
  28.4 5.7 %collective-permute-start.4 = (f32[24,1024]{1,0:T(8,128)S(1)}, f32[24,1024]{1,0:T(8,128)S(1)}, u32[]{:S(2)}, u32[]{:S(2)}) collective-permute-start(f32[24,1024]{1,0:T(8,128)S(1)} %get-tuple-element.22), channel_id=1, source_target_pairs={{1,6},{2,5},{5,10},{6,9},{9,14},{10,13},{13,18},{14,17},{17,22},{1... | collective-permute-start | bytes 294920 | tf_op jit(solution)/shard_map/ppermute | solution.py:471
  29.1 13.3 %collective-permute-start.10 = (f32[24,512]{1,0:T(8,128)S(1)}, f32[24,512]{1,0:T(8,128)S(1)}, u32[]{:S(2)}, u32[]{:S(2)}) collective-permute-start(f32[24,512]{1,0:T(8,128)S(1)} %get-tuple-element.24.refs_4_), channel_id=1, source_target_pairs={{0,3},{1,2},{2,1},{3,0},{4,7},{5,6},{6,5},{7,4},{8,11},{9,10},{10,... | collective-permute-start | bytes 147464 | tf_op jit(solution)/shard_map/ppermute | solution.py:471
  31.8 12.6 %collective-permute-start.8 = (f32[24,512]{1,0:T(8,128)S(1)}, f32[24,512]{1,0:T(8,128)S(1)}, u32[]{:S(2)}, u32[]{:S(2)}) collective-permute-start(f32[24,512]{1,0:T(8,128)S(1)} %get-tuple-element.24.refs_4_), channel_id=1, source_target_pairs={{0,1},{1,0},{2,3},{3,2},{4,5},{5,4},{6,7},{7,6},{8,9},{9,8},{10,11... | collective-permute-start | bytes 147464 | tf_op jit(solution)/shard_map/ppermute | solution.py:471
  32.4 12.0 %collective-permute-start.9 = (f32[24,512]{1,0:T(8,128)S(1)}, f32[24,512]{1,0:T(8,128)S(1)}, u32[]{:S(2)}, u32[]{:S(2)}) collective-permute-start(f32[24,512]{1,0:T(8,128)S(1)} %get-tuple-element.24.refs_4_), channel_id=1, source_target_pairs={{0,2},{1,3},{2,0},{3,1},{4,6},{5,7},{6,4},{7,5},{8,10},{9,11},{10,... | collective-permute-start | bytes 147464 | tf_op jit(solution)/shard_map/ppermute | solution.py:471
  34.1 0.7 %copy-start.5 = (s32[8]{0:T(128)S(1)}, s32[8]{0:T(128)}, u32[]{:S(2)}) copy-start(s32[8]{0:T(128)} %refs_4_.3) | copy-start | bytes 100
  39.7 4.7 %collective-permute-start.5 = (f32[16,512]{1,0:T(8,128)S(1)}, f32[16,512]{1,0:T(8,128)S(1)}, u32[]{:S(2)}, u32[]{:S(2)}) collective-permute-start(f32[16,512]{1,0:T(8,128)S(1)} %shard_map.84.refs_0_), channel_id=1, source_target_pairs={{0,1},{1,0},{2,3},{3,2},{4,5},{5,4},{6,7},{7,6},{8,9},{9,8},{10,11... | collective-permute-start | bytes 98312 | tf_op jit(solution)/shard_map/ppermute | solution.py:471
  42.0 5.4 %collective-permute-start.6 = (f32[16,512]{1,0:T(8,128)S(1)}, f32[16,512]{1,0:T(8,128)S(1)}, u32[]{:S(2)}, u32[]{:S(2)}) collective-permute-start(f32[16,512]{1,0:T(8,128)S(1)} %shard_map.84.refs_0_), channel_id=1, source_target_pairs={{0,2},{1,3},{2,0},{3,1},{4,6},{5,7},{6,4},{7,5},{8,10},{9,11},{10,... | collective-permute-start | bytes 98312 | tf_op jit(solution)/shard_map/ppermute | solution.py:471
  42.4 5.8 %collective-permute-start.7 = (f32[16,512]{1,0:T(8,128)S(1)}, f32[16,512]{1,0:T(8,128)S(1)}, u32[]{:S(2)}, u32[]{:S(2)}) collective-permute-start(f32[16,512]{1,0:T(8,128)S(1)} %shard_map.84.refs_0_), channel_id=1, source_target_pairs={{0,3},{1,2},{2,1},{3,0},{4,7},{5,6},{6,5},{7,4},{8,11},{9,10},{10,... | collective-permute-start | bytes 98312 | tf_op jit(solution)/shard_map/ppermute | solution.py:471
  48.4 1.4 %collective-permute-start.11 = (f32[4,64,128]{2,1,0:T(8,128)S(1)}, f32[4,64,128]{2,1,0:T(8,128)S(1)}, u32[]{:S(2)}, u32[]{:S(2)}) collective-permute-start(f32[4,64,128]{2,1,0:T(8,128)S(1)} %get-tuple-element.25.refs_0_), channel_id=1, source_target_pairs={{0,4},{4,0},{8,12},{12,8},{16,20},{20,16},{24,28},{28,24},{1,5},{5... | collective-permute-start | bytes 393224 | tf_op jit(solution)/shard_map/ppermute | solution.py:516
  51.0 5.7 %collective-permute-start.12 = (f32[4,64,128]{2,1,0:T(8,128)S(1)}, f32[4,64,128]{2,1,0:T(8,128)S(1)}, u32[]{:S(2)}, u32[]{:S(2)}) collective-permute-start(f32[4,64,128]{2,1,0:T(8,128)S(1)} %get-tuple-element.27.refs_0_), channel_id=1, source_target_pairs={{0,8},{4,12},{8,0},{12,4},{16,24},{20,28},{24,16},{28,20},{1,9},{5... | collective-permute-start | bytes 393224 | tf_op jit(solution)/shard_map/ppermute | solution.py:516
  58.3 5.0 %collective-permute-start.13 = (f32[4,64,128]{2,1,0:T(8,128)S(1)}, f32[4,64,128]{2,1,0:T(8,128)S(1)}, u32[]{:S(2)}, u32[]{:S(2)}) collective-permute-start(f32[4,64,128]{2,1,0:T(8,128)S(1)} %get-tuple-element.29.refs_0_), channel_id=1, source_target_pairs={{0,16},{4,20},{8,24},{12,28},{16,0},{20,4},{24,8},{28,12},{1,17},{... | collective-permute-start | bytes 393224 | tf_op jit(solution)/shard_map/ppermute | solution.py:516

commit v4 on v3

--- a/solution.py
+++ b/solution.py
@@ -7,10 +7,10 @@
 from jax.experimental.pallas import tpu as pltpu
 from jax.sharding import PartitionSpec as P
 
+
 STEP_MOST = 20
 CSUB = 5
 BLK_R = 8
-BLK_C = 128
 SUB = 8
 LANES = 128
 MAIN = STEP_MOST // SUB * SUB
@@ -20,6 +20,7 @@
 PAD = SUB
 VM = pl.BlockSpec(memory_space=pltpu.VMEM)
 SM = pl.BlockSpec(memory_space=pltpu.SMEM)
+FAR = pl.BlockSpec(memory_space=pltpu.HBM)
 F32 = jnp.float32
 GRANT = 16 << 20
 
@@ -38,6 +39,10 @@
         compiler_params=pltpu.CompilerParams(vmem_limit_bytes=GRANT),
         cost_estimate=pl.CostEstimate(flops=flops, bytes_accessed=1 << 20, transcendentals=0),
     )
+
+
+def far(value):
+    return pltpu.with_memory_space_constraint(value, pltpu.HBM)
 
 
 def iota(axis, shape=(SUB, LANES)):
@@ -82,10 +87,33 @@
     return top + ref[(*index, pl.ds(first + 1, rows, stride=2), slice(None))]
 
 
-def pack_body(point, rate, source, table, classes, pay_a, pay_b, coarse, tmp):
+def fetch(pairs, sems):
+    copies = [pltpu.make_async_copy(source, target, sems.at[i]) for i, (source, target) in enumerate(pairs)]
+    for copy in copies:
+        copy.start()
+    return copies
+
+
+def pack_body(
+    point_far, rate_far, source_far, initial_far, table_far, classes_far,
+    pay_a, pay_b, coarse, blocks_out, point, rate, source, initial, table, classes, tmp, sems,
+):
+    copies = fetch(
+        (
+            (table_far, table), (classes_far, classes), (rate_far, rate),
+            (point_far, point), (source_far, source), (initial_far, initial),
+        ), sems,
+    )
     rows, width = point.shape
     blocks, tiles = rows // BLK_R, width // LANES
     odd = lax.rem(lax.axis_index("space"), 2) == 1
+    copies[0].wait()
+    copies[1].wait()
+    for b in range(blocks):
+        for c in range(tiles):
+            blocks_out[b : b + 1, cols(c)] = jnp.full((1, LANES), table[classes[b, c]], F32)
+    for copy in copies[2:5]:
+        copy.wait()
 
     def fill(out, high):
         main = rows - MAIN if high else 0
@@ -95,11 +123,8 @@
             at = 3 * MAIN + i * REST
             out[at : at + REST, :] = ref[rest : rest + REST, :]
         first = blocks - HT if high else 0
-        for b in range(HT):
-            for c in range(tiles):
-                value = table[classes[first + b, c]]
-                at = 3 * MAIN + 3 * REST + b
-                out[at : at + 1, cols(c)] = jnp.full((1, LANES), value, F32)
+        at = 3 * MAIN + 3 * REST
+        out[at : at + HT, :] = blocks_out[first : first + HT, :]
 
     @pl.when(odd)
     def _():
@@ -117,10 +142,11 @@
     for c in range(tiles // 2):
         wide = jnp.concatenate([row_pairs(tmp, (2 * c + k,), 0, rows // 2) for k in (0, 1)], axis=1)
         coarse[: rows // 2, cols(c)] = 0.25 * dot(wide, pairs)
-        for b in range(blocks):
-            halves = [jnp.full((1, LANES), table[classes[b, 2 * c + k]], F32) for k in (0, 1)]
-            at = rows // 2 + b
-            coarse[at : at + 1, cols(c)] = jnp.where(iota(1, (1, LANES)) < LANES // 2, halves[0], halves[1])
+        halves = [blocks_out[0:blocks, cols(2 * c + k)] for k in (0, 1)]
+        coarse[rows // 2 : rows // 2 + blocks, cols(c)] = jnp.where(
+            iota(1, (blocks, LANES)) < LANES // 2, halves[0], halves[1]
+        )
+    copies[5].wait()
 
 
 def sweep(state, spare, weights, force, count, tiles, strip_tiles, wave):
@@ -182,15 +208,19 @@
 
 
 def first_body(
-    point, rate, source, got_a, got_b, initial, table, classes, steps, waveform,
-    relaxed, edge_a, edge_b, weights, state, spare, force, rates, conduct,
+    point, rate, source, got_a, got_b, initial, own_blocks, steps_far, waveform_far,
+    relaxed, edge_a, edge_b, weights, state, spare, force, rates, conduct, steps, waveform, sems,
 ):
+    copies = fetch(((steps_far, steps), (waveform_far, waveform)), sems)
     rows, width = point.shape
-    tiles, strip_tiles, blocks = width // LANES, rows // SUB, rows // BLK_R
+    tiles, strip_tiles = width // LANES, rows // SUB
+    every = 2 * HT + strip_tiles
     mine, strip = lax.axis_index("tm"), lax.axis_index("space")
     odd = lax.rem(strip, 2) == 1
-    start = lax.fori_loop(0, mine, lambda i, total: total + steps[i], jnp.int32(0))
-    count = steps[mine]
+    zero = jnp.zeros((SUB, LANES), F32)
+
+    def block(row):
+        return jnp.broadcast_to(row, (SUB, LANES))
 
     for c in range(tiles):
         for r in range(strip_tiles):
@@ -198,12 +228,7 @@
             state[c, PAD + HALO + r * SUB : PAD + HALO + (r + 1) * SUB, :] = point[at, cols(c)]
             rates[c, to, :] = rate[at, cols(c)]
             force[c, to, :] = source[at, cols(c)]
-        for b in range(blocks):
-            at = PAD + HALO + b * BLK_R
-            conduct[c, at : at + BLK_R, :] = jnp.full((BLK_R, LANES), table[classes[b, c]], F32)
-        zero = jnp.zeros((SUB, LANES), F32)
-        conduct[c, 0:PAD, :] = zero
-        conduct[c, PAD + 2 * HALO + rows :, :] = zero
+            conduct[c, to, :] = block(own_blocks[r : r + 1, cols(c)])
         for at in (0, HALO + rows + HALO - SUB):
             rates[c, at : at + SUB, :] = zero
             force[c, at : at + SUB, :] = zero
@@ -214,27 +239,40 @@
         unpack(rates, tiles, rows, payload, above, 1)
         unpack(force, tiles, rows, payload, above, 2)
         for b in range(HT):
-            at = PAD + b * BLK_R + (0 if above else HALO + rows)
+            at = b * SUB + (0 if above else HALO + rows)
             row = 3 * MAIN + 3 * REST + b
             for c in range(tiles):
-                conduct[c, at : at + BLK_R, :] = jnp.broadcast_to(payload[row : row + 1, cols(c)], (BLK_R, LANES))
+                conduct[c, at : at + SUB, :] = block(payload[row : row + 1, cols(c)])
 
     with_halos(odd, got_a, got_b, place)
 
-    zero = jnp.zeros((SUB, LANES), F32)
-    for r in range(2 * HT + strip_tiles):
-        at = PAD + r * SUB
-        here = [conduct[c, at : at + SUB, :] for c in range(tiles)]
-        for c in range(tiles):
-            left, right = beside(here, c, zero)
-            above = conduct[c, at - 1 : at + SUB - 1, :]
-            below = conduct[c, at + 1 : at + SUB + 1, :]
-            own = rates[c, r * SUB : (r + 1) * SUB, :]
-            w = [own * jnp.sqrt(here[c] * other) for other in (above, below, left, right)]
+    sub, lane = iota(0), iota(1)
+    here = [conduct[c, 0:SUB, :] for c in range(tiles)]
+    over = [zero] * tiles
+    for r in range(every):
+        if r + 1 < every:
+            follow = [conduct[c, (r + 1) * SUB : (r + 2) * SUB, :] for c in range(tiles)]
+            under = [jnp.sqrt(k * f) for k, f in zip(here, follow)]
+        else:
+            follow, under = here, [zero] * tiles
+        sides = [zero] + [jnp.sqrt(here[c] * here[c + 1]) for c in range(tiles - 1)] + [zero]
+        for c in range(tiles):
+            own, k = rates[c, r * SUB : (r + 1) * SUB, :], here[c]
+            w = [
+                own * jnp.where(sub == 0, over[c], k),
+                own * jnp.where(sub == SUB - 1, under[c], k),
+                own * jnp.where(lane == 0, sides[c], k),
+                own * jnp.where(lane == LANES - 1, sides[c + 1], k),
+            ]
             weights[0, c, r * SUB : (r + 1) * SUB, :] = 1.0 - (((w[0] + w[1]) + w[2]) + w[3])
-            for k in range(4):
-                weights[k + 1, c, r * SUB : (r + 1) * SUB, :] = w[k]
-
+            for i in range(4):
+                weights[i + 1, c, r * SUB : (r + 1) * SUB, :] = w[i]
+        here, over = follow, under
+
+    for copy in copies:
+        copy.wait()
+    start = lax.fori_loop(0, mine, lambda i, total: total + steps[i], jnp.int32(0))
+    count = steps[mine]
     sweep(state, spare, weights, force, count, tiles, strip_tiles, lambda t: waveform[start + t])
 
     def give(read):
@@ -267,12 +305,14 @@
         give(lambda r, c: state[c, PAD + HALO + r * SUB : PAD + HALO + (r + 1) * SUB, :])
 
 
-def second_body(relaxed, edge_a, edge_b, point, got_a, got_b, weights, steps, coarse, state, spare, tmp):
+def second_body(
+    relaxed, edge_a, edge_b, point, got_a, got_b, weights, steps_far, coarse, state, spare, tmp, steps, sems
+):
+    copies = fetch(((steps_far, steps),), sems)
     rows, width = point.shape
     tiles, strip_tiles = width // LANES, rows // SUB
     mine, strip = lax.axis_index("tm"), lax.axis_index("space")
     odd = lax.rem(strip, 2) == 1
-    count = steps[mine]
     for c in range(tiles):
         for r in range(strip_tiles):
             at = slice(r * SUB, (r + 1) * SUB)
@@ -291,6 +331,8 @@
                 state[c, PAD + at : PAD + at + SUB, :] = edge[r * SUB : (r + 1) * SUB, cols(c)] - tmp[c, at : at + SUB, :]
 
     with_halos(odd, (edge_a, got_a), (edge_b, got_b), place)
+    copies[0].wait()
+    count = steps[mine]
     sweep(state, spare, weights, None, count, tiles, strip_tiles, None)
     pairs = halve()
     for c in range(tiles // 2):
@@ -470,37 +512,45 @@
                     pairs.append((j * strips + s, ((j + ahead) % intervals) * strips + to))
         return lax.ppermute(value, both, pairs)
 
-    pay_a, pay_b, field = call(
-        pack_body, [VM, VM, VM, SM, SM],
-        (f32(packed, width), f32(packed, width), f32(fields_rows, width // 2)),
-        [pltpu.VMEM((tiles, rows, LANES), F32)], 1 << 20,
-    )(point, node_rate, source_map, cond_table, class_map)
+    strip = f32(rows, width)
+    pay_a, pay_b, field, own_blocks, point, rate, source, initial = call(
+        pack_body, [FAR] * 6,
+        (f32(packed, width), f32(packed, width), f32(fields_rows, width // 2), f32(SUB, width), strip, strip, strip, strip),
+        [
+            pltpu.SMEM(cond_table.shape, F32),
+            pltpu.SMEM(class_map.shape, jnp.int32),
+            pltpu.VMEM((tiles, rows, LANES), F32),
+            pltpu.SemaphoreType.DMA((6,)),
+        ],
+        1 << 20,
+    )(*[far(x) for x in (point, node_rate, source_map, initial_state, cond_table, class_map)])
     got_a = exchange(pay_a, 0, lambda s: side(s, "a"))
     got_b = exchange(pay_b, 0, lambda s: side(s, "b"))
-    fields = [field] + [exchange(field, 0, lambda s, k=k: s ^ k) for k in range(1, strips)]
-
+    fields = [field]
+    for k in range(1, strips):
+        fields.append(exchange(field, 0, lambda s, k=k: s ^ k))
+
+    grid = pltpu.VMEM((tiles, height + 2 * PAD, LANES), F32)
+    flat = pltpu.VMEM((tiles, height, LANES), F32)
+    steps_near = pltpu.SMEM(interval_steps.shape, jnp.int32)
     passed, edge_a, edge_b, weights = call(
-        first_body, [VM] * 6 + [SM] * 4,
-        (f32(rows, width), f32(HALO, width), f32(HALO, width), f32(5, tiles, height, LANES)),
-        [
-            pltpu.VMEM((tiles, height + 2 * PAD, LANES), F32),
-            pltpu.VMEM((tiles, height + 2 * PAD, LANES), F32),
-            pltpu.VMEM((tiles, height, LANES), F32),
-            pltpu.VMEM((tiles, height, LANES), F32),
-            pltpu.VMEM((tiles, height + 2 * PAD, LANES), F32),
-        ],
+        first_body, [VM] * 7 + [FAR] * 2,
+        (strip, f32(HALO, width), f32(HALO, width), f32(5, tiles, height, LANES)),
+        [grid, grid, flat, flat, flat, steps_near, pltpu.SMEM(waveform.shape, F32), pltpu.SemaphoreType.DMA((2,))],
         1 << 24,
-    )(point, node_rate, source_map, got_a, got_b, initial_state, cond_table, class_map, interval_steps, waveform)
+    )(point, rate, source, got_a, got_b, initial, own_blocks, far(interval_steps), far(waveform))
     relaxed = exchange(passed, 1, lambda s: s)
     edge_a = exchange(edge_a, 1, lambda s: side(s, "a"))
     edge_b = exchange(edge_b, 1, lambda s: side(s, "b"))
 
     change = call(
-        second_body, [VM] * 7 + [SM], f32(crows, width // 2),
-        [pltpu.VMEM((tiles, height + 2 * PAD, LANES), F32)] * 2 + [pltpu.VMEM((tiles, height, LANES), F32)],
+        second_body, [VM] * 7 + [FAR], f32(crows, width // 2),
+        [grid, grid, flat, steps_near, pltpu.SemaphoreType.DMA((1,))],
         1 << 24,
-    )(relaxed, edge_a, edge_b, point, got_a, got_b, weights, interval_steps)
-    changes = [change] + [exchange(change, 0, lambda s, k=k: s ^ k) for k in range(1, strips)]
+    )(relaxed, edge_a, edge_b, point, got_a, got_b, weights, far(interval_steps))
+    changes = [change]
+    for k in range(1, strips):
+        changes.append(exchange(change, 0, lambda s, k=k: s ^ k))
 
     def assemble(*refs):
         assemble_body(refs[:strips], refs[strips : 2 * strips], *refs[2 * strips :])
@@ -547,4 +597,5 @@
         P("space", None),
         P(),
     )
+
     return jax.shard_map(shards, mesh=mesh, in_specs=placed, out_specs=P("tm", "space", None), check_vma=False)

time: 65.7 us -> 56.2 us (0.86)
  local copies, waits for them, and re-layouts: 6.92 us -> 0.01 us
  Pallas kernels: 15.7 us -> 13.8 us
    unnamed x20 -> x2, local copies, waits for them, and re-layouts: 6.92 us -> 0.01 us
    pallas_call x3, Pallas kernels: 11.2 us -> 9.28 us  [the longest x1 4.03 us: shards(): call(second_body, [VM] * 7 + [FAR], f32(crows, width // 2), [grid, grid,...]
  transfers between devices with their start and end apart: 14 -> 14, of which waited for: 6 -> 6; matrix products, arithmetic and copies ran while one was open for 0% -> 0% of each run, Pallas kernels for 8% -> 7%
where the time goes in v4:
time: 56.2 us; the launch traced here: 56 us
  starting transfers between devices  22 us (39%)
  waiting for transfers between devices  20 us (36%)
  Pallas kernels  13.8 us (25%)
    ppermute x11, starting transfers between devices, exchange(): return lax.ppermute(value, both, pairs)  20.6 us
    ppermute x3, waiting for transfers between devices, shards(): lax.ppermute(total, 'tm', [(j, j ^ 1 << stage) for j in range(intervals)])  10.7 us
    ppermute x11, waiting for transfers between devices, exchange(): return lax.ppermute(value, both, pairs)  9.35 us
    pallas_call x1, Pallas kernels, shards(): call(second_body, [VM] * 7 + [FAR], f32(crows, width // 2), [grid, grid,...  4.03 us
    pallas_call x1, Pallas kernels, shards(): call(first_body, [VM] * 7 + [FAR] * 2, (strip, f32(HALO, width), f32(HALO...  3.76 us
    pallas_call x2, Pallas kernels, shards(): call(body, specs, (f32(ctiles, cheight, LANES), f32(ctiles, crows, LANES)...  2.76 us
    pallas_call x1, Pallas kernels, shards(): call(body, specs + [VM], f32(rows, width), buffers + [pltpu.VMEM((ctiles,...  1.57 us
    pallas_call x1, Pallas kernels, shards(): call(pack_body, [FAR] * 6, (f32(packed, width), f32(packed, width), f32(f...  1.49 us
  transfers between devices with their start and end apart: 14, of which 6 were waited for; matrix products, arithmetic and copies ran while one was open for 0% of the time, Pallas kernels for 7%

profile of v4, /device:TPU:0, one launch (start us, length us, event | category | flops | bytes accessed | tf_op | source)
XLA Modules:
  0.0 56.0 jit_solution(10843560740090651740)
XLA Ops:
  0.0 1.5 %shard_map.82 = (f32[64,1024]{1,0:T(8,128)S(1)}, f32[64,1024]{1,0:T(8,128)S(1)}, f32[24,512]{1,0:T(8,128)S(1)}, f32[8,1024]{1,0:T(8,128)S(1)}, f32[32,1024]{1,0:...) custom-call(f32[32,1024]{1,0:T(8,128)} %bitcast.2, f32[32,1024]{1,0:T(8,128)} %rate_far.1, ...), custom_call_target="tpu_custom_call" | custom-call | flops 1048576 | bytes 1048576 | tf_op jit(solution)/shard_map/pallas_call | solution.py:516
  1.5 3.1 %collective-permute-start = (f32[64,1024]{1,0:T(8,128)S(1)}, f32[64,1024]{1,0:T(8,128)S(1)}, u32[]{:S(2)}, u32[]{:S(2)}) collective-permute-start(f32[64,1024]{1,0:T(8,128)S(1)} %get-tuple-element.26), channel_id=1, source_target_pairs={{0,1},{1,0},{2,3},{3,2},{4,5},{5,4},{6,7},{7,6},{8,9},{9,8},{10,11... | collective-permute-start | bytes 786440 | tf_op jit(solution)/shard_map/ppermute | solution.py:513
  4.6 0.7 %collective-permute-start.1 = (f32[64,1024]{1,0:T(8,128)S(1)}, f32[64,1024]{1,0:T(8,128)S(1)}, u32[]{:S(2)}, u32[]{:S(2)}) collective-permute-start(f32[64,1024]{1,0:T(8,128)S(1)} %get-tuple-element.27), channel_id=1, source_target_pairs={{1,2},{2,1},{5,6},{6,5},{9,10},{10,9},{13,14},{14,13},{17,18},{18,... | collective-permute-start | bytes 786440 | tf_op jit(solution)/shard_map/ppermute | solution.py:513
  5.3 5.6 %collective-permute-done.got_a = f32[64,1024]{1,0:T(8,128)S(1)} collective-permute-done((f32[64,1024]{1,0:T(8,128)S(1)}, f32[64,1024]{1,0:T(8,128)S(1)}, u32[]{:S(2)}, u32[]{:S(2)}) %collective-permute-start) | collective-permute-done | bytes 262176 | tf_op jit(solution)/shard_map/ppermute | solution.py:513
  10.9 0.0 collective-permute-done.1.got_b
  10.9 3.8 %shard_map.83 = (f32[32,1024]{1,0:T(8,128)S(1)}, f32[24,1024]{1,0:T(8,128)S(1)}, f32[24,1024]{1,0:T(8,128)S(1)}, f32[5,8,80,128]{3,2,1,0:T(8,128)S(1)}) custom-call(f32[32,1024]{1,0:T(8,128)S(1)} %get-tuple-element.23.point, f32[32,1024]{1,0:T(8,128)S(1)} %get-tuple-element.24.rate, f32[32,1024]{1,0:T(8,128)S(1)} %get-tuple-element.25.source, ...), custom_call_target="tpu_custom_call" | custom-call | flops 16777216 | bytes 1048576 | tf_op jit(solution)/shard_map/pallas_call | solution.py:536
  14.7 0.0 copy-start
  14.7 0.1 collective-permute-start.2
  14.8 6.2 %collective-permute-start.3 = (f32[24,1024]{1,0:T(8,128)S(1)}, f32[24,1024]{1,0:T(8,128)S(1)}, u32[]{:S(2)}, u32[]{:S(2)}) collective-permute-start(f32[24,1024]{1,0:T(8,128)S(1)} %get-tuple-element.31), channel_id=1, source_target_pairs={{0,5},{1,4},{2,7},{3,6},{4,9},{5,8},{6,11},{7,10},{8,13},{9,12},{1... | collective-permute-start | bytes 294920 | tf_op jit(solution)/shard_map/ppermute | solution.py:513
  21.0 0.7 %collective-permute-start.4 = (f32[24,1024]{1,0:T(8,128)S(1)}, f32[24,1024]{1,0:T(8,128)S(1)}, u32[]{:S(2)}, u32[]{:S(2)}) collective-permute-start(f32[24,1024]{1,0:T(8,128)S(1)} %get-tuple-element.32), channel_id=1, source_target_pairs={{1,6},{2,5},{5,10},{6,9},{9,14},{10,13},{13,18},{14,17},{17,22},{1... | collective-permute-start | bytes 294920 | tf_op jit(solution)/shard_map/ppermute | solution.py:513
  21.7 2.7 %collective-permute-start.10 = (f32[24,512]{1,0:T(8,128)S(1)}, f32[24,512]{1,0:T(8,128)S(1)}, u32[]{:S(2)}, u32[]{:S(2)}) collective-permute-start(f32[24,512]{1,0:T(8,128)S(1)} %get-tuple-element.34.refs_4_), channel_id=1, source_target_pairs={{0,3},{1,2},{2,1},{3,0},{4,7},{5,6},{6,5},{7,4},{8,11},{9,10},{10,... | collective-permute-start | bytes 147464 | tf_op jit(solution)/shard_map/ppermute | solution.py:513
  24.4 0.6 %collective-permute-start.8 = (f32[24,512]{1,0:T(8,128)S(1)}, f32[24,512]{1,0:T(8,128)S(1)}, u32[]{:S(2)}, u32[]{:S(2)}) collective-permute-start(f32[24,512]{1,0:T(8,128)S(1)} %get-tuple-element.34.refs_4_), channel_id=1, source_target_pairs={{0,1},{1,0},{2,3},{3,2},{4,5},{5,4},{6,7},{7,6},{8,9},{9,8},{10,11... | collective-permute-start | bytes 147464 | tf_op jit(solution)/shard_map/ppermute | solution.py:513
  25.0 0.0 collective-permute-done.3.edge_a
  25.0 1.8 %collective-permute-start.9 = (f32[24,512]{1,0:T(8,128)S(1)}, f32[24,512]{1,0:T(8,128)S(1)}, u32[]{:S(2)}, u32[]{:S(2)}) collective-permute-start(f32[24,512]{1,0:T(8,128)S(1)} %get-tuple-element.34.refs_4_), channel_id=1, source_target_pairs={{0,2},{1,3},{2,0},{3,1},{4,6},{5,7},{6,4},{7,5},{8,10},{9,11},{10,... | collective-permute-start | bytes 147464 | tf_op jit(solution)/shard_map/ppermute | solution.py:513
  26.9 0.0 collective-permute-done.2.relaxed.refs_5_
  26.9 4.0 %shard_map.84.refs_0_ = f32[16,512]{1,0:T(8,128)S(1)} custom-call(f32[32,1024]{1,0:T(8,128)S(1)} %collective-permute-done.2.relaxed.refs_5_, f32[24,1024]{1,0:T(8,128)S(1)} %collective-permute-done.3.edge_a, f32[24,1024]{1,0:T(8,128)S(1)} %collective-permute-done.4.edge_b, f32[32,1024]{1,0:T(8,128)S(1)} %get-tuple-element.23.point, ...), custom_call_target="tpu_custom_call" | custom-call | flops 16777216 | bytes 1048576 | tf_op jit(solution)/shard_map/pallas_call | solution.py:546
  30.9 2.3 %collective-permute-start.5 = (f32[16,512]{1,0:T(8,128)S(1)}, f32[16,512]{1,0:T(8,128)S(1)}, u32[]{:S(2)}, u32[]{:S(2)}) collective-permute-start(f32[16,512]{1,0:T(8,128)S(1)} %shard_map.84.refs_0_), channel_id=1, source_target_pairs={{0,1},{1,0},{2,3},{3,2},{4,5},{5,4},{6,7},{7,6},{8,9},{9,8},{10,11... | collective-permute-start | bytes 98312 | tf_op jit(solution)/shard_map/ppermute | solution.py:513
  33.2 0.3 collective-permute-start.6
  33.5 2.1 %collective-permute-start.7 = (f32[16,512]{1,0:T(8,128)S(1)}, f32[16,512]{1,0:T(8,128)S(1)}, u32[]{:S(2)}, u32[]{:S(2)}) collective-permute-start(f32[16,512]{1,0:T(8,128)S(1)} %shard_map.84.refs_0_), channel_id=1, source_target_pairs={{0,3},{1,2},{2,1},{3,0},{4,7},{5,6},{6,5},{7,4},{8,11},{9,10},{10,... | collective-permute-start | bytes 98312 | tf_op jit(solution)/shard_map/ppermute | solution.py:513
  35.6 0.0 collective-permute-done.8.refs_5_
  35.6 3.2 %collective-permute-done.6.refs_2_ = f32[16,512]{1,0:T(8,128)S(1)} collective-permute-done((f32[16,512]{1,0:T(8,128)S(1)}, f32[16,512]{1,0:T(8,128)S(1)}, u32[]{:S(2)}, u32[]{:S(2)}) %collective-permute-start.6) | collective-permute-done | bytes 32800 | tf_op jit(solution)/shard_map/ppermute | solution.py:513
  38.8 0.5 collective-permute-done.7.refs_3_
  39.3 0.2 shard_map.85
  39.5 0.2 collective-permute-start.11
  39.8 1.2 %collective-permute-done.11.refs_1_ = f32[4,64,128]{2,1,0:T(8,128)S(1)} collective-permute-done((f32[4,64,128]{2,1,0:T(8,128)S(1)}, f32[4,64,128]{2,1,0:T(8,128)S(1)}, u32[]{:S(2)}, u32[]{:S(2)}) %collective-permute-start.11) | collective-permute-done | bytes 131104 | tf_op jit(solution)/shard_map/ppermute | solution.py:566
  41.0 1.1 %shard_map.86 = (f32[4,64,128]{2,1,0:T(8,128)S(1)}, f32[4,16,128]{2,1,0:T(8,128)S(1)}) custom-call(f32[4,64,128]{2,1,0:T(8,128)S(1)} %get-tuple-element.35.refs_0_, f32[4,64,128]{2,1,0:T(8,128)S(1)} %collective-permute-done.11.refs_1_, f32[5,4,64,128]{3,2,1,0:T(8,128)S(1)} %get-tuple-element.36.refs_2_.refs_3_, s32[8]{0:T(128)S(1)} %copy-done), custom_call_target="tpu_custom_call" | custom-call | flops 8388608 | bytes 1048576 | tf_op jit(solution)/shard_map/pallas_call | solution.py:583
  42.1 1.1 %collective-permute-start.12 = (f32[4,64,128]{2,1,0:T(8,128)S(1)}, f32[4,64,128]{2,1,0:T(8,128)S(1)}, u32[]{:S(2)}, u32[]{:S(2)}) collective-permute-start(f32[4,64,128]{2,1,0:T(8,128)S(1)} %get-tuple-element.37.refs_0_), channel_id=1, source_target_pairs={{0,8},{4,12},{8,0},{12,4},{16,24},{20,28},{24,16},{28,20},{1,9},{5... | collective-permute-start | bytes 393224 | tf_op jit(solution)/shard_map/ppermute | solution.py:566
  43.2 4.5 %collective-permute-done.12.refs_1_ = f32[4,64,128]{2,1,0:T(8,128)S(1)} collective-permute-done((f32[4,64,128]{2,1,0:T(8,128)S(1)}, f32[4,64,128]{2,1,0:T(8,128)S(1)}, u32[]{:S(2)}, u32[]{:S(2)}) %collective-permute-start.12) | collective-permute-done | bytes 131104 | tf_op jit(solution)/shard_map/ppermute | solution.py:566
  47.7 1.6 %shard_map.87 = (f32[4,64,128]{2,1,0:T(8,128)S(1)}, f32[4,16,128]{2,1,0:T(8,128)S(1)}) custom-call(f32[4,64,128]{2,1,0:T(8,128)S(1)} %get-tuple-element.37.refs_0_, f32[4,64,128]{2,1,0:T(8,128)S(1)} %collective-permute-done.12.refs_1_, f32[4,16,128]{2,1,0:T(8,128)S(1)} %get-tuple-element.38.refs_2_, f32[5,4,64,128]{3,2,1,0:T(8,128)S(1)} %get-tuple-element.36.refs_2_.refs_3_, ...), custom_call_target="tpu_custom_call" | custom-call | flops 8388608 | bytes 1048576 | tf_op jit(solution)/shard_map/pallas_call | solution.py:583
  49.4 0.1 collective-permute-start.13
  49.4 5.0 %collective-permute-done.13.refs_1_ = f32[4,64,128]{2,1,0:T(8,128)S(1)} collective-permute-done((f32[4,64,128]{2,1,0:T(8,128)S(1)}, f32[4,64,128]{2,1,0:T(8,128)S(1)}, u32[]{:S(2)}, u32[]{:S(2)}) %collective-permute-start.13) | collective-permute-done | bytes 131104 | tf_op jit(solution)/shard_map/ppermute | solution.py:566
  54.4 1.6 %shard_map.88 = f32[32,1024]{1,0:T(8,128)} custom-call(f32[4,64,128]{2,1,0:T(8,128)S(1)} %get-tuple-element.39.refs_0_, f32[4,64,128]{2,1,0:T(8,128)S(1)} %collective-permute-done.13.refs_1_, f32[4,16,128]{2,1,0:T(8,128)S(1)} %get-tuple-element.40.refs_2_, f32[5,4,64,128]{3,2,1,0:T(8,128)S(1)} %get-tuple-element.36.refs_2_.refs_3_, s32[8]{0:T(128)S(1)} %copy-done, ...), custom_call_target="tpu_custom_call" | custom-call | flops 8388608 | bytes 1048576 | tf_op jit(solution)/shard_map/pallas_call | solution.py:578
  (5 shorter events, 0.0 us)
Async XLA Ops:
  1.5 9.4 %collective-permute-start = (f32[64,1024]{1,0:T(8,128)S(1)}, f32[64,1024]{1,0:T(8,128)S(1)}, u32[]{:S(2)}, u32[]{:S(2)}) collective-permute-start(f32[64,1024]{1,0:T(8,128)S(1)} %get-tuple-element.26), channel_id=1, source_target_pairs={{0,1},{1,0},{2,3},{3,2},{4,5},{5,4},{6,7},{7,6},{8,9},{9,8},{10,11... | collective-permute-start | bytes 786440 | tf_op jit(solution)/shard_map/ppermute | solution.py:513
  4.6 6.3 %collective-permute-start.1 = (f32[64,1024]{1,0:T(8,128)S(1)}, f32[64,1024]{1,0:T(8,128)S(1)}, u32[]{:S(2)}, u32[]{:S(2)}) collective-permute-start(f32[64,1024]{1,0:T(8,128)S(1)} %get-tuple-element.27), channel_id=1, source_target_pairs={{1,2},{2,1},{5,6},{6,5},{9,10},{10,9},{13,14},{14,13},{17,18},{18,... | collective-permute-start | bytes 786440 | tf_op jit(solution)/shard_map/ppermute | solution.py:513
  14.7 26.3 %copy-start = (s32[8]{0:T(128)S(1)}, s32[8]{0:T(128)}, u32[]{:S(2)}) copy-start(s32[8]{0:T(128)} %refs_4_.3) | copy-start | bytes 100
  14.7 12.2 %collective-permute-start.2 = (f32[32,1024]{1,0:T(8,128)S(1)}, f32[32,1024]{1,0:T(8,128)S(1)}, u32[]{:S(2)}, u32[]{:S(2)}) collective-permute-start(f32[32,1024]{1,0:T(8,128)S(1)} %get-tuple-element.30), channel_id=1, source_target_pairs={{0,4},{1,5},{2,6},{3,7},{4,8},{5,9},{6,10},{7,11},{8,12},{9,13},{1... | collective-permute-start | bytes 393224 | tf_op jit(solution)/shard_map/ppermute | solution.py:513
  14.8 10.2 %collective-permute-start.3 = (f32[24,1024]{1,0:T(8,128)S(1)}, f32[24,1024]{1,0:T(8,128)S(1)}, u32[]{:S(2)}, u32[]{:S(2)}) collective-permute-start(f32[24,1024]{1,0:T(8,128)S(1)} %get-tuple-element.31), channel_id=1, source_target_pairs={{0,5},{1,4},{2,7},{3,6},{4,9},{5,8},{6,11},{7,10},{8,13},{9,12},{1... | collective-permute-start | bytes 294920 | tf_op jit(solution)/shard_map/ppermute | solution.py:513
  21.0 5.8 %collective-permute-start.4 = (f32[24,1024]{1,0:T(8,128)S(1)}, f32[24,1024]{1,0:T(8,128)S(1)}, u32[]{:S(2)}, u32[]{:S(2)}) collective-permute-start(f32[24,1024]{1,0:T(8,128)S(1)} %get-tuple-element.32), channel_id=1, source_target_pairs={{1,6},{2,5},{5,10},{6,9},{9,14},{10,13},{13,18},{14,17},{17,22},{1... | collective-permute-start | bytes 294920 | tf_op jit(solution)/shard_map/ppermute | solution.py:513
  21.7 11.8 %collective-permute-start.10 = (f32[24,512]{1,0:T(8,128)S(1)}, f32[24,512]{1,0:T(8,128)S(1)}, u32[]{:S(2)}, u32[]{:S(2)}) collective-permute-start(f32[24,512]{1,0:T(8,128)S(1)} %get-tuple-element.34.refs_4_), channel_id=1, source_target_pairs={{0,3},{1,2},{2,1},{3,0},{4,7},{5,6},{6,5},{7,4},{8,11},{9,10},{10,... | collective-permute-start | bytes 147464 | tf_op jit(solution)/shard_map/ppermute | solution.py:513
  24.4 11.2 %collective-permute-start.8 = (f32[24,512]{1,0:T(8,128)S(1)}, f32[24,512]{1,0:T(8,128)S(1)}, u32[]{:S(2)}, u32[]{:S(2)}) collective-permute-start(f32[24,512]{1,0:T(8,128)S(1)} %get-tuple-element.34.refs_4_), channel_id=1, source_target_pairs={{0,1},{1,0},{2,3},{3,2},{4,5},{5,4},{6,7},{7,6},{8,9},{9,8},{10,11... | collective-permute-start | bytes 147464 | tf_op jit(solution)/shard_map/ppermute | solution.py:513
  25.0 10.6 %collective-permute-start.9 = (f32[24,512]{1,0:T(8,128)S(1)}, f32[24,512]{1,0:T(8,128)S(1)}, u32[]{:S(2)}, u32[]{:S(2)}) collective-permute-start(f32[24,512]{1,0:T(8,128)S(1)} %get-tuple-element.34.refs_4_), channel_id=1, source_target_pairs={{0,2},{1,3},{2,0},{3,1},{4,6},{5,7},{6,4},{7,5},{8,10},{9,11},{10,... | collective-permute-start | bytes 147464 | tf_op jit(solution)/shard_map/ppermute | solution.py:513
  30.9 4.7 %collective-permute-start.5 = (f32[16,512]{1,0:T(8,128)S(1)}, f32[16,512]{1,0:T(8,128)S(1)}, u32[]{:S(2)}, u32[]{:S(2)}) collective-permute-start(f32[16,512]{1,0:T(8,128)S(1)} %shard_map.84.refs_0_), channel_id=1, source_target_pairs={{0,1},{1,0},{2,3},{3,2},{4,5},{5,4},{6,7},{7,6},{8,9},{9,8},{10,11... | collective-permute-start | bytes 98312 | tf_op jit(solution)/shard_map/ppermute | solution.py:513
  33.2 5.6 %collective-permute-start.6 = (f32[16,512]{1,0:T(8,128)S(1)}, f32[16,512]{1,0:T(8,128)S(1)}, u32[]{:S(2)}, u32[]{:S(2)}) collective-permute-start(f32[16,512]{1,0:T(8,128)S(1)} %shard_map.84.refs_0_), channel_id=1, source_target_pairs={{0,2},{1,3},{2,0},{3,1},{4,6},{5,7},{6,4},{7,5},{8,10},{9,11},{10,... | collective-permute-start | bytes 98312 | tf_op jit(solution)/shard_map/ppermute | solution.py:513
  33.5 5.8 %collective-permute-start.7 = (f32[16,512]{1,0:T(8,128)S(1)}, f32[16,512]{1,0:T(8,128)S(1)}, u32[]{:S(2)}, u32[]{:S(2)}) collective-permute-start(f32[16,512]{1,0:T(8,128)S(1)} %shard_map.84.refs_0_), channel_id=1, source_target_pairs={{0,3},{1,2},{2,1},{3,0},{4,7},{5,6},{6,5},{7,4},{8,11},{9,10},{10,... | collective-permute-start | bytes 98312 | tf_op jit(solution)/shard_map/ppermute | solution.py:513
  39.5 1.4 %collective-permute-start.11 = (f32[4,64,128]{2,1,0:T(8,128)S(1)}, f32[4,64,128]{2,1,0:T(8,128)S(1)}, u32[]{:S(2)}, u32[]{:S(2)}) collective-permute-start(f32[4,64,128]{2,1,0:T(8,128)S(1)} %get-tuple-element.35.refs_0_), channel_id=1, source_target_pairs={{0,4},{4,0},{8,12},{12,8},{16,20},{20,16},{24,28},{28,24},{1,5},{5... | collective-permute-start | bytes 393224 | tf_op jit(solution)/shard_map/ppermute | solution.py:566
  42.1 5.6 %collective-permute-start.12 = (f32[4,64,128]{2,1,0:T(8,128)S(1)}, f32[4,64,128]{2,1,0:T(8,128)S(1)}, u32[]{:S(2)}, u32[]{:S(2)}) collective-permute-start(f32[4,64,128]{2,1,0:T(8,128)S(1)} %get-tuple-element.37.refs_0_), channel_id=1, source_target_pairs={{0,8},{4,12},{8,0},{12,4},{16,24},{20,28},{24,16},{28,20},{1,9},{5... | collective-permute-start | bytes 393224 | tf_op jit(solution)/shard_map/ppermute | solution.py:566
  49.4 5.0 %collective-permute-start.13 = (f32[4,64,128]{2,1,0:T(8,128)S(1)}, f32[4,64,128]{2,1,0:T(8,128)S(1)}, u32[]{:S(2)}, u32[]{:S(2)}) collective-permute-start(f32[4,64,128]{2,1,0:T(8,128)S(1)} %get-tuple-element.39.refs_0_), channel_id=1, source_target_pairs={{0,16},{4,20},{8,24},{12,28},{16,0},{20,4},{24,8},{28,12},{1,17},{... | collective-permute-start | bytes 393224 | tf_op jit(solution)/shard_map/ppermute | solution.py:566

commit v5 on v4

--- a/solution.py
+++ b/solution.py
@@ -19,7 +19,6 @@
 HT = HALO // SUB
 PAD = SUB
 VM = pl.BlockSpec(memory_space=pltpu.VMEM)
-SM = pl.BlockSpec(memory_space=pltpu.SMEM)
 FAR = pl.BlockSpec(memory_space=pltpu.HBM)
 F32 = jnp.float32
 GRANT = 16 << 20
@@ -141,9 +140,10 @@
     pairs = halve()
     for c in range(tiles // 2):
         wide = jnp.concatenate([row_pairs(tmp, (2 * c + k,), 0, rows // 2) for k in (0, 1)], axis=1)
-        coarse[: rows // 2, cols(c)] = 0.25 * dot(wide, pairs)
+        coarse[c * (rows // 2) : (c + 1) * (rows // 2), :] = 0.25 * dot(wide, pairs)
         halves = [blocks_out[0:blocks, cols(2 * c + k)] for k in (0, 1)]
-        coarse[rows // 2 : rows // 2 + blocks, cols(c)] = jnp.where(
+        at = tiles // 2 * (rows // 2) + c * blocks
+        coarse[at : at + blocks, :] = jnp.where(
             iota(1, (blocks, LANES)) < LANES // 2, halves[0], halves[1]
         )
     copies[5].wait()
@@ -209,7 +209,7 @@
 
 def first_body(
     point, rate, source, got_a, got_b, initial, own_blocks, steps_far, waveform_far,
-    relaxed, edge_a, edge_b, weights, state, spare, force, rates, conduct, steps, waveform, sems,
+    relaxed, edge_a, edge_b, weights, factors, state, spare, force, rates, conduct, steps, waveform, sems,
 ):
     copies = fetch(((steps_far, steps), (waveform_far, waveform)), sems)
     rows, width = point.shape
@@ -273,6 +273,9 @@
         copy.wait()
     start = lax.fori_loop(0, mine, lambda i, total: total + steps[i], jnp.int32(0))
     count = steps[mine]
+    for i in range(steps.shape[0]):
+        value = steps[i].astype(F32) * (1.0 / (4.0 * CSUB))
+        factors[i : i + 1, :] = jnp.full((1, LANES), value, F32)
     sweep(state, spare, weights, force, count, tiles, strip_tiles, lambda t: waveform[start + t])
 
     def give(read):
@@ -356,9 +359,9 @@
             for r in range(rows // SUB):
                 to = pl.multiple_of(base + r * SUB, SUB)
                 total[c, pl.ds(to, SUB), :] = strips[k][r * SUB : (r + 1) * SUB, cols(c)]
-                weights[0, c, pl.ds(to, SUB), :] = fields[k][r * SUB : (r + 1) * SUB, cols(c)]
-                block = rows + r * (SUB // per_block)
-                two = [jnp.broadcast_to(fields[k][block + i : block + i + 1, cols(c)], (SUB, LANES)) for i in (0, 1)]
+                weights[0, c, pl.ds(to, SUB), :] = fields[k][c * rows + r * SUB : c * rows + (r + 1) * SUB, :]
+                block = tiles * rows + c * (rows // per_block) + r * (SUB // per_block)
+                two = [jnp.broadcast_to(fields[k][block + i : block + i + 1, :], (SUB, LANES)) for i in (0, 1)]
                 conduct[c, pl.ds(PAD + to, SUB), :] = jnp.where(iota(0) < per_block, two[0], two[1])
     for r in range(count * rows // SUB):
         at = PAD + r * SUB
@@ -398,7 +401,7 @@
 
 
 def scan_body(stage, final, refs):
-    total, got, before, weights, steps = refs[:5]
+    total, got, before, weights, factors = refs[:5]
     tiles, height, _ = total.shape
     size = 1 << stage
     mine, strip = lax.axis_index("tm"), lax.axis_index("space")
@@ -450,7 +453,7 @@
         def _():
             keep()
 
-        link(buffers, weights, steps[first + i].astype(F32) * (1.0 / (4.0 * CSUB)))
+        link(buffers, weights, jnp.broadcast_to(factors[pl.ds(first + i, 1), :], (SUB, LANES)))
 
     if final:
         turns = jnp.where(upper, mine - first, 0)
@@ -496,7 +499,7 @@
     tiles, ctiles, crows, blocks = width // LANES, width // LANES // 2, rows // 2, rows // BLK_R
     height, cheight = rows + 2 * HALO, crows * strips
     packed = -(-(3 * STEP_MOST + HT) // SUB) * SUB
-    fields_rows = -(-(crows + blocks) // SUB) * SUB
+    fields_rows = -(-ctiles * (crows + blocks) // SUB) * SUB
     both = ("tm", "space")
 
     def side(s, which):
@@ -515,7 +518,7 @@
     strip = f32(rows, width)
     pay_a, pay_b, field, own_blocks, point, rate, source, initial = call(
         pack_body, [FAR] * 6,
-        (f32(packed, width), f32(packed, width), f32(fields_rows, width // 2), f32(SUB, width), strip, strip, strip, strip),
+        (f32(packed, width), f32(packed, width), f32(fields_rows, LANES), f32(SUB, width), strip, strip, strip, strip),
         [
             pltpu.SMEM(cond_table.shape, F32),
             pltpu.SMEM(class_map.shape, jnp.int32),
@@ -533,9 +536,9 @@
     grid = pltpu.VMEM((tiles, height + 2 * PAD, LANES), F32)
     flat = pltpu.VMEM((tiles, height, LANES), F32)
     steps_near = pltpu.SMEM(interval_steps.shape, jnp.int32)
-    passed, edge_a, edge_b, weights = call(
+    passed, edge_a, edge_b, weights, factors = call(
         first_body, [VM] * 7 + [FAR] * 2,
-        (strip, f32(HALO, width), f32(HALO, width), f32(5, tiles, height, LANES)),
+        (strip, f32(HALO, width), f32(HALO, width), f32(5, tiles, height, LANES), f32(-(-intervals // SUB) * SUB, LANES)),
         [grid, grid, flat, flat, flat, steps_near, pltpu.SMEM(waveform.shape, F32), pltpu.SemaphoreType.DMA((2,))],
         1 << 24,
     )(point, rate, source, got_a, got_b, initial, own_blocks, far(interval_steps), far(waveform))
@@ -572,8 +575,8 @@
             scan_body(stage, final, refs)
 
         buffers = [pltpu.VMEM((ctiles, cheight + 2 * PAD, LANES), F32)] * 3
-        lead = [total, got] + ([errors] if some else []) + [coarse_weights, interval_steps]
-        specs = [VM] * (len(lead) - 1) + [SM]
+        lead = [total, got] + ([errors] if some else []) + [coarse_weights, factors]
+        specs = [VM] * len(lead)
         if final:
             out = call(
                 body, specs + [VM], f32(rows, width),

time: 56.2 us -> 56.6 us (level)
    pallas_call x2, Pallas kernels: 2.76 us -> 1.65 us  [shards(): call(body, specs, (f32(ctiles, cheight, LANES), f32(ctiles, crows, LANES)...]
    pallas_call x1, Pallas kernels: 3.76 us -> 4.81 us  [shards(): call(first_body, [VM] * 7 + [FAR] * 2, (strip, f32(HALO, width), f32(HALO...]
    pallas_call x1, Pallas kernels: 4.03 us -> 5 us  [shards(): call(second_body, [VM] * 7 + [FAR], f32(crows, width // 2), [grid, grid,...]
  transfers between devices with their start and end apart: 14 -> 14, of which waited for: 6 -> 6; matrix products, arithmetic and copies ran while one was open for 0% -> 0% of each run, Pallas kernels for 7% -> 9%
where the time goes in v5:
time: 56.6 us; the launch traced here: 56.4 us
  starting transfers between devices  21.9 us (39%)
  waiting for transfers between devices  20.2 us (36%)
  Pallas kernels  14.2 us (25%)
    ppermute x11, starting transfers between devices, exchange(): return lax.ppermute(value, both, pairs)  20.4 us
    ppermute x3, waiting for transfers between devices, shards(): lax.ppermute(total, 'tm', [(j, j ^ 1 << stage) for j in range(intervals)])  10.6 us
    ppermute x11, waiting for transfers between devices, exchange(): return lax.ppermute(value, both, pairs)  9.62 us
    pallas_call x1, Pallas kernels, shards(): call(second_body, [VM] * 7 + [FAR], f32(crows, width // 2), [grid, grid,...  5 us
    pallas_call x1, Pallas kernels, shards(): call(first_body, [VM] * 7 + [FAR] * 2, (strip, f32(HALO, width), f32(HALO...  4.81 us
    pallas_call x2, Pallas kernels, shards(): call(body, specs, (f32(ctiles, cheight, LANES), f32(ctiles, crows, LANES)...  1.65 us
    ppermute x3, starting transfers between devices, shards(): lax.ppermute(total, 'tm', [(j, j ^ 1 << stage) for j in range(intervals)])  1.5 us
    pallas_call x1, Pallas kernels, shards(): call(pack_body, [FAR] * 6, (f32(packed, width), f32(packed, width), f32(f...  1.49 us
  transfers between devices with their start and end apart: 14, of which 6 were waited for; matrix products, arithmetic and copies ran while one was open for 0% of the time, Pallas kernels for 9%

profile of v5, /device:TPU:0, one launch (start us, length us, event | category | flops | bytes accessed | tf_op | source)
XLA Modules:
  0.0 56.4 jit_solution(2158184605396963674)
XLA Ops:
  0.0 1.5 %shard_map.82 = (f32[64,1024]{1,0:T(8,128)S(1)}, f32[64,1024]{1,0:T(8,128)S(1)}, f32[80,128]{1,0:T(8,128)S(1)}, f32[8,1024]{1,0:T(8,128)S(1)}, f32[32,1024]{1,0:...) custom-call(f32[32,1024]{1,0:T(8,128)} %bitcast.2, f32[32,1024]{1,0:T(8,128)} %rate_far.1, ...), custom_call_target="tpu_custom_call" | custom-call | flops 1048576 | bytes 1048576 | tf_op jit(solution)/shard_map/pallas_call | solution.py:519
  1.5 3.1 %collective-permute-start = (f32[64,1024]{1,0:T(8,128)S(1)}, f32[64,1024]{1,0:T(8,128)S(1)}, u32[]{:S(2)}, u32[]{:S(2)}) collective-permute-start(f32[64,1024]{1,0:T(8,128)S(1)} %get-tuple-element.27), channel_id=1, source_target_pairs={{0,1},{1,0},{2,3},{3,2},{4,5},{5,4},{6,7},{7,6},{8,9},{9,8},{10,11... | collective-permute-start | bytes 786440 | tf_op jit(solution)/shard_map/ppermute | solution.py:516
  4.6 0.7 %collective-permute-start.1 = (f32[64,1024]{1,0:T(8,128)S(1)}, f32[64,1024]{1,0:T(8,128)S(1)}, u32[]{:S(2)}, u32[]{:S(2)}) collective-permute-start(f32[64,1024]{1,0:T(8,128)S(1)} %get-tuple-element.28), channel_id=1, source_target_pairs={{1,2},{2,1},{5,6},{6,5},{9,10},{10,9},{13,14},{14,13},{17,18},{18,... | collective-permute-start | bytes 786440 | tf_op jit(solution)/shard_map/ppermute | solution.py:516
  5.3 5.6 %collective-permute-done.got_a = f32[64,1024]{1,0:T(8,128)S(1)} collective-permute-done((f32[64,1024]{1,0:T(8,128)S(1)}, f32[64,1024]{1,0:T(8,128)S(1)}, u32[]{:S(2)}, u32[]{:S(2)}) %collective-permute-start) | collective-permute-done | bytes 262176 | tf_op jit(solution)/shard_map/ppermute | solution.py:516
  10.9 0.0 collective-permute-done.1.got_b
  10.9 4.8 %shard_map.83 = (f32[32,1024]{1,0:T(8,128)S(1)}, f32[24,1024]{1,0:T(8,128)S(1)}, f32[24,1024]{1,0:T(8,128)S(1)}, f32[5,8,80,128]{3,2,1,0:T(8,128)S(1)}, f32[8,128]{1,0:T(8,128)S(1)}) custom-call(f32[32,1024]{1,0:T(8,128)S(1)} %get-tuple-element.24.point, f32[32,1024]{1,0:T(8,128)S(1)} %get-tuple-element.25.rate, f32[32,1024]{1,0:T(8,128)S(1)} %get-tuple-element.26.source, ...), custom_call_target="tpu_custom_call" | custom-call | flops 16777216 | bytes 1048576 | tf_op jit(solution)/shard_map/pallas_call | solution.py:539
  15.7 0.1 collective-permute-start.2
  15.8 6.4 %collective-permute-start.3 = (f32[24,1024]{1,0:T(8,128)S(1)}, f32[24,1024]{1,0:T(8,128)S(1)}, u32[]{:S(2)}, u32[]{:S(2)}) collective-permute-start(f32[24,1024]{1,0:T(8,128)S(1)} %get-tuple-element.32), channel_id=1, source_target_pairs={{0,5},{1,4},{2,7},{3,6},{4,9},{5,8},{6,11},{7,10},{8,13},{9,12},{1... | collective-permute-start | bytes 294920 | tf_op jit(solution)/shard_map/ppermute | solution.py:516
  22.2 0.7 %collective-permute-start.4 = (f32[24,1024]{1,0:T(8,128)S(1)}, f32[24,1024]{1,0:T(8,128)S(1)}, u32[]{:S(2)}, u32[]{:S(2)}) collective-permute-start(f32[24,1024]{1,0:T(8,128)S(1)} %get-tuple-element.33), channel_id=1, source_target_pairs={{1,6},{2,5},{5,10},{6,9},{9,14},{10,13},{13,18},{14,17},{17,22},{1... | collective-permute-start | bytes 294920 | tf_op jit(solution)/shard_map/ppermute | solution.py:516
  22.9 2.7 %collective-permute-start.10 = (f32[80,128]{1,0:T(8,128)S(1)}, f32[80,128]{1,0:T(8,128)S(1)}, u32[]{:S(2)}, u32[]{:S(2)}) collective-permute-start(f32[80,128]{1,0:T(8,128)S(1)} %get-tuple-element.35.refs_4_), channel_id=1, source_target_pairs={{0,3},{1,2},{2,1},{3,0},{4,7},{5,6},{6,5},{7,4},{8,11},{9,10},{10,... | collective-permute-start | bytes 122888 | tf_op jit(solution)/shard_map/ppermute | solution.py:516
  25.6 0.6 %collective-permute-start.8 = (f32[80,128]{1,0:T(8,128)S(1)}, f32[80,128]{1,0:T(8,128)S(1)}, u32[]{:S(2)}, u32[]{:S(2)}) collective-permute-start(f32[80,128]{1,0:T(8,128)S(1)} %get-tuple-element.35.refs_4_), channel_id=1, source_target_pairs={{0,1},{1,0},{2,3},{3,2},{4,5},{5,4},{6,7},{7,6},{8,9},{9,8},{10,11... | collective-permute-start | bytes 122888 | tf_op jit(solution)/shard_map/ppermute | solution.py:516
  26.2 0.0 collective-permute-done.3.edge_a
  26.2 1.7 %collective-permute-start.9 = (f32[80,128]{1,0:T(8,128)S(1)}, f32[80,128]{1,0:T(8,128)S(1)}, u32[]{:S(2)}, u32[]{:S(2)}) collective-permute-start(f32[80,128]{1,0:T(8,128)S(1)} %get-tuple-element.35.refs_4_), channel_id=1, source_target_pairs={{0,2},{1,3},{2,0},{3,1},{4,6},{5,7},{6,4},{7,5},{8,10},{9,11},{10,... | collective-permute-start | bytes 122888 | tf_op jit(solution)/shard_map/ppermute | solution.py:516
  27.9 0.0 collective-permute-done.4.edge_b
  27.9 0.0 collective-permute-done.2.relaxed.refs_5_
  27.9 5.0 %shard_map.84.refs_0_ = f32[16,512]{1,0:T(8,128)S(1)} custom-call(f32[32,1024]{1,0:T(8,128)S(1)} %collective-permute-done.2.relaxed.refs_5_, f32[24,1024]{1,0:T(8,128)S(1)} %collective-permute-done.3.edge_a, f32[24,1024]{1,0:T(8,128)S(1)} %collective-permute-done.4.edge_b, f32[32,1024]{1,0:T(8,128)S(1)} %get-tuple-element.24.point, ...), custom_call_target="tpu_custom_call" | custom-call | flops 16777216 | bytes 1048576 | tf_op jit(solution)/shard_map/pallas_call | solution.py:549
  32.9 2.1 %collective-permute-start.5 = (f32[16,512]{1,0:T(8,128)S(1)}, f32[16,512]{1,0:T(8,128)S(1)}, u32[]{:S(2)}, u32[]{:S(2)}) collective-permute-start(f32[16,512]{1,0:T(8,128)S(1)} %shard_map.84.refs_0_), channel_id=1, source_target_pairs={{0,1},{1,0},{2,3},{3,2},{4,5},{5,4},{6,7},{7,6},{8,9},{9,8},{10,11... | collective-permute-start | bytes 98312 | tf_op jit(solution)/shard_map/ppermute | solution.py:516
  35.0 0.6 %collective-permute-start.6 = (f32[16,512]{1,0:T(8,128)S(1)}, f32[16,512]{1,0:T(8,128)S(1)}, u32[]{:S(2)}, u32[]{:S(2)}) collective-permute-start(f32[16,512]{1,0:T(8,128)S(1)} %shard_map.84.refs_0_), channel_id=1, source_target_pairs={{0,2},{1,3},{2,0},{3,1},{4,6},{5,7},{6,4},{7,5},{8,10},{9,11},{10,... | collective-permute-start | bytes 98312 | tf_op jit(solution)/shard_map/ppermute | solution.py:516
  35.6 0.0 collective-permute-done.10.refs_7_
  35.6 1.8 %collective-permute-start.7 = (f32[16,512]{1,0:T(8,128)S(1)}, f32[16,512]{1,0:T(8,128)S(1)}, u32[]{:S(2)}, u32[]{:S(2)}) collective-permute-start(f32[16,512]{1,0:T(8,128)S(1)} %shard_map.84.refs_0_), channel_id=1, source_target_pairs={{0,3},{1,2},{2,1},{3,0},{4,7},{5,6},{6,5},{7,4},{8,11},{9,10},{10,... | collective-permute-start | bytes 98312 | tf_op jit(solution)/shard_map/ppermute | solution.py:516
  37.4 3.0 %collective-permute-done.6.refs_2_ = f32[16,512]{1,0:T(8,128)S(1)} collective-permute-done((f32[16,512]{1,0:T(8,128)S(1)}, f32[16,512]{1,0:T(8,128)S(1)}, u32[]{:S(2)}, u32[]{:S(2)}) %collective-permute-start.6) | collective-permute-done | bytes 32800 | tf_op jit(solution)/shard_map/ppermute | solution.py:516
  40.4 1.0 %collective-permute-done.7.refs_3_ = f32[16,512]{1,0:T(8,128)S(1)} collective-permute-done((f32[16,512]{1,0:T(8,128)S(1)}, f32[16,512]{1,0:T(8,128)S(1)}, u32[]{:S(2)}, u32[]{:S(2)}) %collective-permute-start.7) | collective-permute-done | bytes 32800 | tf_op jit(solution)/shard_map/ppermute | solution.py:516
  41.4 0.2 shard_map.85
  41.6 0.2 collective-permute-start.11
  41.9 1.2 %collective-permute-done.11.refs_1_ = f32[4,64,128]{2,1,0:T(8,128)S(1)} collective-permute-done((f32[4,64,128]{2,1,0:T(8,128)S(1)}, f32[4,64,128]{2,1,0:T(8,128)S(1)}, u32[]{:S(2)}, u32[]{:S(2)}) %collective-permute-start.11) | collective-permute-done | bytes 131104 | tf_op jit(solution)/shard_map/ppermute | solution.py:569
  43.1 0.6 shard_map.86
  43.6 1.2 %collective-permute-start.12 = (f32[4,64,128]{2,1,0:T(8,128)S(1)}, f32[4,64,128]{2,1,0:T(8,128)S(1)}, u32[]{:S(2)}, u32[]{:S(2)}) collective-permute-start(f32[4,64,128]{2,1,0:T(8,128)S(1)} %get-tuple-element.39.refs_0_), channel_id=1, source_target_pairs={{0,8},{4,12},{8,0},{12,4},{16,24},{20,28},{24,16},{28,20},{1,9},{5... | collective-permute-start | bytes 393224 | tf_op jit(solution)/shard_map/ppermute | solution.py:569
  44.8 4.4 %collective-permute-done.12.refs_1_ = f32[4,64,128]{2,1,0:T(8,128)S(1)} collective-permute-done((f32[4,64,128]{2,1,0:T(8,128)S(1)}, f32[4,64,128]{2,1,0:T(8,128)S(1)}, u32[]{:S(2)}, u32[]{:S(2)}) %collective-permute-start.12) | collective-permute-done | bytes 131104 | tf_op jit(solution)/shard_map/ppermute | solution.py:569
  49.3 1.1 %shard_map.87 = (f32[4,64,128]{2,1,0:T(8,128)S(1)}, f32[4,16,128]{2,1,0:T(8,128)S(1)}) custom-call(f32[4,64,128]{2,1,0:T(8,128)S(1)} %get-tuple-element.39.refs_0_, f32[4,64,128]{2,1,0:T(8,128)S(1)} %collective-permute-done.12.refs_1_, f32[4,16,128]{2,1,0:T(8,128)S(1)} %get-tuple-element.40.refs_2_, f32[5,4,64,128]{3,2,1,0:T(8,128)S(1)} %get-tuple-element.37.refs_2_.refs_3_, ...), custom_call_target="tpu_custom_call" | custom-call | flops 8388608 | bytes 1048576 | tf_op jit(solution)/shard_map/pallas_call | solution.py:586
  50.4 0.1 collective-permute-start.13
  50.4 5.0 %collective-permute-done.13.refs_1_ = f32[4,64,128]{2,1,0:T(8,128)S(1)} collective-permute-done((f32[4,64,128]{2,1,0:T(8,128)S(1)}, f32[4,64,128]{2,1,0:T(8,128)S(1)}, u32[]{:S(2)}, u32[]{:S(2)}) %collective-permute-start.13) | collective-permute-done | bytes 131104 | tf_op jit(solution)/shard_map/ppermute | solution.py:569
  55.4 1.0 %shard_map.88 = f32[32,1024]{1,0:T(8,128)} custom-call(f32[4,64,128]{2,1,0:T(8,128)S(1)} %get-tuple-element.41.refs_0_, f32[4,64,128]{2,1,0:T(8,128)S(1)} %collective-permute-done.13.refs_1_, f32[4,16,128]{2,1,0:T(8,128)S(1)} %get-tuple-element.42.refs_2_, f32[5,4,64,128]{3,2,1,0:T(8,128)S(1)} %get-tuple-element.37.refs_2_.refs_3_, ...), custom_call_target="tpu_custom_call" | custom-call | flops 8388608 | bytes 1048576 | tf_op jit(solution)/shard_map/pallas_call | solution.py:581
  (3 shorter events, 0.0 us)
Async XLA Ops:
  1.5 9.4 %collective-permute-start = (f32[64,1024]{1,0:T(8,128)S(1)}, f32[64,1024]{1,0:T(8,128)S(1)}, u32[]{:S(2)}, u32[]{:S(2)}) collective-permute-start(f32[64,1024]{1,0:T(8,128)S(1)} %get-tuple-element.27), channel_id=1, source_target_pairs={{0,1},{1,0},{2,3},{3,2},{4,5},{5,4},{6,7},{7,6},{8,9},{9,8},{10,11... | collective-permute-start | bytes 786440 | tf_op jit(solution)/shard_map/ppermute | solution.py:516
  4.6 6.3 %collective-permute-start.1 = (f32[64,1024]{1,0:T(8,128)S(1)}, f32[64,1024]{1,0:T(8,128)S(1)}, u32[]{:S(2)}, u32[]{:S(2)}) collective-permute-start(f32[64,1024]{1,0:T(8,128)S(1)} %get-tuple-element.28), channel_id=1, source_target_pairs={{1,2},{2,1},{5,6},{6,5},{9,10},{10,9},{13,14},{14,13},{17,18},{18,... | collective-permute-start | bytes 786440 | tf_op jit(solution)/shard_map/ppermute | solution.py:516
  15.7 12.2 %collective-permute-start.2 = (f32[32,1024]{1,0:T(8,128)S(1)}, f32[32,1024]{1,0:T(8,128)S(1)}, u32[]{:S(2)}, u32[]{:S(2)}) collective-permute-start(f32[32,1024]{1,0:T(8,128)S(1)} %get-tuple-element.31), channel_id=1, source_target_pairs={{0,4},{1,5},{2,6},{3,7},{4,8},{5,9},{6,10},{7,11},{8,12},{9,13},{1... | collective-permute-start | bytes 393224 | tf_op jit(solution)/shard_map/ppermute | solution.py:516
  15.8 10.4 %collective-permute-start.3 = (f32[24,1024]{1,0:T(8,128)S(1)}, f32[24,1024]{1,0:T(8,128)S(1)}, u32[]{:S(2)}, u32[]{:S(2)}) collective-permute-start(f32[24,1024]{1,0:T(8,128)S(1)} %get-tuple-element.32), channel_id=1, source_target_pairs={{0,5},{1,4},{2,7},{3,6},{4,9},{5,8},{6,11},{7,10},{8,13},{9,12},{1... | collective-permute-start | bytes 294920 | tf_op jit(solution)/shard_map/ppermute | solution.py:516
  22.2 5.7 %collective-permute-start.4 = (f32[24,1024]{1,0:T(8,128)S(1)}, f32[24,1024]{1,0:T(8,128)S(1)}, u32[]{:S(2)}, u32[]{:S(2)}) collective-permute-start(f32[24,1024]{1,0:T(8,128)S(1)} %get-tuple-element.33), channel_id=1, source_target_pairs={{1,6},{2,5},{5,10},{6,9},{9,14},{10,13},{13,18},{14,17},{17,22},{1... | collective-permute-start | bytes 294920 | tf_op jit(solution)/shard_map/ppermute | solution.py:516
  22.9 12.7 %collective-permute-start.10 = (f32[80,128]{1,0:T(8,128)S(1)}, f32[80,128]{1,0:T(8,128)S(1)}, u32[]{:S(2)}, u32[]{:S(2)}) collective-permute-start(f32[80,128]{1,0:T(8,128)S(1)} %get-tuple-element.35.refs_4_), channel_id=1, source_target_pairs={{0,3},{1,2},{2,1},{3,0},{4,7},{5,6},{6,5},{7,4},{8,11},{9,10},{10,... | collective-permute-start | bytes 122888 | tf_op jit(solution)/shard_map/ppermute | solution.py:516
  25.6 11.9 %collective-permute-start.8 = (f32[80,128]{1,0:T(8,128)S(1)}, f32[80,128]{1,0:T(8,128)S(1)}, u32[]{:S(2)}, u32[]{:S(2)}) collective-permute-start(f32[80,128]{1,0:T(8,128)S(1)} %get-tuple-element.35.refs_4_), channel_id=1, source_target_pairs={{0,1},{1,0},{2,3},{3,2},{4,5},{5,4},{6,7},{7,6},{8,9},{9,8},{10,11... | collective-permute-start | bytes 122888 | tf_op jit(solution)/shard_map/ppermute | solution.py:516
  26.2 11.2 %collective-permute-start.9 = (f32[80,128]{1,0:T(8,128)S(1)}, f32[80,128]{1,0:T(8,128)S(1)}, u32[]{:S(2)}, u32[]{:S(2)}) collective-permute-start(f32[80,128]{1,0:T(8,128)S(1)} %get-tuple-element.35.refs_4_), channel_id=1, source_target_pairs={{0,2},{1,3},{2,0},{3,1},{4,6},{5,7},{6,4},{7,5},{8,10},{9,11},{10,... | collective-permute-start | bytes 122888 | tf_op jit(solution)/shard_map/ppermute | solution.py:516
  32.9 4.5 %collective-permute-start.5 = (f32[16,512]{1,0:T(8,128)S(1)}, f32[16,512]{1,0:T(8,128)S(1)}, u32[]{:S(2)}, u32[]{:S(2)}) collective-permute-start(f32[16,512]{1,0:T(8,128)S(1)} %shard_map.84.refs_0_), channel_id=1, source_target_pairs={{0,1},{1,0},{2,3},{3,2},{4,5},{5,4},{6,7},{7,6},{8,9},{9,8},{10,11... | collective-permute-start | bytes 98312 | tf_op jit(solution)/shard_map/ppermute | solution.py:516
  35.0 5.5 %collective-permute-start.6 = (f32[16,512]{1,0:T(8,128)S(1)}, f32[16,512]{1,0:T(8,128)S(1)}, u32[]{:S(2)}, u32[]{:S(2)}) collective-permute-start(f32[16,512]{1,0:T(8,128)S(1)} %shard_map.84.refs_0_), channel_id=1, source_target_pairs={{0,2},{1,3},{2,0},{3,1},{4,6},{5,7},{6,4},{7,5},{8,10},{9,11},{10,... | collective-permute-start | bytes 98312 | tf_op jit(solution)/shard_map/ppermute | solution.py:516
  35.6 5.8 %collective-permute-start.7 = (f32[16,512]{1,0:T(8,128)S(1)}, f32[16,512]{1,0:T(8,128)S(1)}, u32[]{:S(2)}, u32[]{:S(2)}) collective-permute-start(f32[16,512]{1,0:T(8,128)S(1)} %shard_map.84.refs_0_), channel_id=1, source_target_pairs={{0,3},{1,2},{2,1},{3,0},{4,7},{5,6},{6,5},{7,4},{8,11},{9,10},{10,... | collective-permute-start | bytes 98312 | tf_op jit(solution)/shard_map/ppermute | solution.py:516
  41.6 1.4 %collective-permute-start.11 = (f32[4,64,128]{2,1,0:T(8,128)S(1)}, f32[4,64,128]{2,1,0:T(8,128)S(1)}, u32[]{:S(2)}, u32[]{:S(2)}) collective-permute-start(f32[4,64,128]{2,1,0:T(8,128)S(1)} %get-tuple-element.36.refs_0_), channel_id=1, source_target_pairs={{0,4},{4,0},{8,12},{12,8},{16,20},{20,16},{24,28},{28,24},{1,5},{5... | collective-permute-start | bytes 393224 | tf_op jit(solution)/shard_map/ppermute | solution.py:569
  43.6 5.6 %collective-permute-start.12 = (f32[4,64,128]{2,1,0:T(8,128)S(1)}, f32[4,64,128]{2,1,0:T(8,128)S(1)}, u32[]{:S(2)}, u32[]{:S(2)}) collective-permute-start(f32[4,64,128]{2,1,0:T(8,128)S(1)} %get-tuple-element.39.refs_0_), channel_id=1, source_target_pairs={{0,8},{4,12},{8,0},{12,4},{16,24},{20,28},{24,16},{28,20},{1,9},{5... | collective-permute-start | bytes 393224 | tf_op jit(solution)/shard_map/ppermute | solution.py:569
  50.4 5.0 %collective-permute-start.13 = (f32[4,64,128]{2,1,0:T(8,128)S(1)}, f32[4,64,128]{2,1,0:T(8,128)S(1)}, u32[]{:S(2)}, u32[]{:S(2)}) collective-permute-start(f32[4,64,128]{2,1,0:T(8,128)S(1)} %get-tuple-element.41.refs_0_), channel_id=1, source_target_pairs={{0,16},{4,20},{8,24},{12,28},{16,0},{20,4},{24,8},{28,12},{1,17},{... | collective-permute-start | bytes 393224 | tf_op jit(solution)/shard_map/ppermute | solution.py:569

commit v6 on v5

--- a/solution.py
+++ b/solution.py
@@ -95,7 +95,7 @@
 
 def pack_body(
     point_far, rate_far, source_far, initial_far, table_far, classes_far,
-    pay_a, pay_b, coarse, blocks_out, point, rate, source, initial, table, classes, tmp, sems,
+    pay_a, pay_b, blocks_out, point, rate, source, initial, table, classes, sems,
 ):
     copies = fetch(
         (
@@ -135,6 +135,12 @@
         fill(pay_a, True)
         fill(pay_b, False)
 
+    copies[5].wait()
+
+
+def coarsen_body(rate, blocks_out, coarse, tmp):
+    rows, width = rate.shape
+    blocks, tiles = rows // BLK_R, width // LANES
     for c in range(tiles):
         tmp[c, :, :] = rate[:, cols(c)]
     pairs = halve()
@@ -146,7 +152,6 @@
         coarse[at : at + blocks, :] = jnp.where(
             iota(1, (blocks, LANES)) < LANES // 2, halves[0], halves[1]
         )
-    copies[5].wait()
 
 
 def sweep(state, spare, weights, force, count, tiles, strip_tiles, wave):
@@ -516,19 +521,21 @@
         return lax.ppermute(value, both, pairs)
 
     strip = f32(rows, width)
-    pay_a, pay_b, field, own_blocks, point, rate, source, initial = call(
+    pay_a, pay_b, own_blocks, point, rate, source, initial = call(
         pack_body, [FAR] * 6,
-        (f32(packed, width), f32(packed, width), f32(fields_rows, LANES), f32(SUB, width), strip, strip, strip, strip),
+        (f32(packed, width), f32(packed, width), f32(SUB, width), strip, strip, strip, strip),
         [
             pltpu.SMEM(cond_table.shape, F32),
             pltpu.SMEM(class_map.shape, jnp.int32),
-            pltpu.VMEM((tiles, rows, LANES), F32),
             pltpu.SemaphoreType.DMA((6,)),
         ],
         1 << 20,
     )(*[far(x) for x in (point, node_rate, source_map, initial_state, cond_table, class_map)])
     got_a = exchange(pay_a, 0, lambda s: side(s, "a"))
     got_b = exchange(pay_b, 0, lambda s: side(s, "b"))
+    field = call(
+        coarsen_body, [VM] * 2, f32(fields_rows, LANES), [pltpu.VMEM((tiles, rows, LANES), F32)], 1 << 20
+    )(rate, own_blocks)
     fields = [field]
     for k in range(1, strips):
         fields.append(exchange(field, 0, lambda s, k=k: s ^ k))

time: 56.6 us -> 56.6 us (level)
  starting transfers between devices: 21.9 us -> 20.9 us
  waiting for transfers between devices: 20.2 us -> 21.2 us
    ppermute x3, waiting for transfers between devices: 10.6 us -> 11.3 us  [shards(): lax.ppermute(total, 'tm', [(j, j ^ 1 << stage) for j in range(intervals)])]
    ppermute x3, starting transfers between devices: 1.5 us -> 0.76 us  [shards(): lax.ppermute(total, 'tm', [(j, j ^ 1 << stage) for j in range(intervals)])]
    pallas_call x1 -> x2, Pallas kernels: 1.49 us -> 1.49 us  [the longest x1 1.15 us: shards(): call(pack_body, [FAR] * 6, (f32(packed, width), f32(packed, width), f32(S...]
where the time goes in v6:
time: 56.6 us; the launch traced here: 56.4 us
  waiting for transfers between devices  21.2 us (37%)
  starting transfers between devices  20.9 us (37%)
  Pallas kernels  14.2 us (25%)
    ppermute x11, starting transfers between devices, exchange(): return lax.ppermute(value, both, pairs)  20.1 us
    ppermute x3, waiting for transfers between devices, shards(): lax.ppermute(total, 'tm', [(j, j ^ 1 << stage) for j in range(intervals)])  11.3 us
    ppermute x11, waiting for transfers between devices, exchange(): return lax.ppermute(value, both, pairs)  9.88 us
    pallas_call x1, Pallas kernels, shards(): call(second_body, [VM] * 7 + [FAR], f32(crows, width // 2), [grid, grid,...  5 us
    pallas_call x1, Pallas kernels, shards(): call(first_body, [VM] * 7 + [FAR] * 2, (strip, f32(HALO, width), f32(HALO...  4.81 us
    pallas_call x2, Pallas kernels, shards(): call(body, specs, (f32(ctiles, cheight, LANES), f32(ctiles, crows, LANES)...  1.66 us
    pallas_call x1, Pallas kernels, shards(): call(pack_body, [FAR] * 6, (f32(packed, width), f32(packed, width), f32(S...  1.15 us
  transfers between devices with their start and end apart: 14, of which 6 were waited for; matrix products, arithmetic and copies ran while one was open for 0% of the time, Pallas kernels for 9%

profile of v6, /device:TPU:0, one launch (start us, length us, event | category | flops | bytes accessed | tf_op | source)
XLA Modules:
  0.0 56.4 jit_solution(9697384478609408226)
XLA Ops:
  0.0 1.1 %shard_map.82 = (f32[64,1024]{1,0:T(8,128)S(1)}, f32[64,1024]{1,0:T(8,128)S(1)}, f32[8,1024]{1,0:T(8,128)S(1)}, f32[32,1024]{1,0:T(8,128)S(1)}, f32[32,1024]{1,0...) custom-call(f32[32,1024]{1,0:T(8,128)} %bitcast.2, f32[32,1024]{1,0:T(8,128)} %rate_far.1, ...), custom_call_target="tpu_custom_call" | custom-call | flops 1048576 | bytes 1048576 | tf_op jit(solution)/shard_map/pallas_call | solution.py:524
  1.2 3.1 %collective-permute-start = (f32[64,1024]{1,0:T(8,128)S(1)}, f32[64,1024]{1,0:T(8,128)S(1)}, u32[]{:S(2)}, u32[]{:S(2)}) collective-permute-start(f32[64,1024]{1,0:T(8,128)S(1)} %get-tuple-element.26), channel_id=1, source_target_pairs={{0,1},{1,0},{2,3},{3,2},{4,5},{5,4},{6,7},{7,6},{8,9},{9,8},{10,11... | collective-permute-start | bytes 786440 | tf_op jit(solution)/shard_map/ppermute | solution.py:521
  4.3 0.7 %collective-permute-start.1 = (f32[64,1024]{1,0:T(8,128)S(1)}, f32[64,1024]{1,0:T(8,128)S(1)}, u32[]{:S(2)}, u32[]{:S(2)}) collective-permute-start(f32[64,1024]{1,0:T(8,128)S(1)} %get-tuple-element.27), channel_id=1, source_target_pairs={{1,2},{2,1},{5,6},{6,5},{9,10},{10,9},{13,14},{14,13},{17,18},{18,... | collective-permute-start | bytes 786440 | tf_op jit(solution)/shard_map/ppermute | solution.py:521
  4.9 5.6 %collective-permute-done.got_a = f32[64,1024]{1,0:T(8,128)S(1)} collective-permute-done((f32[64,1024]{1,0:T(8,128)S(1)}, f32[64,1024]{1,0:T(8,128)S(1)}, u32[]{:S(2)}, u32[]{:S(2)}) %collective-permute-start) | collective-permute-done | bytes 262176 | tf_op jit(solution)/shard_map/ppermute | solution.py:521
  10.6 0.0 collective-permute-done.1.got_b
  10.6 4.8 %shard_map.83 = (f32[32,1024]{1,0:T(8,128)S(1)}, f32[24,1024]{1,0:T(8,128)S(1)}, f32[24,1024]{1,0:T(8,128)S(1)}, f32[5,8,80,128]{3,2,1,0:T(8,128)S(1)}, f32[8,128]{1,0:T(8,128)S(1)}) custom-call(f32[32,1024]{1,0:T(8,128)S(1)} %get-tuple-element.23.point, f32[32,1024]{1,0:T(8,128)S(1)} %get-tuple-element.24.rate, f32[32,1024]{1,0:T(8,128)S(1)} %get-tuple-element.25.source, ...), custom_call_target="tpu_custom_call" | custom-call | flops 16777216 | bytes 1048576 | tf_op jit(solution)/shard_map/pallas_call | solution.py:546
  15.4 0.1 collective-permute-start.2
  15.5 6.4 %collective-permute-start.3 = (f32[24,1024]{1,0:T(8,128)S(1)}, f32[24,1024]{1,0:T(8,128)S(1)}, u32[]{:S(2)}, u32[]{:S(2)}) collective-permute-start(f32[24,1024]{1,0:T(8,128)S(1)} %get-tuple-element.31), channel_id=1, source_target_pairs={{0,5},{1,4},{2,7},{3,6},{4,9},{5,8},{6,11},{7,10},{8,13},{9,12},{1... | collective-permute-start | bytes 294920 | tf_op jit(solution)/shard_map/ppermute | solution.py:521
  21.8 0.7 %collective-permute-start.4 = (f32[24,1024]{1,0:T(8,128)S(1)}, f32[24,1024]{1,0:T(8,128)S(1)}, u32[]{:S(2)}, u32[]{:S(2)}) collective-permute-start(f32[24,1024]{1,0:T(8,128)S(1)} %get-tuple-element.32), channel_id=1, source_target_pairs={{1,6},{2,5},{5,10},{6,9},{9,14},{10,13},{13,18},{14,17},{17,22},{1... | collective-permute-start | bytes 294920 | tf_op jit(solution)/shard_map/ppermute | solution.py:521
  22.5 0.3 shard_map.85.refs_4_
  22.9 2.7 %collective-permute-start.10 = (f32[80,128]{1,0:T(8,128)S(1)}, f32[80,128]{1,0:T(8,128)S(1)}, u32[]{:S(2)}, u32[]{:S(2)}) collective-permute-start(f32[80,128]{1,0:T(8,128)S(1)} %shard_map.85.refs_4_), channel_id=1, source_target_pairs={{0,3},{1,2},{2,1},{3,0},{4,7},{5,6},{6,5},{7,4},{8,11},{9,10},{10,... | collective-permute-start | bytes 122888 | tf_op jit(solution)/shard_map/ppermute | solution.py:521
  25.6 0.6 %collective-permute-start.8 = (f32[80,128]{1,0:T(8,128)S(1)}, f32[80,128]{1,0:T(8,128)S(1)}, u32[]{:S(2)}, u32[]{:S(2)}) collective-permute-start(f32[80,128]{1,0:T(8,128)S(1)} %shard_map.85.refs_4_), channel_id=1, source_target_pairs={{0,1},{1,0},{2,3},{3,2},{4,5},{5,4},{6,7},{7,6},{8,9},{9,8},{10,11... | collective-permute-start | bytes 122888 | tf_op jit(solution)/shard_map/ppermute | solution.py:521
  26.2 0.0 collective-permute-done.3.edge_a
  26.2 1.3 %collective-permute-start.9 = (f32[80,128]{1,0:T(8,128)S(1)}, f32[80,128]{1,0:T(8,128)S(1)}, u32[]{:S(2)}, u32[]{:S(2)}) collective-permute-start(f32[80,128]{1,0:T(8,128)S(1)} %shard_map.85.refs_4_), channel_id=1, source_target_pairs={{0,2},{1,3},{2,0},{3,1},{4,6},{5,7},{6,4},{7,5},{8,10},{9,11},{10,... | collective-permute-start | bytes 122888 | tf_op jit(solution)/shard_map/ppermute | solution.py:521
  27.5 5.0 %shard_map.84.refs_0_ = f32[16,512]{1,0:T(8,128)S(1)} custom-call(f32[32,1024]{1,0:T(8,128)S(1)} %collective-permute-done.2.relaxed.refs_5_, f32[24,1024]{1,0:T(8,128)S(1)} %collective-permute-done.3.edge_a, f32[24,1024]{1,0:T(8,128)S(1)} %collective-permute-done.4.edge_b, f32[32,1024]{1,0:T(8,128)S(1)} %get-tuple-element.23.point, ...), custom_call_target="tpu_custom_call" | custom-call | flops 16777216 | bytes 1048576 | tf_op jit(solution)/shard_map/pallas_call | solution.py:556
  32.6 2.1 %collective-permute-start.5 = (f32[16,512]{1,0:T(8,128)S(1)}, f32[16,512]{1,0:T(8,128)S(1)}, u32[]{:S(2)}, u32[]{:S(2)}) collective-permute-start(f32[16,512]{1,0:T(8,128)S(1)} %shard_map.84.refs_0_), channel_id=1, source_target_pairs={{0,1},{1,0},{2,3},{3,2},{4,5},{5,4},{6,7},{7,6},{8,9},{9,8},{10,11... | collective-permute-start | bytes 98312 | tf_op jit(solution)/shard_map/ppermute | solution.py:521
  34.7 0.9 %collective-permute-start.6 = (f32[16,512]{1,0:T(8,128)S(1)}, f32[16,512]{1,0:T(8,128)S(1)}, u32[]{:S(2)}, u32[]{:S(2)}) collective-permute-start(f32[16,512]{1,0:T(8,128)S(1)} %shard_map.84.refs_0_), channel_id=1, source_target_pairs={{0,2},{1,3},{2,0},{3,1},{4,6},{5,7},{6,4},{7,5},{8,10},{9,11},{10,... | collective-permute-start | bytes 98312 | tf_op jit(solution)/shard_map/ppermute | solution.py:521
  35.6 1.6 %collective-permute-start.7 = (f32[16,512]{1,0:T(8,128)S(1)}, f32[16,512]{1,0:T(8,128)S(1)}, u32[]{:S(2)}, u32[]{:S(2)}) collective-permute-start(f32[16,512]{1,0:T(8,128)S(1)} %shard_map.84.refs_0_), channel_id=1, source_target_pairs={{0,3},{1,2},{2,1},{3,0},{4,7},{5,6},{6,5},{7,4},{8,11},{9,10},{10,... | collective-permute-start | bytes 98312 | tf_op jit(solution)/shard_map/ppermute | solution.py:521
  37.1 0.0 collective-permute-done.8.refs_5_
  37.1 0.0 collective-permute-done.9.refs_6_
  37.2 2.9 %collective-permute-done.6.refs_2_ = f32[16,512]{1,0:T(8,128)S(1)} collective-permute-done((f32[16,512]{1,0:T(8,128)S(1)}, f32[16,512]{1,0:T(8,128)S(1)}, u32[]{:S(2)}, u32[]{:S(2)}) %collective-permute-start.6) | collective-permute-done | bytes 32800 | tf_op jit(solution)/shard_map/ppermute | solution.py:521
  40.1 1.3 %collective-permute-done.7.refs_3_ = f32[16,512]{1,0:T(8,128)S(1)} collective-permute-done((f32[16,512]{1,0:T(8,128)S(1)}, f32[16,512]{1,0:T(8,128)S(1)}, u32[]{:S(2)}, u32[]{:S(2)}) %collective-permute-start.7) | collective-permute-done | bytes 32800 | tf_op jit(solution)/shard_map/ppermute | solution.py:521
  41.4 0.2 shard_map.86
  41.6 0.2 collective-permute-start.11
  41.9 1.2 %collective-permute-done.11.refs_1_ = f32[4,64,128]{2,1,0:T(8,128)S(1)} collective-permute-done((f32[4,64,128]{2,1,0:T(8,128)S(1)}, f32[4,64,128]{2,1,0:T(8,128)S(1)}, u32[]{:S(2)}, u32[]{:S(2)}) %collective-permute-start.11) | collective-permute-done | bytes 131104 | tf_op jit(solution)/shard_map/ppermute | solution.py:576
  43.0 0.6 shard_map.87
  43.6 0.5 collective-permute-start.12
  44.1 5.2 %collective-permute-done.12.refs_1_ = f32[4,64,128]{2,1,0:T(8,128)S(1)} collective-permute-done((f32[4,64,128]{2,1,0:T(8,128)S(1)}, f32[4,64,128]{2,1,0:T(8,128)S(1)}, u32[]{:S(2)}, u32[]{:S(2)}) %collective-permute-start.12) | collective-permute-done | bytes 131104 | tf_op jit(solution)/shard_map/ppermute | solution.py:576
  49.2 1.1 %shard_map.88 = (f32[4,64,128]{2,1,0:T(8,128)S(1)}, f32[4,16,128]{2,1,0:T(8,128)S(1)}) custom-call(f32[4,64,128]{2,1,0:T(8,128)S(1)} %get-tuple-element.37.refs_0_, f32[4,64,128]{2,1,0:T(8,128)S(1)} %collective-permute-done.12.refs_1_, f32[4,16,128]{2,1,0:T(8,128)S(1)} %get-tuple-element.38.refs_2_, f32[5,4,64,128]{3,2,1,0:T(8,128)S(1)} %get-tuple-element.35.refs_2_.refs_3_, ...), custom_call_target="tpu_custom_call" | custom-call | flops 8388608 | bytes 1048576 | tf_op jit(solution)/shard_map/pallas_call | solution.py:593
  50.3 0.1 collective-permute-start.13
  50.4 5.0 %collective-permute-done.13.refs_1_ = f32[4,64,128]{2,1,0:T(8,128)S(1)} collective-permute-done((f32[4,64,128]{2,1,0:T(8,128)S(1)}, f32[4,64,128]{2,1,0:T(8,128)S(1)}, u32[]{:S(2)}, u32[]{:S(2)}) %collective-permute-start.13) | collective-permute-done | bytes 131104 | tf_op jit(solution)/shard_map/ppermute | solution.py:576
  55.4 1.0 %shard_map.89 = f32[32,1024]{1,0:T(8,128)} custom-call(f32[4,64,128]{2,1,0:T(8,128)S(1)} %get-tuple-element.39.refs_0_, f32[4,64,128]{2,1,0:T(8,128)S(1)} %collective-permute-done.13.refs_1_, f32[4,16,128]{2,1,0:T(8,128)S(1)} %get-tuple-element.40.refs_2_, f32[5,4,64,128]{3,2,1,0:T(8,128)S(1)} %get-tuple-element.35.refs_2_.refs_3_, ...), custom_call_target="tpu_custom_call" | custom-call | flops 8388608 | bytes 1048576 | tf_op jit(solution)/shard_map/pallas_call | solution.py:588
  (4 shorter events, 0.0 us)
Async XLA Ops:
  1.2 9.4 %collective-permute-start = (f32[64,1024]{1,0:T(8,128)S(1)}, f32[64,1024]{1,0:T(8,128)S(1)}, u32[]{:S(2)}, u32[]{:S(2)}) collective-permute-start(f32[64,1024]{1,0:T(8,128)S(1)} %get-tuple-element.26), channel_id=1, source_target_pairs={{0,1},{1,0},{2,3},{3,2},{4,5},{5,4},{6,7},{7,6},{8,9},{9,8},{10,11... | collective-permute-start | bytes 786440 | tf_op jit(solution)/shard_map/ppermute | solution.py:521
  4.3 6.3 %collective-permute-start.1 = (f32[64,1024]{1,0:T(8,128)S(1)}, f32[64,1024]{1,0:T(8,128)S(1)}, u32[]{:S(2)}, u32[]{:S(2)}) collective-permute-start(f32[64,1024]{1,0:T(8,128)S(1)} %get-tuple-element.27), channel_id=1, source_target_pairs={{1,2},{2,1},{5,6},{6,5},{9,10},{10,9},{13,14},{14,13},{17,18},{18,... | collective-permute-start | bytes 786440 | tf_op jit(solution)/shard_map/ppermute | solution.py:521
  15.4 12.2 %collective-permute-start.2 = (f32[32,1024]{1,0:T(8,128)S(1)}, f32[32,1024]{1,0:T(8,128)S(1)}, u32[]{:S(2)}, u32[]{:S(2)}) collective-permute-start(f32[32,1024]{1,0:T(8,128)S(1)} %get-tuple-element.30), channel_id=1, source_target_pairs={{0,4},{1,5},{2,6},{3,7},{4,8},{5,9},{6,10},{7,11},{8,12},{9,13},{1... | collective-permute-start | bytes 393224 | tf_op jit(solution)/shard_map/ppermute | solution.py:521
  15.5 10.7 %collective-permute-start.3 = (f32[24,1024]{1,0:T(8,128)S(1)}, f32[24,1024]{1,0:T(8,128)S(1)}, u32[]{:S(2)}, u32[]{:S(2)}) collective-permute-start(f32[24,1024]{1,0:T(8,128)S(1)} %get-tuple-element.31), channel_id=1, source_target_pairs={{0,5},{1,4},{2,7},{3,6},{4,9},{5,8},{6,11},{7,10},{8,13},{9,12},{1... | collective-permute-start | bytes 294920 | tf_op jit(solution)/shard_map/ppermute | solution.py:521
  21.8 5.7 %collective-permute-start.4 = (f32[24,1024]{1,0:T(8,128)S(1)}, f32[24,1024]{1,0:T(8,128)S(1)}, u32[]{:S(2)}, u32[]{:S(2)}) collective-permute-start(f32[24,1024]{1,0:T(8,128)S(1)} %get-tuple-element.32), channel_id=1, source_target_pairs={{1,6},{2,5},{5,10},{6,9},{9,14},{10,13},{13,18},{14,17},{17,22},{1... | collective-permute-start | bytes 294920 | tf_op jit(solution)/shard_map/ppermute | solution.py:521
  22.9 12.7 %collective-permute-start.10 = (f32[80,128]{1,0:T(8,128)S(1)}, f32[80,128]{1,0:T(8,128)S(1)}, u32[]{:S(2)}, u32[]{:S(2)}) collective-permute-start(f32[80,128]{1,0:T(8,128)S(1)} %shard_map.85.refs_4_), channel_id=1, source_target_pairs={{0,3},{1,2},{2,1},{3,0},{4,7},{5,6},{6,5},{7,4},{8,11},{9,10},{10,... | collective-permute-start | bytes 122888 | tf_op jit(solution)/shard_map/ppermute | solution.py:521
  25.6 11.6 %collective-permute-start.8 = (f32[80,128]{1,0:T(8,128)S(1)}, f32[80,128]{1,0:T(8,128)S(1)}, u32[]{:S(2)}, u32[]{:S(2)}) collective-permute-start(f32[80,128]{1,0:T(8,128)S(1)} %shard_map.85.refs_4_), channel_id=1, source_target_pairs={{0,1},{1,0},{2,3},{3,2},{4,5},{5,4},{6,7},{7,6},{8,9},{9,8},{10,11... | collective-permute-start | bytes 122888 | tf_op jit(solution)/shard_map/ppermute | solution.py:521
  26.2 11.0 %collective-permute-start.9 = (f32[80,128]{1,0:T(8,128)S(1)}, f32[80,128]{1,0:T(8,128)S(1)}, u32[]{:S(2)}, u32[]{:S(2)}) collective-permute-start(f32[80,128]{1,0:T(8,128)S(1)} %shard_map.85.refs_4_), channel_id=1, source_target_pairs={{0,2},{1,3},{2,0},{3,1},{4,6},{5,7},{6,4},{7,5},{8,10},{9,11},{10,... | collective-permute-start | bytes 122888 | tf_op jit(solution)/shard_map/ppermute | solution.py:521
  32.6 4.6 %collective-permute-start.5 = (f32[16,512]{1,0:T(8,128)S(1)}, f32[16,512]{1,0:T(8,128)S(1)}, u32[]{:S(2)}, u32[]{:S(2)}) collective-permute-start(f32[16,512]{1,0:T(8,128)S(1)} %shard_map.84.refs_0_), channel_id=1, source_target_pairs={{0,1},{1,0},{2,3},{3,2},{4,5},{5,4},{6,7},{7,6},{8,9},{9,8},{10,11... | collective-permute-start | bytes 98312 | tf_op jit(solution)/shard_map/ppermute | solution.py:521
  34.7 5.4 %collective-permute-start.6 = (f32[16,512]{1,0:T(8,128)S(1)}, f32[16,512]{1,0:T(8,128)S(1)}, u32[]{:S(2)}, u32[]{:S(2)}) collective-permute-start(f32[16,512]{1,0:T(8,128)S(1)} %shard_map.84.refs_0_), channel_id=1, source_target_pairs={{0,2},{1,3},{2,0},{3,1},{4,6},{5,7},{6,4},{7,5},{8,10},{9,11},{10,... | collective-permute-start | bytes 98312 | tf_op jit(solution)/shard_map/ppermute | solution.py:521
  35.6 5.8 %collective-permute-start.7 = (f32[16,512]{1,0:T(8,128)S(1)}, f32[16,512]{1,0:T(8,128)S(1)}, u32[]{:S(2)}, u32[]{:S(2)}) collective-permute-start(f32[16,512]{1,0:T(8,128)S(1)} %shard_map.84.refs_0_), channel_id=1, source_target_pairs={{0,3},{1,2},{2,1},{3,0},{4,7},{5,6},{6,5},{7,4},{8,11},{9,10},{10,... | collective-permute-start | bytes 98312 | tf_op jit(solution)/shard_map/ppermute | solution.py:521
  41.6 1.4 %collective-permute-start.11 = (f32[4,64,128]{2,1,0:T(8,128)S(1)}, f32[4,64,128]{2,1,0:T(8,128)S(1)}, u32[]{:S(2)}, u32[]{:S(2)}) collective-permute-start(f32[4,64,128]{2,1,0:T(8,128)S(1)} %get-tuple-element.34.refs_0_), channel_id=1, source_target_pairs={{0,4},{4,0},{8,12},{12,8},{16,20},{20,16},{24,28},{28,24},{1,5},{5... | collective-permute-start | bytes 393224 | tf_op jit(solution)/shard_map/ppermute | solution.py:576
  43.6 5.6 %collective-permute-start.12 = (f32[4,64,128]{2,1,0:T(8,128)S(1)}, f32[4,64,128]{2,1,0:T(8,128)S(1)}, u32[]{:S(2)}, u32[]{:S(2)}) collective-permute-start(f32[4,64,128]{2,1,0:T(8,128)S(1)} %get-tuple-element.37.refs_0_), channel_id=1, source_target_pairs={{0,8},{4,12},{8,0},{12,4},{16,24},{20,28},{24,16},{28,20},{1,9},{5... | collective-permute-start | bytes 393224 | tf_op jit(solution)/shard_map/ppermute | solution.py:576
  50.3 5.0 %collective-permute-start.13 = (f32[4,64,128]{2,1,0:T(8,128)S(1)}, f32[4,64,128]{2,1,0:T(8,128)S(1)}, u32[]{:S(2)}, u32[]{:S(2)}) collective-permute-start(f32[4,64,128]{2,1,0:T(8,128)S(1)} %get-tuple-element.39.refs_0_), channel_id=1, source_target_pairs={{0,16},{4,20},{8,24},{12,28},{16,0},{20,4},{24,8},{28,12},{1,17},{... | collective-permute-start | bytes 393224 | tf_op jit(solution)/shard_map/ppermute | solution.py:576
